TPU v7x, 32 devices: a whole 2x2x4 slice. The times are simulated.
32 devices in a mesh: hot: 4 (over y, x), tt: 8 (over z, core).
Axes of the slice: x: 2, y: 2, z: 4, core: 2. Of those that a mesh axis runs over, the one named last changes fastest.
Arguments:
- hot_table: float32 [1024, 256], P('hot'), may hold values from -1.5 to 1.5
- hot_accum: float32 [1024], P('hot'), may hold values from 0.05 to 1
- hot_owner: int32 [8192, 1], P(('hot', 'tt')), may hold values from 0 to 3; in each aligned block of 256 rows (0 to 255, 256 to 511, ...) at most 128 rows name the same one
- hot_row: int32 [32, 256], P(('hot', 'tt')), may hold values from 0 to 255
- hot_bag: int32 [32, 256], P(('hot', 'tt')), may hold values from 0 to 63, never falling along the last dimension, each value on 1 to 12 neighbouring positions
- cold_owner: int32 [16384, 1], P(('hot', 'tt')), may hold values from 0 to 7; in each aligned block of 512 rows (0 to 511, 512 to 1023, ...) at most 128 rows name the same one
- first_index: int32 [32, 512], P(('hot', 'tt')), may hold values from 0 to 127
- mid_index: int32 [32, 512], P(('hot', 'tt')), may hold values from 0 to 63
- last_index: int32 [32, 512], P(('hot', 'tt')), may hold values from 0 to 63
- cold_bag: int32 [32, 512], P(('hot', 'tt')), may hold values from 0 to 63, never falling along the last dimension, each value on 1 to 24 neighbouring positions
- core_first: float32 [1024, 256], P('tt'), may hold values from -1 to 1
- core_mid: bfloat16 [64, 8192], replicated, may hold values from -1 to 1
- core_last: bfloat16 [64, 128], replicated, may hold values from -6 to 6
- bag_grads: bfloat16 [2048, 256], P(('hot', 'tt')), may hold values from -6 to 6
Outputs:
- pooled: float32 [2048, 256], P(('hot', 'tt'))
- new_table: float32 [1024, 256], P('hot')
- new_accum: float32 [1024], P('hot')
- new_first: float32 [1024, 256], P('tt')
Inputs may be any that keep to these rules, and one draw needn't show every extreme that they name: `hot_owner`: among the 256 hot lookups of one device no owner appears more than 128 times; some owner appears exactly that often. `cold_owner`: among the 512 cold lookups of one device no owner appears more than 128 times; some owner appears exactly that often. `hot_bag`: never falling along a device's lookups; every bag of a device has at least one hot lookup. `cold_bag`: never falling along a device's lookups; every bag of a device has at least one cold lookup.
All inputs are finite; a program needn't handle non-finite values.
Results may differ from a plain program's by a relative error of at most 0.005.
Values may be sent and summed in bfloat16 or wider, within the bound.
No kernel may reach another device: no remote copies, remote signals or barrier semaphores. Data moves between devices by JAX's collectives and lax.ppermute only.
A program may use at most 64 MiB of HBM per device.

v0:
```python
import math

import jax
import jax.numpy as jnp
from jax import lax
from jax.sharding import PartitionSpec as P

E1 = 8
E2 = 8
E3 = 4
RANK = 32


def slots_of(owners, peer_count):
    chosen = (owners[:, None] == jnp.arange(peer_count, dtype=jnp.int32)[None, :]).astype(jnp.int32)
    before = jnp.cumsum(chosen, axis=0) - chosen
    return jnp.sum(before * chosen, axis=1)


def slot_source(slot_keys, total_slots):
    lookups = slot_keys.shape[0]
    empty = jnp.full((total_slots,), lookups, jnp.int32)
    return empty.at[slot_keys].set(jnp.arange(lookups, dtype=jnp.int32))


def packed(values, source, fill_value):
    return jnp.take(values, source, axis=0, mode="fill", fill_value=fill_value)


def owner_sum(targets, values, held, precision):
    block_rows = math.gcd(held, 512)
    starts = jnp.arange(held // block_rows, dtype=jnp.int32) * block_rows
    offsets = jnp.arange(block_rows, dtype=jnp.int32)

    def owner_one_block(start):
        picks = ((start + offsets)[:, None] == targets[None, :]).astype(values.dtype)
        return jnp.dot(picks, values, precision=precision, preferred_element_type=jnp.float32)

    return lax.map(owner_one_block, starts).reshape(held, values.shape[1])


def adagrad(table_part, accum_part, grad_part):
    accum_next = accum_part + jnp.mean(grad_part * grad_part, axis=1)
    return (table_part - 0.1 * grad_part / (jnp.sqrt(accum_next)[:, None] + 1e-08), accum_next)


def rank_maps(core_mid, core_last, middle, lasts):
    lookups = middle.shape[0]
    block_rows = math.gcd(lookups, 128)

    def rank_one_block(indices):
        mid_part, last_part = indices
        mid_cores = core_mid[mid_part].reshape(-1, RANK, E2, RANK)
        last_cores = core_last[last_part].reshape(-1, RANK, E3)
        made = jnp.einsum(
            "nawb,nbe->nawe", mid_cores, last_cores, preferred_element_type=jnp.float32
        )
        return made.astype(jnp.bfloat16).reshape(-1, RANK * E2 * E3)

    blocks = lax.map(
        rank_one_block, (middle.reshape(-1, block_rows), lasts.reshape(-1, block_rows))
    )
    return blocks.reshape(lookups, RANK * E2 * E3)


def local(
    hot_table,
    hot_accum,
    hot_owner,
    hot_row,
    hot_bag,
    cold_owner,
    first_index,
    mid_index,
    last_index,
    cold_bag,
    core_first,
    core_mid,
    core_last,
    bag_grads,
):
    rows_held = hot_table.shape[0]
    feature_width = hot_table.shape[1]
    tail_width = feature_width // E1
    bag_count = bag_grads.shape[0]
    bag_range = jnp.arange(bag_count, dtype=jnp.int32)
    hot_peers = lax.axis_size("hot")
    hot_lookups = hot_owner.shape[0]
    hot_cap = 2 * hot_lookups // hot_peers
    row_owner = hot_owner[:, 0]
    row_key = row_owner * hot_cap + slots_of(row_owner, hot_peers)
    row_source = slot_source(row_key, hot_peers * hot_cap)
    request = packed(hot_row[0], row_source, -1).reshape(hot_peers, hot_cap)
    wanted = lax.all_to_all(request, "hot", split_axis=0, concat_axis=0, tiled=True)
    picked = hot_table[jnp.maximum(wanted, 0)].astype(jnp.bfloat16)
    replies = lax.all_to_all(picked, "hot", split_axis=0, concat_axis=0, tiled=True)
    served = wanted
    hot_rows = replies.reshape(-1, feature_width)[row_key]
    hot_pick = (hot_bag[0][:, None] == bag_range[None, :]).astype(jnp.bfloat16)
    hot_cot = jnp.dot(hot_pick, bag_grads, preferred_element_type=jnp.float32).astype(jnp.bfloat16)
    sending = packed(hot_cot, row_source, 0).reshape(hot_peers, hot_cap, feature_width)
    received = lax.all_to_all(sending, "hot", split_axis=0, concat_axis=0, tiled=True)
    row_grad = owner_sum(served.reshape(-1), received.reshape(-1, feature_width), rows_held, None)
    total_grad = lax.psum(row_grad, "tt")
    new_table, new_accum = adagrad(hot_table, hot_accum, total_grad)
    slices_held = core_first.shape[0]
    tt_peers = lax.axis_size("tt")
    cold_lookups = cold_owner.shape[0]
    cold_cap = 2 * cold_lookups // tt_peers
    slice_owner = cold_owner[:, 0]
    slice_key = slice_owner * cold_cap + slots_of(slice_owner, tt_peers)
    slice_source = slot_source(slice_key, tt_peers * cold_cap)
    maps = rank_maps(core_mid, core_last, mid_index[0], last_index[0])
    cold_pick = (cold_bag[0][:, None] == bag_range[None, :]).astype(jnp.bfloat16)
    cold_cot = jnp.dot(cold_pick, bag_grads, preferred_element_type=jnp.float32).astype(
        jnp.bfloat16
    )
    slice_request = packed(first_index[0], slice_source, -1).reshape(tt_peers, cold_cap)
    wanted = lax.all_to_all(slice_request, "tt", split_axis=0, concat_axis=0, tiled=True)
    slices = core_first[jnp.maximum(wanted, 0)].astype(jnp.bfloat16)
    back = lax.all_to_all(slices, "tt", split_axis=0, concat_axis=0, tiled=True)
    slices = back.reshape(-1, E1 * RANK)[slice_key].reshape(cold_lookups, E1, RANK)
    maps_three = maps.reshape(cold_lookups, RANK, tail_width)
    cold_rows = jnp.einsum("kea,kaj->kej", slices, maps_three, preferred_element_type=jnp.float32)
    cold_rows = cold_rows.astype(jnp.bfloat16).reshape(cold_lookups, feature_width)
    local_terms = jnp.einsum(
        "kej,kaj->kea",
        cold_cot.reshape(cold_lookups, E1, tail_width),
        maps_three,
        preferred_element_type=jnp.float32,
    )
    grad_out = packed(local_terms.reshape(cold_lookups, E1 * RANK), slice_source, 0).reshape(
        tt_peers, cold_cap, E1 * RANK
    )
    terms = lax.all_to_all(grad_out, "tt", split_axis=0, concat_axis=0, tiled=True).reshape(
        -1, E1 * RANK
    )
    core_grad = owner_sum(wanted.reshape(-1), terms, slices_held, lax.Precision.HIGHEST)
    core_total = lax.psum(core_grad, "hot")
    new_first = core_first - 0.01 * core_total
    all_rows = jnp.concatenate([hot_rows, cold_rows], axis=0)
    all_picks = jnp.concatenate([hot_pick, cold_pick], axis=0)
    pooled = jnp.einsum("lb,le->be", all_picks, all_rows, preferred_element_type=jnp.float32)
    return (pooled, new_table, new_accum, new_first)


def solution(mesh):
    placed = (
        P("hot", None),
        P("hot"),
        P(("hot", "tt"), None),
        P(("hot", "tt"), None),
        P(("hot", "tt"), None),
        P(("hot", "tt"), None),
        P(("hot", "tt"), None),
        P(("hot", "tt"), None),
        P(("hot", "tt"), None),
        P(("hot", "tt"), None),
        P("tt", None),
        P(),
        P(),
        P(("hot", "tt"), None),
    )
    return jax.shard_map(
        local,
        mesh=mesh,
        in_specs=placed,
        out_specs=(P(("hot", "tt"), None), P("hot", None), P("hot"), P("tt", None)),
        check_vma=False,
    )
```

profile of v0, /device:TPU:0, one launch (start us, length us, event | category | flops | bytes accessed | tf_op | source)
XLA Modules:
  0.0 373.3 jit_solution(5396923980867032876)
XLA Ops:
  8.7 1.2 reduce-window.14
  11.7 1.4 scatter_custom_fusion
  13.1 3.6 gather_fusion.2
  17.3 5.2 %all-to-all-start = ((s32[4,1,128]{2,1,0:T(1,128)}), s32[4,1,128]{2,1,0:T(1,128)S(1)}, u32[]{:S(2)}, u32[]{:S(2)}) async-start(s32[4,1,128]{2,1,0:T(1,128)} %bitcast.17), calls=%async_computation | async-start | bytes 4096 | tf_op jit(solution)/shard_map/all_to_all | solution.py:94
  23.2 1.1 reduce-window.16
  24.6 0.8 fusion.13
  26.1 2.6 scatter_custom_fusion.1
  28.7 154.8 %while.2 = (s32[]{:T(128)}, bf16[4,128,1024]{2,1,0:T(8,128)(2,1)S(1)}, s32[4,128]{1,0:T(4,128)}, bf16[64,8192]{1,0:T(8,128)(2,1)}, s32[4,128]{1,0:T(4,128)}, /*index=5*/bf16[64,128]{1,0:T(8,128)(2,1)}, s32[]{:T(128)}) while((s32[]{:T(128)}, bf16[4,128,1024]{2,1,0:T(8,128)(2,1)S(1)}, s32[4,128]{1,0:T(4,128)}, bf16[64,8192]{1,0:T(8,128)(2,1)}, ...), condition=%wide.region_9.10_spmd, body=%wide.region_8.9_spmd.sunk | while | flops 8522498 | bytes 16822392 | solution.py:60
  29.4 6.5 %gather_fusion = bf16[128,8192]{1,0:T(8,128)(2,1)} fusion(bf16[64,8192]{1,0:T(8,128)(2,1)} %get-tuple-element.145, s32[1024]{0:T(1024)S(1)} %pad_clamp_fusion.8), kind=kCustom, calls=%fused_computation.clone.1 | custom fusion | bytes 4194816 | tf_op jit(solution)/shard_map/while/body/eval_jaxpr/gather | solution.py:53
  35.9 3.2 copy.55
  39.2 11.7 %copy.56 = bf16[128,32,8,32]{3,1,2,0:T(8,128)(2,1)} copy(bf16[128,32,8,32]{0,3,2,1:T(8,128)(2,1)S(1)} %bitcast.108) | data formatting | bytes 4194304 | tf_op jit(solution)/shard_map/while/body/eval_jaxpr/reshape | solution.py:53
  50.9 0.7 gather_fusion.1
  51.9 14.3 %convolution_convert_fusion.5 = bf16[128,32,8,4]{1,3,2,0:T(4,128)(2,1)S(1)} fusion(bf16[128,32,8,32]{3,1,2,0:T(8,128)(2,1)} %copy.56, bf16[128,32,4,1]{1,2,3,0:T(4,128)(2,1)S(1)} %copy.58), kind=kOutput, calls=%fused_computation.12.clone.1 | convolution fusion | flops 8519680 | bytes 2392064 | tf_op jit(solution)/shard_map/while/body/eval_jaxpr/nawb,nbe->nawe/dot_general | solution.py:55
  66.1 1.1 copy.59
  68.1 6.5 %gather_fusion = bf16[128,8192]{1,0:T(8,128)(2,1)} fusion(bf16[64,8192]{1,0:T(8,128)(2,1)} %get-tuple-element.145, s32[1024]{0:T(1024)S(1)} %pad_clamp_fusion.8), kind=kCustom, calls=%fused_computation.clone.1 | custom fusion | bytes 4194816 | tf_op jit(solution)/shard_map/while/body/eval_jaxpr/gather | solution.py:53
  74.6 3.2 copy.55
  77.8 11.7 %copy.56 = bf16[128,32,8,32]{3,1,2,0:T(8,128)(2,1)} copy(bf16[128,32,8,32]{0,3,2,1:T(8,128)(2,1)S(1)} %bitcast.108) | data formatting | bytes 4194304 | tf_op jit(solution)/shard_map/while/body/eval_jaxpr/reshape | solution.py:53
  90.6 14.3 %convolution_convert_fusion.5 = bf16[128,32,8,4]{1,3,2,0:T(4,128)(2,1)S(1)} fusion(bf16[128,32,8,32]{3,1,2,0:T(8,128)(2,1)} %copy.56, bf16[128,32,4,1]{1,2,3,0:T(4,128)(2,1)S(1)} %copy.58), kind=kOutput, calls=%fused_computation.12.clone.1 | convolution fusion | flops 8519680 | bytes 2392064 | tf_op jit(solution)/shard_map/while/body/eval_jaxpr/nawb,nbe->nawe/dot_general | solution.py:55
  104.8 1.1 copy.59
  106.8 6.5 %gather_fusion = bf16[128,8192]{1,0:T(8,128)(2,1)} fusion(bf16[64,8192]{1,0:T(8,128)(2,1)} %get-tuple-element.145, s32[1024]{0:T(1024)S(1)} %pad_clamp_fusion.8), kind=kCustom, calls=%fused_computation.clone.1 | custom fusion | bytes 4194816 | tf_op jit(solution)/shard_map/while/body/eval_jaxpr/gather | solution.py:53
  113.3 3.2 copy.55
  116.5 11.7 %copy.56 = bf16[128,32,8,32]{3,1,2,0:T(8,128)(2,1)} copy(bf16[128,32,8,32]{0,3,2,1:T(8,128)(2,1)S(1)} %bitcast.108) | data formatting | bytes 4194304 | tf_op jit(solution)/shard_map/while/body/eval_jaxpr/reshape | solution.py:53
  128.3 0.7 gather_fusion.1
  129.3 14.3 %convolution_convert_fusion.5 = bf16[128,32,8,4]{1,3,2,0:T(4,128)(2,1)S(1)} fusion(bf16[128,32,8,32]{3,1,2,0:T(8,128)(2,1)} %copy.56, bf16[128,32,4,1]{1,2,3,0:T(4,128)(2,1)S(1)} %copy.58), kind=kOutput, calls=%fused_computation.12.clone.1 | convolution fusion | flops 8519680 | bytes 2392064 | tf_op jit(solution)/shard_map/while/body/eval_jaxpr/nawb,nbe->nawe/dot_general | solution.py:55
  143.5 1.1 copy.59
  145.5 6.5 %gather_fusion = bf16[128,8192]{1,0:T(8,128)(2,1)} fusion(bf16[64,8192]{1,0:T(8,128)(2,1)} %get-tuple-element.145, s32[1024]{0:T(1024)S(1)} %pad_clamp_fusion.8), kind=kCustom, calls=%fused_computation.clone.1 | custom fusion | bytes 4194816 | tf_op jit(solution)/shard_map/while/body/eval_jaxpr/gather | solution.py:53
  152.0 3.2 copy.55
  155.2 11.7 %copy.56 = bf16[128,32,8,32]{3,1,2,0:T(8,128)(2,1)} copy(bf16[128,32,8,32]{0,3,2,1:T(8,128)(2,1)S(1)} %bitcast.108) | data formatting | bytes 4194304 | tf_op jit(solution)/shard_map/while/body/eval_jaxpr/reshape | solution.py:53
  168.0 14.3 %convolution_convert_fusion.5 = bf16[128,32,8,4]{1,3,2,0:T(4,128)(2,1)S(1)} fusion(bf16[128,32,8,32]{3,1,2,0:T(8,128)(2,1)} %copy.56, bf16[128,32,4,1]{1,2,3,0:T(4,128)(2,1)S(1)} %copy.58), kind=kOutput, calls=%fused_computation.12.clone.1 | convolution fusion | flops 8519680 | bytes 2392064 | tf_op jit(solution)/shard_map/while/body/eval_jaxpr/nawb,nbe->nawe/dot_general | solution.py:55
  182.2 1.1 copy.59
  183.8 2.0 gather_fusion.8
  185.8 6.9 %gather_fusion.5 = s32[1024]{0:T(1024)S(1)} fusion(s32[512]{0:T(512)S(1)} %bitcast.106, s32[1024]{0:T(1024)S(1)} %fusion.18), kind=kCustom, calls=%fused_computation.5 | custom fusion | bytes 12288 | tf_op jit(solution)/shard_map/jit(_take)/gather | solution.py:27
  192.6 0.8 broadcast_select_fusion.1
  194.1 4.4 %reshape.359 = bf16[512,32,32]{2,1,0:T(8,128)(2,1)} reshape(bf16[4,128,1024]{2,1,0:T(8,128)(2,1)S(1)} %get-tuple-element.66) | data formatting | bytes 2097152 | tf_op jit(solution)/shard_map/reshape;reshape | solution.py:123
  198.4 4.9 %all-to-all-start.2 = ((s32[8,1,128]{2,1,0:T(1,128)}), s32[8,1,128]{2,1,0:T(1,128)S(1)}, u32[]{:S(2)}, u32[]{:S(2)}) async-start(s32[8,1,128]{2,1,0:T(1,128)} %bitcast.28), calls=%async_computation.2 | async-start | bytes 8192 | tf_op jit(solution)/shard_map/all_to_all | solution.py:119
  203.3 2.2 gather_fusion.3
  205.5 3.3 all-to-all-done.2
  208.8 4.2 %all-to-all-start.4 = ((bf16[4,128,256]{2,1,0:T(8,128)(2,1)}), bf16[4,128,256]{2,1,0:T(8,128)(2,1)S(1)}, u32[]{:S(2)}, u32[]{:S(2)}) async-start(bf16[4,128,256]{2,1,0:T(8,128)(2,1)} %broadcast_select_fusion.1), calls=%async_computation.4 | async-start | bytes 524288 | tf_op jit(solution)/shard_map/all_to_all | solution.py:102
  213.0 5.4 %all-to-all-done.4 = bf16[4,128,256]{2,1,0:T(8,128)(2,1)S(1)} async-done(((bf16[4,128,256]{2,1,0:T(8,128)(2,1)}), bf16[4,128,256]{2,1,0:T(8,128)(2,1)S(1)}, u32[]{:S(2)}, u32[]{:S(2)}) %all-to-all-start.4) | async-done | bytes 262176 | tf_op jit(solution)/shard_map/all_to_all | solution.py:102
  218.4 3.4 all-to-all-start.1
  221.8 4.6 %gather_fusion.6 = bf16[1024,256]{1,0:T(8,128)(2,1)} fusion(f32[128,256]{1,0:T(8,128)S(1)} %copy-done.2, s32[1024]{0:T(1024)S(1)} %broadcast_clamp_fusion), kind=kCustom, calls=%fused_computation.6 | custom fusion | bytes 1052672 | tf_op jit(solution)/shard_map/gather | solution.py:120
  226.4 0.7 all-to-all-done.1
  227.1 3.5 all-to-all-start.3
  231.0 1.7 copy.36
  232.7 4.8 %fusion.25 = f32[512,8,32]{2,1,0:T(8,128)S(1)} fusion(bf16[512,8,32]{2,1,0:T(8,128)(2,1)} %copy.36, bf16[512,32,32]{2,1,0:T(8,128)(2,1)} %reshape.359), kind=kOutput, calls=%fused_computation.83 | convolution fusion | flops 8388608 | bytes 1835008 | tf_op jit(solution)/shard_map/kej,kaj->kea/dot_general | solution.py:126
  237.4 1.5 copy.38
  238.9 1.2 copy.39
  240.2 3.5 gather_fusion.9
  243.7 1.2 broadcast_select_fusion
  244.9 1.0 all-to-all-done.3
  245.9 4.0 %all-to-all-start.5 = ((f32[8,128,256]{2,1,0:T(8,128)}), f32[8,128,256]{2,1,0:T(8,128)S(1)}, u32[]{:S(2)}, u32[]{:S(2)}) async-start(f32[8,128,256]{2,1,0:T(8,128)} %broadcast_select_fusion), calls=%async_computation.5 | async-start | bytes 2097152 | tf_op jit(solution)/shard_map/all_to_all | solution.py:135
  250.2 0.9 fusion.4
  251.2 1.2 gather_fusion.4
  252.5 63.3 %all-reduce.3.cloned.1.call-done = f32[256,256]{1,0:T(8,128)} async-done(((f32[256,256]{1,0:T(8,128)}), f32[256,256]{1,0:T(8,128)}) %all-reduce.3.cloned.1.call-update) | async-done | bytes 262160 | tf_op jit(solution)/shard_map/psum | solution.py:104
  315.8 1.1 multiply_reduce_fusion
  317.5 1.8 divide_subtract_fusion
  319.2 1.9 gather_fusion.7
  321.3 0.8 copy.32
  322.1 1.2 fusion.5
  323.4 3.4 convolution_convert_fusion.1
  326.8 0.7 copy.34
  327.5 0.9 fusion.6
  328.4 35.9 %all-reduce.5.cloned.1.call-done = f32[128,256]{1,0:T(8,128)} async-done(((f32[128,256]{1,0:T(8,128)}), f32[128,256]{1,0:T(8,128)}) %all-reduce.5.cloned.1.call-update) | async-done | bytes 131088 | tf_op jit(solution)/shard_map/psum | solution.py:139
  364.2 1.6 multiply_subtract_fusion
  (97 shorter events, 13.2 us)
Async XLA Ops:
  8.0 175.5 %copy-start = (bf16[64,256]{1,0:T(8,128)(2,1)S(1)}, bf16[64,256]{1,0:T(8,128)(2,1)}, u32[]{:S(2)}) copy-start(bf16[64,256]{1,0:T(8,128)(2,1)} %param.29) | copy-start | bytes 98308
  17.3 181.1 %all-to-all-start = ((s32[4,1,128]{2,1,0:T(1,128)}), s32[4,1,128]{2,1,0:T(1,128)S(1)}, u32[]{:S(2)}, u32[]{:S(2)}) async-start(s32[4,1,128]{2,1,0:T(1,128)} %bitcast.17), calls=%async_computation | async-start | bytes 4096 | tf_op jit(solution)/shard_map/all_to_all | solution.py:94
  28.7 154.8 %copy-start.8 = (s32[1,256]{1,0:T(1,128)S(1)}, s32[1,256]{1,0:T(1,128)}, u32[]{:S(2)}) copy-start(s32[1,256]{1,0:T(1,128)} %param.20) | copy-start | bytes 3076
  39.1 11.7 %copy-start.3 = (bf16[64,128]{1,0:T(8,128)(2,1)S(1)}, bf16[64,128]{1,0:T(8,128)(2,1)}, u32[]{:S(2)}) copy-start(bf16[64,128]{1,0:T(8,128)(2,1)} %get-tuple-element.147) | copy-start | bytes 49156 | tf_op jit(solution)/shard_map/while
  77.8 11.7 %copy-start.3 = (bf16[64,128]{1,0:T(8,128)(2,1)S(1)}, bf16[64,128]{1,0:T(8,128)(2,1)}, u32[]{:S(2)}) copy-start(bf16[64,128]{1,0:T(8,128)(2,1)} %get-tuple-element.147) | copy-start | bytes 49156 | tf_op jit(solution)/shard_map/while
  116.5 11.7 %copy-start.3 = (bf16[64,128]{1,0:T(8,128)(2,1)S(1)}, bf16[64,128]{1,0:T(8,128)(2,1)}, u32[]{:S(2)}) copy-start(bf16[64,128]{1,0:T(8,128)(2,1)} %get-tuple-element.147) | copy-start | bytes 49156 | tf_op jit(solution)/shard_map/while
  155.2 11.7 %copy-start.3 = (bf16[64,128]{1,0:T(8,128)(2,1)S(1)}, bf16[64,128]{1,0:T(8,128)(2,1)}, u32[]{:S(2)}) copy-start(bf16[64,128]{1,0:T(8,128)(2,1)} %get-tuple-element.147) | copy-start | bytes 49156 | tf_op jit(solution)/shard_map/while
  183.5 2.2 copy-start.1
  185.7 17.6 %copy-start.4 = (f32[256,256]{1,0:T(8,128)S(1)}, f32[256,256]{1,0:T(8,128)}, u32[]{:S(2)}) copy-start(f32[256,256]{1,0:T(8,128)} %param.16) | copy-start | bytes 786436
  194.0 27.7 %copy-start.2 = (f32[128,256]{1,0:T(8,128)S(1)}, f32[128,256]{1,0:T(8,128)}, u32[]{:S(2)}) copy-start(f32[128,256]{1,0:T(8,128)} %param.26) | copy-start | bytes 393220
  198.4 10.4 %all-to-all-start.2 = ((s32[8,1,128]{2,1,0:T(1,128)}), s32[8,1,128]{2,1,0:T(1,128)S(1)}, u32[]{:S(2)}, u32[]{:S(2)}) async-start(s32[8,1,128]{2,1,0:T(1,128)} %bitcast.28), calls=%async_computation.2 | async-start | bytes 8192 | tf_op jit(solution)/shard_map/all_to_all | solution.py:119
  203.3 27.3 %copy-start.7 = (s32[1,512]{1,0:T(1,128)S(1)}, s32[1,512]{1,0:T(1,128)}, u32[]{:S(2)}) copy-start(s32[1,512]{1,0:T(1,128)} %param.25) | copy-start | bytes 6148
  208.8 9.6 %all-to-all-start.4 = ((bf16[4,128,256]{2,1,0:T(8,128)(2,1)}), bf16[4,128,256]{2,1,0:T(8,128)(2,1)S(1)}, u32[]{:S(2)}, u32[]{:S(2)}) async-start(bf16[4,128,256]{2,1,0:T(8,128)(2,1)} %broadcast_select_fusion.1), calls=%async_computation.4 | async-start | bytes 524288 | tf_op jit(solution)/shard_map/all_to_all | solution.py:102
  218.4 8.8 %copy-start.5 = (bf16[4,128,256]{2,1,0:T(8,128)(2,1)}, bf16[4,128,256]{2,1,0:T(8,128)(2,1)S(1)}, u32[]{:S(2)}) copy-start(bf16[4,128,256]{2,1,0:T(8,128)(2,1)S(1)} %all-to-all-done.4) | copy-start | bytes 786436
  218.4 8.8 %all-to-all-start.1 = ((bf16[4,128,256]{2,1,0:T(8,128)(2,1)}), bf16[4,128,256]{2,1,0:T(8,128)(2,1)S(1)}, u32[]{:S(2)}, u32[]{:S(2)}) async-start(bf16[4,128,256]{2,1,0:T(8,128)(2,1)} %bitcast.19), calls=%async_computation.1 | async-start | bytes 524288 | tf_op jit(solution)/shard_map/all_to_all | solution.py:96
  227.1 18.8 %all-to-all-start.3 = ((bf16[8,128,256]{2,1,0:T(8,128)(2,1)}), bf16[8,128,256]{2,1,0:T(8,128)(2,1)S(1)}, u32[]{:S(2)}, u32[]{:S(2)}) async-start(bf16[8,128,256]{2,1,0:T(8,128)(2,1)} %bitcast.30), calls=%async_computation.3 | async-start | bytes 1048576 | tf_op jit(solution)/shard_map/all_to_all | solution.py:121
  243.7 6.5 %copy-start.6 = (bf16[4,128,256]{2,1,0:T(8,128)(2,1)S(1)}, bf16[4,128,256]{2,1,0:T(8,128)(2,1)}, u32[]{:S(2)}) copy-start(bf16[4,128,256]{2,1,0:T(8,128)(2,1)} %copy-done.5) | copy-start | bytes 786436
  243.7 73.2 %copy-start.9 = (f32[256]{0:T(256)S(1)}, f32[256]{0:T(256)}, u32[]{:S(2)}) copy-start(f32[256]{0:T(256)} %param.17) | copy-start | bytes 3076
  245.9 76.2 %all-to-all-start.5 = ((f32[8,128,256]{2,1,0:T(8,128)}), f32[8,128,256]{2,1,0:T(8,128)S(1)}, u32[]{:S(2)}, u32[]{:S(2)}) async-start(f32[8,128,256]{2,1,0:T(8,128)} %broadcast_select_fusion), calls=%async_computation.5 | async-start | bytes 2097152 | tf_op jit(solution)/shard_map/all_to_all | solution.py:135
  249.9 66.0 %all-reduce.3.cloned.1.call-start = ((), (), s32[]{:S(2)}) async-start(), calls=%async_computation.6 | async-start | bytes 524288 | tf_op jit(solution)/shard_map/psum | solution.py:104
  251.1 113.1 %all-reduce.5.cloned.1.call-start = ((), (), s32[]{:S(2)}) async-start(), calls=%async_computation.7 | async-start | bytes 262144 | tf_op jit(solution)/shard_map/psum | solution.py:139
Sparse Core Ops, SparseCore 0:
  253.6 62.2 all-reduce.2
Sparse Core Ops, SparseCore 1:
  323.5 40.7 all-reduce.4
where the time goes:
time: 375 us; the launch traced here: 373 us
  local copies, waits for them, and re-layouts  135 us (36%)
  waiting for transfers between devices  110 us (29%)
  matrix products  68.8 us (18%)
  starting transfers between devices  25.2 us (7%)
  other arithmetic  18 us (5%)
  between operations  15.8 us (4%)
    psum x1, waiting for transfers between devices, local(): total_grad = lax.psum(row_grad, 'tt')  63.3 us
    dot_general x4, matrix products, rank_one_block(): jnp.einsum('nawb,nbe->nawe', mid_cores, last_cores, preferred_element_typ...  57 us
    reshape x4, local copies, waits for them, and re-layouts, rank_one_block(): mid_cores = core_mid[mid_part].reshape(-1, RANK, E2, RANK)  46.9 us
    gather x8, local copies, waits for them, and re-layouts, rank_one_block(): mid_cores = core_mid[mid_part].reshape(-1, RANK, E2, RANK)  38.8 us
    psum x1, waiting for transfers between devices, local(): core_total = lax.psum(core_grad, 'hot')  35.9 us
    gather x4, local copies, waits for them, and re-layouts, packed(): return jnp.take(values, source, axis=0, mode='fill', fill_value=fill_value)  15.9 us
  transfers between devices with their start and end apart: 8, of which 6 were waited for; matrix products, arithmetic and copies ran while one was open for 56% of the time, Pallas kernels for 0%

commit v1 on v0

v1 whole, which is shorter than its diff:
```python
import jax
import jax.numpy as jnp
from jax import lax
from jax.experimental import pallas as pl
from jax.experimental.pallas import tpu as pltpu
from jax.sharding import PartitionSpec as P

E1 = 8
E2 = 8
E3 = 4
RANK = 32
TAIL = E2 * E3
LANES = 128
PAD = 16
F32 = jnp.float32
BF16 = jnp.bfloat16
NT = (((1,), (1,)), ((), ()))


def iota(shape, dim):
    return lax.broadcasted_iota(jnp.int32, shape, dim)


def hot(mask):
    return mask.astype(F32).astype(BF16)


def mm(a, b):
    return jnp.dot(a, b, preferred_element_type=F32)


def mm_nt(a, b):
    return lax.dot_general(a, b, NT, preferred_element_type=F32)


def call(body, name, outs, scratch=()):
    return pl.pallas_call(
        body,
        out_shape=tuple(jax.ShapeDtypeStruct(s, d) for s, d in outs),
        scratch_shapes=[pltpu.VMEM(s, d) for s, d in scratch],
        name=name,
    )


def smem():
    return pl.BlockSpec(memory_space=pltpu.SMEM)


def pack_kernel(table, grads, owner, row, bag, first, hot_out, first_out):
    rows, bags = table.shape[0], grads.shape[0]
    looks = jnp.concatenate(
        [owner[...], row[...], bag[...], jnp.zeros((PAD - 3, row.shape[1]), jnp.int32)], axis=0
    )
    turned = first[...].T.astype(BF16)
    for peer in range(hot_out.shape[0]):
        hot_out[peer, 0:rows, :] = table[...].astype(BF16)
        hot_out[peer, rows : rows + bags, :] = grads[...]
        hot_out[peer, rows + bags :, :] = looks.astype(F32).astype(BF16)
    for peer in range(first_out.shape[0]):
        first_out[peer] = turned


def maps_kernel(
    side, mid, last, mid_index, last_index, bag, owner, index, grads,
    keep, send, maps, turned, left, right, lasts_of, cot, terms,
):
    mids, lasts = mid.shape[0], last.shape[0]
    looks = bag.shape[1]

    def turn(t, _):
        at = pl.ds(pl.multiple_of(t * LANES, LANES), LANES)
        block = mid[:, at].astype(F32)
        turned[at, :] = jnp.concatenate([block, block], axis=0).T
        return 0

    lax.fori_loop(0, mid.shape[1] // LANES, turn, 0, unroll=4)
    first_half = iota((RANK * E2, 2 * mids), 1) < mids
    for pair in range(RANK // 2):
        low = turned[pl.ds(2 * pair, RANK * E2, stride=RANK), :]
        high = turned[pl.ds(2 * pair + 1, RANK * E2, stride=RANK), :]
        left[:, pair * 2 * mids : (pair + 1) * 2 * mids] = jnp.where(first_half, low, high).astype(BF16)
    pick_last = hot(iota((lasts, looks), 0) == last_index[...])
    lasts_of[...] = mm(last[...].astype(F32).T.astype(BF16), pick_last)
    pick_bag = hot(iota((grads.shape[0], looks), 0) == bag[...])
    cot[...] = mm(grads[...].astype(F32).T.astype(BF16), pick_bag)
    pick_mid = hot(iota((mids, looks), 0) == mid_index[...])
    for e3 in range(E3):
        for b in range(RANK):
            at = b * E3 + e3
            spread = jnp.broadcast_to(lasts_of[at : at + 1, :], (PAD, looks)).astype(BF16)
            for part in range(0, mids, PAD):
                right[b * mids + part : b * mids + part + PAD, :] = pick_mid[part : part + PAD, :] * spread
        made = mm(left[...], right[...]).astype(BF16).astype(F32)
        for t in range(looks // LANES):
            maps[t, e3 * RANK * E2 : (e3 + 1) * RANK * E2, :] = made[:, t * LANES : (t + 1) * LANES]

    def back(t, _):
        lanes = pl.ds(pl.multiple_of(t * LANES, LANES), LANES)
        sums = [jnp.zeros((RANK, LANES), F32) for _ in range(E1)]
        for e2 in range(E2):
            for e3 in range(E3):
                part = maps[t, pl.ds(e3 * RANK * E2 + e2, RANK, stride=E2), :]
                for e1 in range(E1):
                    at = e1 * TAIL + e2 * E3 + e3
                    sums[e1] = sums[e1] + part * cot[at : at + 1, lanes]
        for e1 in range(E1):
            terms[e1 * RANK : (e1 + 1) * RANK, lanes] = sums[e1]
        return 0

    lax.fori_loop(0, looks // LANES, back, 0)
    whole = terms[...]
    high = whole.astype(BF16)
    low = (whole - high.astype(F32)).astype(BF16)
    own = owner[...]
    held = keep.shape[0]
    slices = held // side[1]
    key = ((own & 1) ^ side[0]) * held + (own >> 1) * slices + index[...]
    step = min(held, 256)
    for half, out in ((0, keep), (1, send)):
        for start in range(0, held, step):
            pick = hot(iota((step, looks), 0) + (half * held + start) == key)
            out[start : start + step, :] = (mm_nt(pick, high) + mm_nt(pick, low)).astype(out.dtype)


def hot_kernel(side, gathered, owner, row, bag, keep, send, pooled):
    peers, bags = gathered.shape[0], pooled.shape[0]
    looks = row.shape[1]
    half = keep.shape[0]
    rows = 2 * half
    at = iota((rows, looks), 0)
    pick_bag = hot(iota((bags, looks), 0) == bag[...])
    mine = row[...]
    total = jnp.zeros(pooled.shape, F32)
    for peer in range(peers):
        pick = hot((at == mine) & (owner[...] == peer))
        total = total + mm(mm_nt(pick_bag, pick).astype(BF16), gathered[peer, 0:rows, :])
    pooled[...] = total
    grad = jnp.zeros((rows, pooled.shape[1]), F32)
    for peer in range(peers):
        sent = gathered[peer, rows + bags :, :].astype(F32).astype(jnp.int32)
        theirs, place, their_bag = sent[0:1, :], sent[1:2, :], sent[2:3, :]
        upper = (place >= half).astype(jnp.int32)
        place = (upper ^ side[0]) * half + place - upper * half
        pick = hot((at == place) & (theirs == side[1]))
        count = mm_nt(pick, hot(iota((bags, looks), 0) == their_bag))
        grad = grad + mm(count.astype(BF16), gathered[peer, rows : rows + bags, :])
    keep[...] = grad[0:half]
    send[...] = grad[half:].astype(BF16)


def pair_kernel(cold_keep, cold_got, hot_keep, hot_got, out):
    peers = out.shape[0]
    slices = cold_keep.shape[0] // peers
    hot_sum = (hot_keep[...] + hot_got[...].astype(F32)).astype(BF16)
    for peer in range(peers):
        at = slice(peer * slices, (peer + 1) * slices)
        out[peer, 0:slices, :] = (cold_keep[at, :] + cold_got[at, :].astype(F32)).astype(BF16)
        out[peer, slices:, :] = hot_sum


def line_kernel(got, cold, hot_half):
    slices = cold.shape[1]
    total = got[0].astype(F32)
    for peer in range(1, got.shape[0]):
        total = total + got[peer].astype(F32)
    sent = total[0:slices].astype(BF16)
    for peer in range(cold.shape[0]):
        cold[peer] = sent
    hot_half[...] = total[slices:]


def rows_kernel(gathered, maps, owner, index, bag, hot_part, pooled, slices_of, rows):
    peers, width, slices = gathered.shape
    looks = bag.shape[1]
    tiles = looks // LANES
    key = owner[...] * slices + index[...]
    total = jnp.zeros((width, looks), F32)
    for peer in range(peers):
        pick = hot(iota((slices, looks), 0) + peer * slices == key)
        total = total + mm(gathered[peer], pick)
    for t in range(tiles):
        slices_of[t] = total[:, t * LANES : (t + 1) * LANES]

    def forward(t, _):
        sums = [[jnp.zeros((E2, LANES), F32) for _ in range(E3)] for _ in range(E1)]
        for a in range(RANK):
            parts = [maps[t, e3 * RANK * E2 + a * E2 : e3 * RANK * E2 + a * E2 + E2, :] for e3 in range(E3)]
            for e1 in range(E1):
                entry = slices_of[t, e1 * RANK + a : e1 * RANK + a + 1, :]
                for e3 in range(E3):
                    sums[e1][e3] = sums[e1][e3] + parts[e3] * entry
        for e1 in range(E1):
            for e3 in range(E3):
                rows[t, pl.ds(e1 * TAIL + e3, E2, stride=E3), :] = sums[e1][e3]
        return 0

    lax.fori_loop(0, tiles, forward, 0)
    out = hot_part[...]
    for t in range(tiles):
        pick = hot(iota((pooled.shape[0], LANES), 0) == bag[:, t * LANES : (t + 1) * LANES])
        out = out + mm_nt(pick, rows[t].astype(BF16))
    pooled[...] = out


def final_kernel(side, cold, first, mine, other, table, accum, new_first, new_table, new_accum):
    total = cold[0].astype(F32)
    for peer in range(1, cold.shape[0]):
        total = total + cold[peer].astype(F32)
    new_first[...] = first[...] - 0.01 * total
    lower = side[0] == 0
    grad = jnp.concatenate(
        [jnp.where(lower, mine[...], other[...]), jnp.where(lower, other[...], mine[...])], axis=0
    )
    rows = grad.shape[0]
    mean = jnp.mean(grad * grad, axis=1, keepdims=True)
    held = jnp.broadcast_to(accum[...], (LANES, rows)).T + mean
    new_accum[...] = held.T[0:1, :]
    new_table[...] = table[...] - 0.1 * grad / (jnp.sqrt(held[:, 0:1]) + 1e-08)


def local(
    hot_table, hot_accum, hot_owner, hot_row, hot_bag, cold_owner, first_index,
    mid_index, last_index, cold_bag, core_first, core_mid, core_last, bag_grads,
):
    rows, width = hot_table.shape
    bags = bag_grads.shape[0]
    slices = core_first.shape[0]
    hot_peers, tt_peers = lax.axis_size("hot"), lax.axis_size("tt")
    pairs = tt_peers // 2
    looks = cold_bag.shape[1]
    assert max(rows, bags, hot_peers) <= 256
    core = lax.axis_index("tt") % 2
    owner = hot_owner.reshape(1, -1)
    slice_owner = cold_owner.reshape(1, -1)
    swap = [(i, i ^ 1) for i in range(tt_peers)]

    hot_pack, first_pack = call(
        pack_kernel, "pack",
        (((hot_peers, rows + bags + PAD, width), BF16), ((tt_peers, width, slices), BF16)),
    )(hot_table, bag_grads, owner, hot_row, hot_bag, core_first)
    hot_all = lax.all_to_all(hot_pack, "hot", 0, 0, tiled=True)
    first_all = lax.all_to_all(first_pack, "tt", 0, 0, tiled=True)

    held = slices * pairs
    side = jnp.stack([core, jnp.int32(pairs)])
    keep, send, maps = pl.pallas_call(
        maps_kernel,
        out_shape=(
            jax.ShapeDtypeStruct((held, width), F32),
            jax.ShapeDtypeStruct((held, width), BF16),
            jax.ShapeDtypeStruct((looks // LANES, E3 * RANK * E2, LANES), F32),
        ),
        in_specs=[smem()] + [pl.BlockSpec(memory_space=pltpu.VMEM)] * 8,
        scratch_shapes=[
            pltpu.VMEM((core_mid.shape[1], LANES), F32),
            pltpu.VMEM((RANK * E2, RANK * core_mid.shape[0]), BF16),
            pltpu.VMEM((RANK * core_mid.shape[0], looks), BF16),
            pltpu.VMEM((RANK * E3, looks), F32),
            pltpu.VMEM((width, looks), F32),
            pltpu.VMEM((width, looks), F32),
        ],
        name="maps",
    )(side, core_mid, core_last, mid_index, last_index, cold_bag, slice_owner, first_index, bag_grads)
    got = lax.ppermute(send, "tt", swap)

    side = jnp.stack([core, lax.axis_index("hot")])
    hot_keep, hot_send, hot_part = pl.pallas_call(
        hot_kernel,
        out_shape=(
            jax.ShapeDtypeStruct((rows // 2, width), F32),
            jax.ShapeDtypeStruct((rows // 2, width), BF16),
            jax.ShapeDtypeStruct((bags, width), F32),
        ),
        in_specs=[smem()] + [pl.BlockSpec(memory_space=pltpu.VMEM)] * 4,
        name="hot",
    )(side, hot_all, owner, hot_row, hot_bag)
    hot_got = lax.ppermute(hot_send, "tt", swap)

    (line_send,) = call(
        pair_kernel, "pair", (((pairs, slices + rows // 2, width), BF16),)
    )(keep, got, hot_keep, hot_got)
    lines = [list(range(c, tt_peers, 2)) for c in range(2)]
    line_got = lax.all_to_all(line_send, "tt", 0, 0, axis_index_groups=lines, tiled=True)

    (pooled,) = call(
        rows_kernel, "rows", (((bags, width), F32),),
        (((looks // LANES, width, LANES), F32), ((looks // LANES, width, LANES), F32)),
    )(first_all, maps, slice_owner, first_index, cold_bag, hot_part)

    cold_send, hot_half = call(
        line_kernel, "line", (((hot_peers, slices, width), BF16), ((rows // 2, width), F32))
    )(line_got)
    cold_got = lax.all_to_all(cold_send, "hot", 0, 0, tiled=True)
    hot_other = lax.ppermute(hot_half, "tt", swap)

    new_first, new_table, new_accum = pl.pallas_call(
        final_kernel,
        out_shape=(
            jax.ShapeDtypeStruct((slices, width), F32),
            jax.ShapeDtypeStruct((rows, width), F32),
            jax.ShapeDtypeStruct((1, rows), F32),
        ),
        in_specs=[smem()] + [pl.BlockSpec(memory_space=pltpu.VMEM)] * 6,
        name="final",
    )(side, cold_got, core_first, hot_half, hot_other, hot_table, hot_accum.reshape(1, -1))
    return pooled, new_table, new_accum.reshape(-1), new_first


def solution(mesh):
    both = P(("hot", "tt"), None)
    placed = (
        P("hot", None), P("hot"), both, both, both, both, both, both, both, both,
        P("tt", None), P(), P(), both,
    )
    return jax.shard_map(
        local,
        mesh=mesh,
        in_specs=placed,
        out_specs=(both, P("hot", None), P("hot"), P("tt", None)),
        check_vma=False,
    )
```

time: 375 us -> 80.1 us (0.21)
  local copies, waits for them, and re-layouts: 135 us -> 2.18 us
  waiting for transfers between devices: 110 us -> 15.3 us
  matrix products: 68.8 us -> 0 us
  Pallas kernels: 0 us -> 26.8 us
  blocking collectives: 0 us -> 20 us
  other arithmetic: 18 us -> 1.25 us
  between operations: 15.8 us -> 0.66 us
  starting transfers between devices: 25.2 us -> 13.4 us
    psum x2 -> x0, waiting for transfers between devices: 99.2 us -> none  [the longest x1 63.3 us: local(): total_grad = lax.psum(row_grad, 'tt')]
    dot_general x11 -> x0, matrix products: 68.8 us -> none  [the longest x4 57 us: rank_one_block(): jnp.einsum('nawb,nbe->nawe', mid_cores, last_cores, preferred_element_typ...]
    gather x26 -> x0, local copies, waits for them, and re-layouts: 68.1 us -> none  [the longest x8 38.8 us: rank_one_block(): mid_cores = core_mid[mid_part].reshape(-1, RANK, E2, RANK)]
    reshape x11 -> x0, local copies, waits for them, and re-layouts: 51.2 us -> none  [the longest x4 46.9 us: rank_one_block(): mid_cores = core_mid[mid_part].reshape(-1, RANK, E2, RANK)]
    pallas_call x0 -> x7, Pallas kernels: none -> 26.8 us  [the longest x1 11.3 us: local(): pl.pallas_call(maps_kernel, out_shape=(jax.ShapeDtypeStruct((held, width)...]
    all_to_all x0 -> x1, blocking collectives: none -> 20 us  [local(): lax.all_to_all(line_send, 'tt', 0, 0, axis_index_groups=lines, tiled=True)]
    all_to_all x6 -> x3, starting transfers between devices: 25.2 us -> 12.9 us  [the longest x1 5.19 us: local(): hot_all = lax.all_to_all(hot_pack, 'hot', 0, 0, tiled=True)]
    select_n x11 -> x0, other arithmetic: 7.4 us -> none  [the longest x5 3.19 us: packed(): return jnp.take(values, source, axis=0, mode='fill', fill_value=fill_value)]
  transfers between devices with their start and end apart: 8 -> 6, of which waited for: 6 -> 3; matrix products, arithmetic and copies ran while one was open for 56% -> 2% of each run, Pallas kernels for 0% -> 26%
where the time goes in v1:
time: 80.1 us; the launch traced here: 79.5 us
  Pallas kernels  26.8 us (33%)
  blocking collectives  20 us (25%)
  waiting for transfers between devices  15.3 us (19%)
  starting transfers between devices  13.4 us (17%)
  local copies, waits for them, and re-layouts  2.18 us (3%)
  other arithmetic  1.25 us (2%)
    all_to_all x1, blocking collectives, local(): lax.all_to_all(line_send, 'tt', 0, 0, axis_index_groups=lines, tiled=True)  20 us
    all_to_all x1, waiting for transfers between devices, local(): first_all = lax.all_to_all(first_pack, 'tt', 0, 0, tiled=True)  13.4 us
    pallas_call x1, Pallas kernels, local(): pl.pallas_call(maps_kernel, out_shape=(jax.ShapeDtypeStruct((held, width)...  11.3 us
    all_to_all x1, starting transfers between devices, local(): hot_all = lax.all_to_all(hot_pack, 'hot', 0, 0, tiled=True)  5.19 us
    pallas_call x1, Pallas kernels, local(): call(rows_kernel, 'rows', (((bags, width), F32),), (((looks // LANES, wid...  4.61 us
    all_to_all x1, starting transfers between devices, local(): cold_got = lax.all_to_all(cold_send, 'hot', 0, 0, tiled=True)  4.2 us
    all_to_all x1, starting transfers between devices, local(): first_all = lax.all_to_all(first_pack, 'tt', 0, 0, tiled=True)  3.49 us
    pallas_call x1, Pallas kernels, local(): pl.pallas_call(hot_kernel, out_shape=(jax.ShapeDtypeStruct((rows // 2, wi...  2.65 us
  transfers between devices with their start and end apart: 6, of which 3 were waited for; matrix products, arithmetic and copies ran while one was open for 2% of the time, Pallas kernels for 26%

profile of v1, /device:TPU:0, one launch (start us, length us, event | category | flops | bytes accessed | tf_op | source)
XLA Modules:
  0.0 79.5 jit_solution(3588343753555254345)
XLA Ops:
  0.6 2.1 %pack.1 = (bf16[4,336,256]{2,1,0:T(8,128)(2,1)}, bf16[8,256,128]{2,1,0:T(8,128)(2,1)}) custom-call(f32[256,256]{1,0:T(8,128)} %table.3, bf16[64,256]{1,0:T(8,128)(2,1)} %grads.3, s32[1,256]{1,0:T(1,128)} %bitcast.8, s32[1,256]{1,0:T(1,128)} %row.3, s32[1,256]{1,0:T(1,128)} %bag.6, f32[128,256]{1,0:T(8,128)} %first.3), custom_call_target="tpu_custom_call" | custom-call | tf_op jit(solution)/shard_map/pack/pallas_call | solution.py:237
  2.8 5.2 %all-to-all-start.1 = ((bf16[4,336,256]{2,1,0:T(8,128)(2,1)}), bf16[4,336,256]{2,1,0:T(8,128)(2,1)S(1)}, u32[]{:S(2)}, u32[]{:S(2)}) async-start(bf16[4,336,256]{2,1,0:T(8,128)(2,1)} %get-tuple-element.19), calls=%async_computation.1 | async-start | bytes 1376256 | tf_op jit(solution)/shard_map/all_to_all | solution.py:241
  8.0 0.6 pad_add_fusion.side
  8.6 11.3 %maps.1 = (f32[512,256]{1,0:T(8,128)}, bf16[512,256]{1,0:T(8,128)(2,1)}, f32[4,1024,128]{2,1,0:T(8,128)}) custom-call(s32[2]{0:T(128)} %pad_add_fusion.side, bf16[64,8192]{1,0:T(8,128)(2,1)} %mid.1, bf16[64,128]{1,0:T(8,128)(2,1)} %last.1, s32[1,512]{1,0:T(1,128)} %mid_index.1, s32[1,512]{1,0:T(1,128)} %last_index.1, s32[1,512]{1,0:T(1,128)} %bag.7, ...), custom_call_target="tpu_custom_call" | custom-call | tf_op jit(solution)/shard_map/maps/pallas_call | solution.py:246
  19.8 0.0 collective-permute-start
  19.8 0.7 pad_add_fusion.1.side
  20.5 0.0 all-to-all-done.1.gathered
  20.5 0.0 copy-start
  20.5 0.9 %copy-done = bf16[4,336,256]{2,1,0:T(8,128)(2,1)} copy-done((bf16[4,336,256]{2,1,0:T(8,128)(2,1)}, bf16[4,336,256]{2,1,0:T(8,128)(2,1)S(1)}, u32[]{:S(2)}) %copy-start) | copy-done | bytes 688152
  21.4 2.7 %hot.1 = (f32[128,256]{1,0:T(8,128)}, bf16[128,256]{1,0:T(8,128)(2,1)}, f32[64,256]{1,0:T(8,128)}) custom-call(s32[2]{0:T(128)} %pad_add_fusion.1.side, bf16[4,336,256]{2,1,0:T(8,128)(2,1)} %copy-done, s32[1,256]{1,0:T(1,128)} %bitcast.9, s32[1,256]{1,0:T(1,128)} %row.3, s32[1,256]{1,0:T(1,128)} %bag.6), custom_call_target="tpu_custom_call" | custom-call | tf_op jit(solution)/shard_map/hot/pallas_call | solution.py:267
  24.0 0.5 collective-permute-start.1
  24.5 0.0 collective-permute-done.cold_got
  24.5 0.0 copy-start.3
  24.5 1.1 %collective-permute-done.1.hot_got = bf16[128,256]{1,0:T(8,128)(2,1)S(1)} collective-permute-done((bf16[128,256]{1,0:T(8,128)(2,1)}, bf16[128,256]{1,0:T(8,128)(2,1)S(1)}, u32[]{:S(2)}, u32[]{:S(2)}) %collective-permute-start.1) | collective-permute-done | bytes 65568 | tf_op jit(solution)/shard_map/ppermute | solution.py:277
  25.6 0.0 copy-start.5
  25.6 0.0 copy-done.3
  25.7 0.6 copy-done.5
  26.3 2.0 %pair.1 = bf16[4,256,256]{2,1,0:T(8,128)(2,1)} custom-call(f32[512,256]{1,0:T(8,128)} %get-tuple-element.21.cold_keep, bf16[512,256]{1,0:T(8,128)(2,1)} %copy-done.3, f32[128,256]{1,0:T(8,128)} %get-tuple-element.23.hot_keep, bf16[128,256]{1,0:T(8,128)(2,1)} %copy-done.5), custom_call_target="tpu_custom_call" | custom-call | tf_op jit(solution)/shard_map/pair/pallas_call | solution.py:279
  28.3 20.0 %all_to_all.20.got = bf16[4,256,256]{2,1,0:T(8,128)(2,1)} all-to-all(bf16[4,256,256]{2,1,0:T(8,128)(2,1)} %pair.1), channel_id=1, replica_groups={{0,2,4,6},{1,3,5,7},{8,10,12,14},{9,11,13,15},{16,18,20,22},{17,19,21,2..., dimensions={0} | all-to-all | bytes 1048576 | tf_op jit(solution)/shard_map/all_to_all | solution.py:283
  48.2 3.5 %all-to-all-start = ((bf16[8,256,128]{2,1,0:T(8,128)(2,1)}), bf16[8,256,128]{2,1,0:T(8,128)(2,1)S(1)}, u32[]{:S(2)}, u32[]{:S(2)}) async-start(bf16[8,256,128]{2,1,0:T(8,128)(2,1)} %get-tuple-element.17), calls=%async_computation | async-start | bytes 1048576 | tf_op jit(solution)/shard_map/all_to_all | solution.py:242
  51.7 1.8 %line.1 = (bf16[4,128,256]{2,1,0:T(8,128)(2,1)}, f32[128,256]{1,0:T(8,128)}) custom-call(bf16[4,256,256]{2,1,0:T(8,128)(2,1)} %all_to_all.20.got), custom_call_target="tpu_custom_call" | custom-call | tf_op jit(solution)/shard_map/line/pallas_call | solution.py:290
  53.6 13.4 %all-to-all-done.gathered = bf16[8,256,128]{2,1,0:T(8,128)(2,1)S(1)} async-done(((bf16[8,256,128]{2,1,0:T(8,128)(2,1)}), bf16[8,256,128]{2,1,0:T(8,128)(2,1)S(1)}, u32[]{:S(2)}, u32[]{:S(2)}) %all-to-all-start) | async-done | bytes 524320 | tf_op jit(solution)/shard_map/all_to_all | solution.py:242
  67.0 0.0 copy-start.1
  67.0 4.2 %all-to-all-start.3 = ((bf16[4,128,256]{2,1,0:T(8,128)(2,1)}), bf16[4,128,256]{2,1,0:T(8,128)(2,1)S(1)}, u32[]{:S(2)}, u32[]{:S(2)}) async-start(bf16[4,128,256]{2,1,0:T(8,128)(2,1)} %get-tuple-element.25), calls=%async_computation.3 | async-start | bytes 524288 | tf_op jit(solution)/shard_map/all_to_all | solution.py:293
  71.2 0.0 collective-permute-start.2
  71.2 0.0 copy-done.1
  71.2 4.6 %rows.1 = f32[64,256]{1,0:T(8,128)} custom-call(bf16[8,256,128]{2,1,0:T(8,128)(2,1)} %copy-done.1, f32[4,1024,128]{2,1,0:T(8,128)} %get-tuple-element.18.maps, s32[1,512]{1,0:T(1,128)} %bitcast.7, s32[1,512]{1,0:T(1,128)} %index.3, s32[1,512]{1,0:T(1,128)} %bag.7, f32[64,256]{1,0:T(8,128)} %get-tuple-element.20.hot_part), custom_call_target="tpu_custom_call" | custom-call | tf_op jit(solution)/shard_map/rows/pallas_call | solution.py:285
  75.8 0.0 collective-permute-done.2.other
  75.8 0.0 copy-start.4
  75.8 0.8 all-to-all-done.3.cold
  76.6 0.0 copy-start.2
  76.6 0.0 copy-done.4
  76.6 0.7 copy-done.2
  77.3 2.2 %final.1 = (f32[128,256]{1,0:T(8,128)}, f32[256,256]{1,0:T(8,128)}, f32[1,256]{1,0:T(1,128)}) custom-call(s32[2]{0:T(128)} %pad_add_fusion.1.side, bf16[4,128,256]{2,1,0:T(8,128)(2,1)} %copy-done.2, f32[128,256]{1,0:T(8,128)} %first.3, f32[128,256]{1,0:T(8,128)} %get-tuple-element.26.mine, f32[128,256]{1,0:T(8,128)} %copy-done.4, f32[256,256]{1,0:T(8,128)} %table.3, ...), custom_call_target="tpu_custom_call" | custom-call | tf_op jit(solution)/shard_map/final/pallas_call | solution.py:296
Async XLA Ops:
  2.8 17.7 %all-to-all-start.1 = ((bf16[4,336,256]{2,1,0:T(8,128)(2,1)}), bf16[4,336,256]{2,1,0:T(8,128)(2,1)S(1)}, u32[]{:S(2)}, u32[]{:S(2)}) async-start(bf16[4,336,256]{2,1,0:T(8,128)(2,1)} %get-tuple-element.19), calls=%async_computation.1 | async-start | bytes 1376256 | tf_op jit(solution)/shard_map/all_to_all | solution.py:241
  19.8 4.7 %collective-permute-start = (bf16[512,256]{1,0:T(8,128)(2,1)}, bf16[512,256]{1,0:T(8,128)(2,1)S(1)}, u32[]{:S(2)}, u32[]{:S(2)}) collective-permute-start(bf16[512,256]{1,0:T(8,128)(2,1)} %get-tuple-element.22), channel_id=1, source_target_pairs={{0,1},{1,0},{2,3},{3,2},{4,5},{5,4},{6,7},{7,6},{8,9},{9,8},{10,11... | collective-permute-start | bytes 786440 | tf_op jit(solution)/shard_map/ppermute | solution.py:264
  20.5 0.9 %copy-start = (bf16[4,336,256]{2,1,0:T(8,128)(2,1)}, bf16[4,336,256]{2,1,0:T(8,128)(2,1)S(1)}, u32[]{:S(2)}) copy-start(bf16[4,336,256]{2,1,0:T(8,128)(2,1)S(1)} %all-to-all-done.1.gathered) | copy-start | bytes 2064388
  24.0 1.6 %collective-permute-start.1 = (bf16[128,256]{1,0:T(8,128)(2,1)}, bf16[128,256]{1,0:T(8,128)(2,1)S(1)}, u32[]{:S(2)}, u32[]{:S(2)}) collective-permute-start(bf16[128,256]{1,0:T(8,128)(2,1)} %get-tuple-element.24), channel_id=1, source_target_pairs={{0,1},{1,0},{2,3},{3,2},{4,5},{5,4},{6,7},{7,6},{8,9},{9,8},{10,11... | collective-permute-start | bytes 196616 | tf_op jit(solution)/shard_map/ppermute | solution.py:277
  24.5 1.1 %copy-start.3 = (bf16[512,256]{1,0:T(8,128)(2,1)}, bf16[512,256]{1,0:T(8,128)(2,1)S(1)}, u32[]{:S(2)}) copy-start(bf16[512,256]{1,0:T(8,128)(2,1)S(1)} %collective-permute-done.cold_got) | copy-start | bytes 786436
  25.6 0.6 copy-start.5
  48.2 18.8 %all-to-all-start = ((bf16[8,256,128]{2,1,0:T(8,128)(2,1)}), bf16[8,256,128]{2,1,0:T(8,128)(2,1)S(1)}, u32[]{:S(2)}, u32[]{:S(2)}) async-start(bf16[8,256,128]{2,1,0:T(8,128)(2,1)} %get-tuple-element.17), calls=%async_computation | async-start | bytes 1048576 | tf_op jit(solution)/shard_map/all_to_all | solution.py:242
  67.0 4.2 %copy-start.1 = (bf16[8,256,128]{2,1,0:T(8,128)(2,1)}, bf16[8,256,128]{2,1,0:T(8,128)(2,1)S(1)}, u32[]{:S(2)}) copy-start(bf16[8,256,128]{2,1,0:T(8,128)(2,1)S(1)} %all-to-all-done.gathered) | copy-start | bytes 1572868
  67.0 9.6 %all-to-all-start.3 = ((bf16[4,128,256]{2,1,0:T(8,128)(2,1)}), bf16[4,128,256]{2,1,0:T(8,128)(2,1)S(1)}, u32[]{:S(2)}, u32[]{:S(2)}) async-start(bf16[4,128,256]{2,1,0:T(8,128)(2,1)} %get-tuple-element.25), calls=%async_computation.3 | async-start | bytes 524288 | tf_op jit(solution)/shard_map/all_to_all | solution.py:293
  71.2 4.6 %collective-permute-start.2 = (f32[128,256]{1,0:T(8,128)}, f32[128,256]{1,0:T(8,128)S(1)}, u32[]{:S(2)}, u32[]{:S(2)}) collective-permute-start(f32[128,256]{1,0:T(8,128)} %get-tuple-element.26.mine), channel_id=1, source_target_pairs={{0,1},{1,0},{2,3},{3,2},{4,5},{5,4},{6,7},{7,6},{8,9},{9,8},{10,11... | collective-permute-start | bytes 393224 | tf_op jit(solution)/shard_map/ppermute | solution.py:294
  75.8 0.8 copy-start.4
  76.6 0.7 copy-start.2

commit v2 on v1

v2 whole, which is shorter than its diff:
```python
import math

import jax
import jax.numpy as jnp
from jax import lax
from jax.experimental import pallas as pl
from jax.experimental.pallas import tpu as pltpu
from jax.sharding import PartitionSpec as P


E1 = 8
E2 = 8
E3 = 4
RANK = 32
TAIL = E2 * E3
LANES = 128
PAD = 16
FEW = 8
F32 = jnp.float32
BF16 = jnp.bfloat16
NT = (((1,), (1,)), ((), ()))


def iota(shape, dim):
    return lax.broadcasted_iota(jnp.int32, shape, dim)


def hot(mask):
    return mask.astype(F32).astype(BF16)


def mm(a, b):
    return jnp.dot(a, b, preferred_element_type=F32)


def mm_nt(a, b):
    return lax.dot_general(a, b, NT, preferred_element_type=F32)


def call(body, outs, args, scratch=(), far=0, spare=4 << 20):
    size = lambda shape, kind: math.prod(shape[:-2]) * max(shape[-2], 8) * max(shape[-1], LANES) * jnp.dtype(kind).itemsize
    scratch = tuple((x.shape, x.dtype) for x in args[:far]) + tuple(scratch)
    held = sum(size(a.shape, a.dtype) for a in args[far:]) + sum(size(*o) for o in tuple(outs) + scratch)
    near = len(args) - far

    def kernel(*refs):
        if not far:
            return body(*refs)
        given, rest, sem = refs[:far], refs[far:-1], refs[-1]
        taken = rest[near + len(outs) :]
        copies = [pltpu.make_async_copy(given[i], taken[i], sem.at[i]) for i in range(far)]
        for copy in copies:
            copy.start()
        for copy in copies:
            copy.wait()
        body(*taken[:far], *rest[: near + len(outs)], *taken[far:])

    args = [pltpu.with_memory_space_constraint(x, pltpu.HBM) for x in args[:far]] + list(args[far:])
    return pl.pallas_call(
        kernel,
        out_shape=tuple(jax.ShapeDtypeStruct(s, d) for s, d in outs),
        in_specs=[pl.BlockSpec(memory_space=pltpu.HBM)] * far + [pl.BlockSpec(memory_space=pltpu.VMEM)] * near,
        out_specs=(pl.BlockSpec(memory_space=pltpu.VMEM),) * len(outs),
        scratch_shapes=[pltpu.VMEM(s, d) for s, d in scratch]
        + ([pltpu.SemaphoreType.DMA((far,))] if far else []),
        compiler_params=pltpu.CompilerParams(vmem_limit_bytes=held + spare),
    )(*args)


def core_of():
    return lax.axis_index("tt") & 1


def tree(parts):
    while len(parts) > 1:
        parts = [parts[i] + parts[i + 1] for i in range(0, len(parts), 2)]
    return parts[0]


def swap(x, axis, bits):
    return lax.ppermute(x, axis, [(i, i ^ bits) for i in range(lax.axis_size(axis))])


def pack_kernel(table, grads, owner, row, bag, first, hot_out, first_out):
    rows, bags = table.shape[0], grads.shape[0]
    looks = jnp.concatenate(
        [owner[...], row[...], bag[...], jnp.zeros((PAD - 3, row.shape[1]), jnp.int32)], axis=0
    )
    turned = first[...].T.astype(BF16)
    for peer in range(hot_out.shape[0]):
        hot_out[peer, 0:rows, :] = table[...].astype(BF16)
        hot_out[peer, rows : rows + bags, :] = grads[...]
        hot_out[peer, rows + bags :, :] = looks.astype(F32).astype(BF16)
    for peer in range(first_out.shape[0]):
        first_out[peer] = turned


def maps_kernel(
    mid, last, mid_index, last_index, bag, owner, index, grads,
    keep, send, maps, keys, turned, left, right, lasts_of, cot, terms,
):
    mids, lasts = mid.shape[0], last.shape[0]
    looks = bag.shape[1]

    def turn(t, _):
        at = pl.ds(pl.multiple_of(t * LANES, LANES), LANES)
        block = mid[:, at].astype(F32)
        turned[at, :] = jnp.concatenate([block, block], axis=0).T
        return 0

    lax.fori_loop(0, mid.shape[1] // LANES, turn, 0, unroll=4)
    first_half = iota((RANK * E2, 2 * mids), 1) < mids
    for pair in range(RANK // 2):
        low = turned[pl.ds(2 * pair, RANK * E2, stride=RANK), :]
        high = turned[pl.ds(2 * pair + 1, RANK * E2, stride=RANK), :]
        left[:, pair * 2 * mids : (pair + 1) * 2 * mids] = jnp.where(first_half, low, high).astype(BF16)
    pick_last = hot(iota((lasts, looks), 0) == last_index[...])
    lasts_of[...] = mm(last[...].astype(F32).T.astype(BF16), pick_last)
    pick_bag = hot(iota((grads.shape[0], looks), 0) == bag[...])
    cot[...] = mm(grads[...].astype(F32).T.astype(BF16), pick_bag)
    pick_mid = hot(iota((mids, looks), 0) == mid_index[...])
    for e3 in range(E3):
        for b in range(RANK):
            at = b * E3 + e3
            spread = jnp.broadcast_to(lasts_of[at : at + 1, :], (PAD, looks)).astype(BF16)
            for part in range(0, mids, PAD):
                right[b * mids + part : b * mids + part + PAD, :] = pick_mid[part : part + PAD, :] * spread
        made = mm(left[...], right[...]).astype(BF16).astype(F32)
        for t in range(looks // LANES):
            maps[t, e3 * RANK * E2 : (e3 + 1) * RANK * E2, :] = made[:, t * LANES : (t + 1) * LANES]

    def back(t, _):
        lanes = pl.ds(pl.multiple_of(t * LANES, LANES), LANES)
        sums = [jnp.zeros((RANK, LANES), F32) for _ in range(E1)]
        for e2 in range(E2):
            for e3 in range(E3):
                part = maps[t, pl.ds(e3 * RANK * E2 + e2, RANK, stride=E2), :]
                for e1 in range(E1):
                    at = e1 * TAIL + e2 * E3 + e3
                    sums[e1] = sums[e1] + part * cot[at : at + 1, lanes]
        for e1 in range(E1):
            terms[e1 * RANK : (e1 + 1) * RANK, lanes] = sums[e1]
        return 0

    lax.fori_loop(0, looks // LANES, back, 0)
    whole = terms[...]
    high = whole.astype(BF16)
    low = (whole - high.astype(F32)).astype(BF16)
    own = owner[...]
    held = keep.shape[0]
    slices = held // (lax.axis_size("tt") // 2)
    key = ((own & 1) ^ core_of()) * held + (own >> 1) * slices + index[...]
    step = min(held, 256)
    keys[0:1, :] = own * slices + index[...]
    keys[1:2, :] = bag[...]
    for half, out in ((0, keep), (1, send)):
        for start in range(0, held, step):
            pick = hot(iota((step, looks), 0) + (half * held + start) == key)
            out[start : start + step, :] = (mm_nt(pick, high) + mm_nt(pick, low)).astype(out.dtype)


def hot_kernel(*refs):
    gathered, (keep, send, pooled) = refs[:-3], refs[-3:]
    me = lax.axis_index("hot")
    if len(gathered) > 1:
        sources = [(me ^ bits, part.at[0]) for bits, part in enumerate(gathered)]
        mine = gathered[0].at[0]
    else:
        sources = [(peer, gathered[0].at[peer]) for peer in range(gathered[0].shape[0])]
        mine = gathered[0].at[me]
    bags = pooled.shape[0]
    half = keep.shape[0]
    rows = 2 * half

    def lookups(part):
        sent = part[rows + bags :, :].astype(F32).astype(jnp.int32)
        return sent[0:1, :], sent[1:2, :], sent[2:3, :]

    owner, row, bag = lookups(mine)
    looks = row.shape[1]
    at = iota((rows, looks), 0)
    pick_bag = hot(iota((bags, looks), 0) == bag)
    total = jnp.zeros(pooled.shape, F32)
    for peer, part in sources:
        pick = hot((at == row) & (owner == peer))
        total = total + mm(mm_nt(pick_bag, pick).astype(BF16), part[0:rows, :])
    pooled[...] = total
    grad = jnp.zeros((rows, pooled.shape[1]), F32)
    for peer, part in sources:
        theirs, place, their_bag = lookups(part)
        upper = (place >= half).astype(jnp.int32)
        place = (upper ^ core_of()) * half + place - upper * half
        pick = hot((at == place) & (theirs == me))
        count = mm_nt(pick, hot(iota((bags, looks), 0) == their_bag))
        grad = grad + mm(count.astype(BF16), part[rows : rows + bags, :])
    keep[...] = grad[0:half]
    send[...] = grad[half:].astype(BF16)


def pair_kernel(cold_keep, cold_got, hot_keep, hot_got, own, *sends):
    slices = cold_keep.shape[0] // (1 + len(sends))
    place = lax.axis_index("tt") >> 1
    hot_sum = (hot_keep[...] + hot_got[...].astype(F32)).astype(BF16)
    for bits, out in enumerate((own,) + sends):
        at = pl.ds(pl.multiple_of((place ^ bits) * slices, slices), slices)
        out[0:slices, :] = (cold_keep[at, :] + cold_got[at, :].astype(F32)).astype(BF16)
        out[slices:, :] = hot_sum


def line_kernel(*refs):
    cold, hot_half = refs[-2:]
    slices = cold.shape[1]
    total = tree([part[...].astype(F32) for part in refs[:-2]])
    sent = total[0:slices].astype(BF16)
    for peer in range(cold.shape[0]):
        cold[peer] = sent
    hot_half[...] = total[slices:]


def rows_kernel(gathered, maps, keys, hot_part, pooled, slices_of, rows):
    peers, width, slices = gathered.shape
    looks = keys.shape[1]
    tiles = looks // LANES
    key = keys[0:1, :]
    total = jnp.zeros((width, looks), F32)
    for peer in range(peers):
        pick = hot(iota((slices, looks), 0) + peer * slices == key)
        total = total + mm(gathered[peer], pick)
    for t in range(tiles):
        slices_of[t] = total[:, t * LANES : (t + 1) * LANES]

    def forward(t, _):
        sums = [[jnp.zeros((E2, LANES), F32) for _ in range(E3)] for _ in range(E1)]
        for a in range(RANK):
            parts = [maps[t, e3 * RANK * E2 + a * E2 : e3 * RANK * E2 + a * E2 + E2, :] for e3 in range(E3)]
            for e1 in range(E1):
                entry = slices_of[t, e1 * RANK + a : e1 * RANK + a + 1, :]
                for e3 in range(E3):
                    sums[e1][e3] = sums[e1][e3] + parts[e3] * entry
        for e1 in range(E1):
            for e3 in range(E3):
                rows[t, pl.ds(e1 * TAIL + e3, E2, stride=E3), :] = sums[e1][e3]
        return 0

    lax.fori_loop(0, tiles, forward, 0)
    out = hot_part[...]
    for t in range(tiles):
        pick = hot(iota((pooled.shape[0], LANES), 0) == keys[1:2, t * LANES : (t + 1) * LANES])
        out = out + mm_nt(pick, rows[t].astype(BF16))
    pooled[...] = out


def final_kernel(first, mine, other, table, accum, *refs):
    parts, (new_first, new_table, new_accum) = refs[:-3], refs[-3:]
    total = tree([part[peer].astype(F32) for part in parts for peer in range(part.shape[0])])
    new_first[...] = first[...] - 0.01 * total
    lower = core_of() == 0
    grad = jnp.concatenate(
        [jnp.where(lower, mine[...], other[...]), jnp.where(lower, other[...], mine[...])], axis=0
    )
    rows = grad.shape[0]
    mean = jnp.mean(grad * grad, axis=1, keepdims=True)
    held = jnp.broadcast_to(accum[...], (LANES, rows)).T + mean
    new_accum[...] = held.T[0:1, :]
    new_table[...] = table[...] - 0.1 * grad / (jnp.sqrt(held[:, 0:1]) + 1e-08)


def local(
    hot_table, hot_accum, hot_owner, hot_row, hot_bag, cold_owner, first_index,
    mid_index, last_index, cold_bag, core_first, core_mid, core_last, bag_grads,
):
    rows, width = hot_table.shape
    bags = bag_grads.shape[0]
    slices = core_first.shape[0]
    hot_peers, tt_peers = lax.axis_size("hot"), lax.axis_size("tt")
    pairs = tt_peers // 2
    looks = cold_bag.shape[1]
    assert max(rows, bags, hot_peers) <= 256
    owner = hot_owner.reshape(1, -1)
    slice_owner = cold_owner.reshape(1, -1)
    held = slices * pairs
    few = hot_peers <= FEW
    tiles = looks // LANES

    hot_pack, first_pack = call(
        pack_kernel,
        (((1 if few else hot_peers, rows + bags + PAD, width), BF16), ((tt_peers, width, slices), BF16)),
        (hot_table, bag_grads, owner, hot_row, hot_bag, core_first),
        far=6,
    )

    def spread(x):
        if few:
            out = [x]
            for bits in range(1, hot_peers):
                out.append(swap(x, "hot", bits))
            return out
        return [lax.all_to_all(x, "hot", 0, 0, tiled=True)]

    hot_all = spread(hot_pack)
    first_all = lax.all_to_all(first_pack, "tt", 0, 0, tiled=True)

    keep, send, maps, keys = call(
        maps_kernel,
        (((held, width), F32), ((held, width), BF16), ((tiles, E3 * RANK * E2, LANES), F32), ((8, looks), jnp.int32)),
        (core_mid, core_last, mid_index, last_index, cold_bag, slice_owner, first_index, bag_grads),
        (
            ((core_mid.shape[1], LANES), F32),
            ((RANK * E2, RANK * core_mid.shape[0]), BF16),
            ((RANK * core_mid.shape[0], looks), BF16),
            ((RANK * E3, looks), F32),
            ((width, looks), F32),
            ((width, looks), F32),
        ),
        far=8,
    )
    got = swap(send, "tt", 1)

    hot_keep, hot_send, hot_part = call(
        hot_kernel, (((rows // 2, width), F32), ((rows // 2, width), BF16), ((bags, width), F32)), hot_all
    )
    hot_got = swap(hot_send, "tt", 1)

    pieces = call(
        pair_kernel, (((slices + rows // 2, width), BF16),) * pairs,
        (keep, got, hot_keep, hot_got),
    )
    parts = [pieces[0]]
    for bits in range(1, pairs):
        parts.append(swap(pieces[bits], "tt", 2 * bits))

    (pooled,) = call(
        rows_kernel, (((bags, width), F32),),
        (first_all, maps, keys, hot_part),
        (((tiles, width, LANES), F32), ((tiles, width, LANES), F32)),
    )

    cold_send, hot_half = call(
        line_kernel, (((1 if few else hot_peers, slices, width), BF16), ((rows // 2, width), F32)), parts
    )
    cold_all = spread(cold_send)
    hot_other = swap(hot_half, "tt", 1)

    new_first, new_table, new_accum = call(
        final_kernel,
        (((slices, width), F32), ((rows, width), F32), ((1, rows), F32)),
        (core_first, hot_half, hot_other, hot_table, hot_accum.reshape(1, -1), *cold_all),
    )
    return pooled, new_table, new_accum.reshape(-1), new_first


def solution(mesh):
    both = P(("hot", "tt"), None)
    placed = (
        P("hot", None), P("hot"), both, both, both, both, both, both, both, both,
        P("tt", None), P(), P(), both,
    )

    return jax.shard_map(
        local,
        mesh=mesh,
        in_specs=placed,
        out_specs=(both, P("hot", None), P("hot"), P("tt", None)),
        check_vma=False,
    )
```

time: 80.1 us -> 59.5 us (0.74)
  blocking collectives: 20 us -> 0 us
  Pallas kernels: 26.8 us -> 16.8 us
  waiting for transfers between devices: 15.3 us -> 23 us
  starting transfers between devices: 13.4 us -> 18.7 us
  local copies, waits for them, and re-layouts: 2.18 us -> 0.02 us
  other arithmetic: 1.25 us -> 0 us
    ppermute x3 -> x12, waiting for transfers between devices: 1.11 us -> 23 us  [swap(): lax.ppermute(x, axis, [(i, i ^ bits) for i in range(lax.axis_size(axis))])]
    all_to_all x1 -> x0, blocking collectives: 20 us -> none  [local(): lax.all_to_all(line_send, 'tt', 0, 0, axis_index_groups=lines, tiled=True)]
    all_to_all x1, waiting for transfers between devices: 13.4 us -> 0.01 us  [local(): first_all = lax.all_to_all(first_pack, 'tt', 0, 0, tiled=True)]
    ppermute x3 -> x12, starting transfers between devices: 0.51 us -> 12.2 us  [swap(): lax.ppermute(x, axis, [(i, i ^ bits) for i in range(lax.axis_size(axis))])]
    pallas_call x7, Pallas kernels: 26.8 us -> 16.8 us  [call(): pl.pallas_call(kernel, out_shape=tuple((jax.ShapeDtypeStruct(s, d) for s,...]
    all_to_all x2 -> x0, starting transfers between devices: 9.4 us -> none  [the longest x1 5.19 us: local(): hot_all = lax.all_to_all(hot_pack, 'hot', 0, 0, tiled=True)]
    all_to_all x1, starting transfers between devices: 3.49 us -> 6.5 us  [local(): first_all = lax.all_to_all(first_pack, 'tt', 0, 0, tiled=True)]
    unnamed x12 -> x6, local copies, waits for them, and re-layouts: 2.18 us -> 0.02 us
  transfers between devices with their start and end apart: 6 -> 13, of which waited for: 3 -> 9; matrix products, arithmetic and copies ran while one was open for 2% -> 0% of each run, Pallas kernels for 26% -> 20%
where the time goes in v2:
time: 59.5 us; the launch traced here: 59.2 us
  waiting for transfers between devices  23 us (39%)
  starting transfers between devices  18.7 us (31%)
  Pallas kernels  16.8 us (28%)
  between operations  0.73 us (1%)
    ppermute x12, waiting for transfers between devices, swap(): lax.ppermute(x, axis, [(i, i ^ bits) for i in range(lax.axis_size(axis))])  23 us
    pallas_call x7, Pallas kernels, call(): pl.pallas_call(kernel, out_shape=tuple((jax.ShapeDtypeStruct(s, d) for s,...  16.8 us
    ppermute x12, starting transfers between devices, swap(): lax.ppermute(x, axis, [(i, i ^ bits) for i in range(lax.axis_size(axis))])  12.2 us
    all_to_all x1, starting transfers between devices, local(): first_all = lax.all_to_all(first_pack, 'tt', 0, 0, tiled=True)  6.5 us
  transfers between devices with their start and end apart: 13, of which 9 were waited for; matrix products, arithmetic and copies ran while one was open for 0% of the time, Pallas kernels for 20%

profile of v2, /device:TPU:0, one launch (start us, length us, event | category | flops | bytes accessed | tf_op | source)
XLA Modules:
  0.0 59.2 jit_solution(18015263483412775195)
XLA Ops:
  0.6 2.1 %shard_map.165 = (bf16[1,336,256]{2,1,0:T(8,128)(2,1)S(1)}, bf16[8,256,128]{2,1,0:T(8,128)(2,1)}) custom-call(f32[256,256]{1,0:T(8,128)} %refs_3_.5, bf16[64,256]{1,0:T(8,128)(2,1)} %refs_7_.1, s32[1,256]{1,0:T(1,128)} %bitcast.6, s32[1,256]{1,0:T(1,128)} %refs_3_.3, s32[1,256]{1,0:T(1,128)} %refs_4_.2, f32[128,256]{1,0:T(8,128)} %refs_0_.5), custom_call_target="tpu_custom_call" | custom-call | tf_op jit(solution)/shard_map/pallas_call | solution.py:59
  2.7 0.0 copy-start
  2.7 0.0 copy-start.1
  2.7 0.0 copy-start.2
  2.7 6.5 %all-to-all-start = ((bf16[8,256,128]{2,1,0:T(8,128)(2,1)}), bf16[8,256,128]{2,1,0:T(8,128)(2,1)S(1)}, u32[]{:S(2)}, u32[]{:S(2)}) async-start(bf16[8,256,128]{2,1,0:T(8,128)(2,1)} %get-tuple-element.22), calls=%async_computation | async-start | bytes 1048576 | tf_op jit(solution)/shard_map/all_to_all | solution.py:301
  9.2 9.8 %shard_map.166 = (f32[512,256]{1,0:T(8,128)S(1)}, bf16[512,256]{1,0:T(8,128)(2,1)S(1)}, f32[4,1024,128]{2,1,0:T(8,128)S(1)}, s32[8,512]{1,0:T(8,128)S(1)}) custom-call(bf16[64,8192]{1,0:T(8,128)(2,1)} %refs_0_.4, bf16[64,128]{1,0:T(8,128)(2,1)} %refs_1_.3, s32[1,512]{1,0:T(1,128)} %refs_2_.1, s32[1,512]{1,0:T(1,128)} %refs_3_.4, s32[1,512]{1,0:T(1,128)} %refs_4_.3, ...), custom_call_target="tpu_custom_call" | custom-call | tf_op jit(solution)/shard_map/pallas_call | solution.py:59
  19.0 0.6 collective-permute-start.3
  19.6 2.5 %collective-permute-start.2 = (bf16[1,336,256]{2,1,0:T(8,128)(2,1)S(1)}, bf16[1,336,256]{2,1,0:T(8,128)(2,1)S(1)}, u32[]{:S(2)}, u32[]{:S(2)}) collective-permute-start(bf16[1,336,256]{2,1,0:T(8,128)(2,1)S(1)} %get-tuple-element.25.refs_0_), channel_id=1, source_target_pairs={{0,24},{8,16},{16,8},{24,0},{1,25},{9,17},{17,9},{25,1},{2,26},{10... | collective-permute-start | bytes 516104 | tf_op jit(solution)/shard_map/ppermute | solution.py:81
  22.1 0.5 collective-permute-start.1
  22.6 0.5 collective-permute-start
  23.1 4.7 %collective-permute-done.2.refs_3_ = bf16[1,336,256]{2,1,0:T(8,128)(2,1)S(1)} collective-permute-done((bf16[1,336,256]{2,1,0:T(8,128)(2,1)S(1)}, bf16[1,336,256]{2,1,0:T(8,128)(2,1)S(1)}, u32[]{:S(2)}, u32[]{:S(2)}) %collective-permute-start.2) | collective-permute-done | bytes 172064 | tf_op jit(solution)/shard_map/ppermute | solution.py:81
  27.8 2.8 %collective-permute-done.1.refs_2_ = bf16[1,336,256]{2,1,0:T(8,128)(2,1)S(1)} collective-permute-done((bf16[1,336,256]{2,1,0:T(8,128)(2,1)S(1)}, bf16[1,336,256]{2,1,0:T(8,128)(2,1)S(1)}, u32[]{:S(2)}, u32[]{:S(2)}) %collective-permute-start.1) | collective-permute-done | bytes 172064 | tf_op jit(solution)/shard_map/ppermute | solution.py:81
  30.6 0.1 collective-permute-done.refs_1_
  30.7 0.9 %shard_map.167 = (f32[128,256]{1,0:T(8,128)S(1)}, bf16[128,256]{1,0:T(8,128)(2,1)S(1)}, f32[64,256]{1,0:T(8,128)S(1)}) custom-call(bf16[1,336,256]{2,1,0:T(8,128)(2,1)S(1)} %get-tuple-element.25.refs_0_, bf16[1,336,256]{2,1,0:T(8,128)(2,1)S(1)} %collective-permute-done.refs_1_, bf16[1,336,256]{2,1,0:T(8,128)(2,1)S(1)} %collective-permute-done.1.refs_2_, ...), custom_call_target="tpu_custom_call" | custom-call | tf_op jit(solution)/shard_map/pallas_call | solution.py:59
  31.5 0.1 collective-permute-start.4
  31.6 1.2 %collective-permute-done.4.refs_3_ = bf16[128,256]{1,0:T(8,128)(2,1)S(1)} collective-permute-done((bf16[128,256]{1,0:T(8,128)(2,1)S(1)}, bf16[128,256]{1,0:T(8,128)(2,1)S(1)}, u32[]{:S(2)}, u32[]{:S(2)}) %collective-permute-start.4) | collective-permute-done | bytes 65568 | tf_op jit(solution)/shard_map/ppermute | solution.py:81
  32.9 0.0 collective-permute-done.3.refs_1_
  32.9 0.1 shard_map.169
  32.9 2.0 %collective-permute-start.5 = (bf16[256,256]{1,0:T(8,128)(2,1)S(1)}, bf16[256,256]{1,0:T(8,128)(2,1)S(1)}, u32[]{:S(2)}, u32[]{:S(2)}) collective-permute-start(bf16[256,256]{1,0:T(8,128)(2,1)S(1)} %get-tuple-element.32), channel_id=1, source_target_pairs={{0,2},{1,3},{2,0},{3,1},{4,6},{5,7},{6,4},{7,5},{8,10},{9,11},{10,... | collective-permute-start | bytes 393224 | tf_op jit(solution)/shard_map/ppermute | solution.py:81
  34.9 2.4 %collective-permute-start.6 = (bf16[256,256]{1,0:T(8,128)(2,1)S(1)}, bf16[256,256]{1,0:T(8,128)(2,1)S(1)}, u32[]{:S(2)}, u32[]{:S(2)}) collective-permute-start(bf16[256,256]{1,0:T(8,128)(2,1)S(1)} %get-tuple-element.33), channel_id=1, source_target_pairs={{0,4},{1,5},{2,6},{3,7},{4,0},{5,1},{6,2},{7,3},{8,12},{9,13},{10,... | collective-permute-start | bytes 393224 | tf_op jit(solution)/shard_map/ppermute | solution.py:81
  37.3 0.1 collective-permute-start.7
  37.4 3.2 %collective-permute-done.5.refs_1_ = bf16[256,256]{1,0:T(8,128)(2,1)S(1)} collective-permute-done((bf16[256,256]{1,0:T(8,128)(2,1)S(1)}, bf16[256,256]{1,0:T(8,128)(2,1)S(1)}, u32[]{:S(2)}, u32[]{:S(2)}) %collective-permute-start.5) | collective-permute-done | bytes 131104 | tf_op jit(solution)/shard_map/ppermute | solution.py:81
  40.6 7.2 %collective-permute-done.6.refs_2_ = bf16[256,256]{1,0:T(8,128)(2,1)S(1)} collective-permute-done((bf16[256,256]{1,0:T(8,128)(2,1)S(1)}, bf16[256,256]{1,0:T(8,128)(2,1)S(1)}, u32[]{:S(2)}, u32[]{:S(2)}) %collective-permute-start.6) | collective-permute-done | bytes 131104 | tf_op jit(solution)/shard_map/ppermute | solution.py:81
  47.8 0.0 collective-permute-done.7.refs_3_
  47.8 0.1 shard_map.170
  47.9 0.1 collective-permute-start.8
  48.0 1.7 %collective-permute-start.11 = (bf16[1,128,256]{2,1,0:T(8,128)(2,1)S(1)}, bf16[1,128,256]{2,1,0:T(8,128)(2,1)S(1)}, u32[]{:S(2)}, u32[]{:S(2)}) collective-permute-start(bf16[1,128,256]{2,1,0:T(8,128)(2,1)S(1)} %get-tuple-element.36.refs_5_), channel_id=1, source_target_pairs={{0,24},{8,16},{16,8},{24,0},{1,25},{9,17},{17,9},{25,1},{2,26},{10... | collective-permute-start | bytes 196616 | tf_op jit(solution)/shard_map/ppermute | solution.py:81
  49.7 1.3 %collective-permute-start.10 = (bf16[1,128,256]{2,1,0:T(8,128)(2,1)S(1)}, bf16[1,128,256]{2,1,0:T(8,128)(2,1)S(1)}, u32[]{:S(2)}, u32[]{:S(2)}) collective-permute-start(bf16[1,128,256]{2,1,0:T(8,128)(2,1)S(1)} %get-tuple-element.36.refs_5_), channel_id=1, source_target_pairs={{0,16},{8,24},{16,0},{24,8},{1,17},{9,25},{17,1},{25,9},{2,18},{10... | collective-permute-start | bytes 196616 | tf_op jit(solution)/shard_map/ppermute | solution.py:81
  51.0 0.5 collective-permute-start.9
  51.5 1.9 %collective-permute-done.11.refs_8_ = bf16[1,128,256]{2,1,0:T(8,128)(2,1)S(1)} collective-permute-done((bf16[1,128,256]{2,1,0:T(8,128)(2,1)S(1)}, bf16[1,128,256]{2,1,0:T(8,128)(2,1)S(1)}, u32[]{:S(2)}, u32[]{:S(2)}) %collective-permute-start.11) | collective-permute-done | bytes 65568 | tf_op jit(solution)/shard_map/ppermute | solution.py:81
  53.5 1.3 %collective-permute-done.10.refs_7_ = bf16[1,128,256]{2,1,0:T(8,128)(2,1)S(1)} collective-permute-done((bf16[1,128,256]{2,1,0:T(8,128)(2,1)S(1)}, bf16[1,128,256]{2,1,0:T(8,128)(2,1)S(1)}, u32[]{:S(2)}, u32[]{:S(2)}) %collective-permute-start.10) | collective-permute-done | bytes 65568 | tf_op jit(solution)/shard_map/ppermute | solution.py:81
  54.8 0.5 collective-permute-done.9.refs_6_
  55.3 0.0 collective-permute-done.8.refs_2_
  55.3 0.0 copy-done
  55.3 0.0 copy-done.1
  55.3 0.0 copy-done.2
  55.3 1.0 %shard_map.171 = (f32[128,256]{1,0:T(8,128)}, f32[256,256]{1,0:T(8,128)}, f32[1,256]{1,0:T(1,128)}) custom-call(f32[128,256]{1,0:T(8,128)S(1)} %copy-done.1, f32[128,256]{1,0:T(8,128)S(1)} %get-tuple-element.35.refs_1_, f32[128,256]{1,0:T(8,128)S(1)} %collective-permute-done.8.refs_2_, f32[256,256]{1,0:T(8,128)S(1)} %copy-done, f32[1,256]{1,0:T(1,128)S(1)} %bitcast.4, ...), custom_call_target="tpu_custom_call" | custom-call | tf_op jit(solution)/shard_map/pallas_call | solution.py:59
  56.3 0.0 all-to-all-done.refs_0_
  56.3 2.9 %shard_map.168 = f32[64,256]{1,0:T(8,128)} custom-call(bf16[8,256,128]{2,1,0:T(8,128)(2,1)S(1)} %all-to-all-done.refs_0_, f32[4,1024,128]{2,1,0:T(8,128)S(1)} %get-tuple-element.23.refs_1_, s32[8,512]{1,0:T(8,128)S(1)} %get-tuple-element.24.refs_2_, f32[64,256]{1,0:T(8,128)S(1)} %get-tuple-element.26.refs_3_), custom_call_target="tpu_custom_call" | custom-call | tf_op jit(solution)/shard_map/pallas_call | solution.py:59
Async XLA Ops:
  2.7 52.6 %copy-start = (f32[256,256]{1,0:T(8,128)S(1)}, f32[256,256]{1,0:T(8,128)}, u32[]{:S(2)}) copy-start(f32[256,256]{1,0:T(8,128)} %refs_3_.5) | copy-start | bytes 786436
  2.7 52.6 %copy-start.1 = (f32[128,256]{1,0:T(8,128)S(1)}, f32[128,256]{1,0:T(8,128)}, u32[]{:S(2)}) copy-start(f32[128,256]{1,0:T(8,128)} %refs_0_.5) | copy-start | bytes 393220
  2.7 52.6 %copy-start.2 = (f32[256]{0:T(256)S(1)}, f32[256]{0:T(256)}, u32[]{:S(2)}) copy-start(f32[256]{0:T(256)} %param.15) | copy-start | bytes 3076
  2.7 53.6 %all-to-all-start = ((bf16[8,256,128]{2,1,0:T(8,128)(2,1)}), bf16[8,256,128]{2,1,0:T(8,128)(2,1)S(1)}, u32[]{:S(2)}, u32[]{:S(2)}) async-start(bf16[8,256,128]{2,1,0:T(8,128)(2,1)} %get-tuple-element.22), calls=%async_computation | async-start | bytes 1048576 | tf_op jit(solution)/shard_map/all_to_all | solution.py:301
  19.0 13.8 %collective-permute-start.3 = (bf16[512,256]{1,0:T(8,128)(2,1)S(1)}, bf16[512,256]{1,0:T(8,128)(2,1)S(1)}, u32[]{:S(2)}, u32[]{:S(2)}) collective-permute-start(bf16[512,256]{1,0:T(8,128)(2,1)S(1)} %get-tuple-element.28), channel_id=1, source_target_pairs={{0,1},{1,0},{2,3},{3,2},{4,5},{5,4},{6,7},{7,6},{8,9},{9,8},{10,11... | collective-permute-start | bytes 786440 | tf_op jit(solution)/shard_map/ppermute | solution.py:81
  19.6 8.2 %collective-permute-start.2 = (bf16[1,336,256]{2,1,0:T(8,128)(2,1)S(1)}, bf16[1,336,256]{2,1,0:T(8,128)(2,1)S(1)}, u32[]{:S(2)}, u32[]{:S(2)}) collective-permute-start(bf16[1,336,256]{2,1,0:T(8,128)(2,1)S(1)} %get-tuple-element.25.refs_0_), channel_id=1, source_target_pairs={{0,24},{8,16},{16,8},{24,0},{1,25},{9,17},{17,9},{25,1},{2,26},{10... | collective-permute-start | bytes 516104 | tf_op jit(solution)/shard_map/ppermute | solution.py:81
  22.1 8.5 %collective-permute-start.1 = (bf16[1,336,256]{2,1,0:T(8,128)(2,1)S(1)}, bf16[1,336,256]{2,1,0:T(8,128)(2,1)S(1)}, u32[]{:S(2)}, u32[]{:S(2)}) collective-permute-start(bf16[1,336,256]{2,1,0:T(8,128)(2,1)S(1)} %get-tuple-element.25.refs_0_), channel_id=1, source_target_pairs={{0,16},{8,24},{16,0},{24,8},{1,17},{9,25},{17,1},{25,9},{2,18},{10... | collective-permute-start | bytes 516104 | tf_op jit(solution)/shard_map/ppermute | solution.py:81
  22.6 8.1 %collective-permute-start = (bf16[1,336,256]{2,1,0:T(8,128)(2,1)S(1)}, bf16[1,336,256]{2,1,0:T(8,128)(2,1)S(1)}, u32[]{:S(2)}, u32[]{:S(2)}) collective-permute-start(bf16[1,336,256]{2,1,0:T(8,128)(2,1)S(1)} %get-tuple-element.25.refs_0_), channel_id=1, source_target_pairs={{0,8},{8,0},{16,24},{24,16},{1,9},{9,1},{17,25},{25,17},{2,10},{10... | collective-permute-start | bytes 516104 | tf_op jit(solution)/shard_map/ppermute | solution.py:81
  31.5 1.3 %collective-permute-start.4 = (bf16[128,256]{1,0:T(8,128)(2,1)S(1)}, bf16[128,256]{1,0:T(8,128)(2,1)S(1)}, u32[]{:S(2)}, u32[]{:S(2)}) collective-permute-start(bf16[128,256]{1,0:T(8,128)(2,1)S(1)} %get-tuple-element.30), channel_id=1, source_target_pairs={{0,1},{1,0},{2,3},{3,2},{4,5},{5,4},{6,7},{7,6},{8,9},{9,8},{10,11... | collective-permute-start | bytes 196616 | tf_op jit(solution)/shard_map/ppermute | solution.py:81
  32.9 7.7 %collective-permute-start.5 = (bf16[256,256]{1,0:T(8,128)(2,1)S(1)}, bf16[256,256]{1,0:T(8,128)(2,1)S(1)}, u32[]{:S(2)}, u32[]{:S(2)}) collective-permute-start(bf16[256,256]{1,0:T(8,128)(2,1)S(1)} %get-tuple-element.32), channel_id=1, source_target_pairs={{0,2},{1,3},{2,0},{3,1},{4,6},{5,7},{6,4},{7,5},{8,10},{9,11},{10,... | collective-permute-start | bytes 393224 | tf_op jit(solution)/shard_map/ppermute | solution.py:81
  34.9 12.9 %collective-permute-start.6 = (bf16[256,256]{1,0:T(8,128)(2,1)S(1)}, bf16[256,256]{1,0:T(8,128)(2,1)S(1)}, u32[]{:S(2)}, u32[]{:S(2)}) collective-permute-start(bf16[256,256]{1,0:T(8,128)(2,1)S(1)} %get-tuple-element.33), channel_id=1, source_target_pairs={{0,4},{1,5},{2,6},{3,7},{4,0},{5,1},{6,2},{7,3},{8,12},{9,13},{10,... | collective-permute-start | bytes 393224 | tf_op jit(solution)/shard_map/ppermute | solution.py:81
  37.3 10.5 %collective-permute-start.7 = (bf16[256,256]{1,0:T(8,128)(2,1)S(1)}, bf16[256,256]{1,0:T(8,128)(2,1)S(1)}, u32[]{:S(2)}, u32[]{:S(2)}) collective-permute-start(bf16[256,256]{1,0:T(8,128)(2,1)S(1)} %get-tuple-element.34), channel_id=1, source_target_pairs={{0,6},{1,7},{2,4},{3,5},{4,2},{5,3},{6,0},{7,1},{8,14},{9,15},{10,... | collective-permute-start | bytes 393224 | tf_op jit(solution)/shard_map/ppermute | solution.py:81
  47.9 7.4 %collective-permute-start.8 = (f32[128,256]{1,0:T(8,128)S(1)}, f32[128,256]{1,0:T(8,128)S(1)}, u32[]{:S(2)}, u32[]{:S(2)}) collective-permute-start(f32[128,256]{1,0:T(8,128)S(1)} %get-tuple-element.35.refs_1_), channel_id=1, source_target_pairs={{0,1},{1,0},{2,3},{3,2},{4,5},{5,4},{6,7},{7,6},{8,9},{9,8},{10,11... | collective-permute-start | bytes 393224 | tf_op jit(solution)/shard_map/ppermute | solution.py:81
  48.0 5.5 %collective-permute-start.11 = (bf16[1,128,256]{2,1,0:T(8,128)(2,1)S(1)}, bf16[1,128,256]{2,1,0:T(8,128)(2,1)S(1)}, u32[]{:S(2)}, u32[]{:S(2)}) collective-permute-start(bf16[1,128,256]{2,1,0:T(8,128)(2,1)S(1)} %get-tuple-element.36.refs_5_), channel_id=1, source_target_pairs={{0,24},{8,16},{16,8},{24,0},{1,25},{9,17},{17,9},{25,1},{2,26},{10... | collective-permute-start | bytes 196616 | tf_op jit(solution)/shard_map/ppermute | solution.py:81
  49.7 5.1 %collective-permute-start.10 = (bf16[1,128,256]{2,1,0:T(8,128)(2,1)S(1)}, bf16[1,128,256]{2,1,0:T(8,128)(2,1)S(1)}, u32[]{:S(2)}, u32[]{:S(2)}) collective-permute-start(bf16[1,128,256]{2,1,0:T(8,128)(2,1)S(1)} %get-tuple-element.36.refs_5_), channel_id=1, source_target_pairs={{0,16},{8,24},{16,0},{24,8},{1,17},{9,25},{17,1},{25,9},{2,18},{10... | collective-permute-start | bytes 196616 | tf_op jit(solution)/shard_map/ppermute | solution.py:81
  51.0 4.3 %collective-permute-start.9 = (bf16[1,128,256]{2,1,0:T(8,128)(2,1)S(1)}, bf16[1,128,256]{2,1,0:T(8,128)(2,1)S(1)}, u32[]{:S(2)}, u32[]{:S(2)}) collective-permute-start(bf16[1,128,256]{2,1,0:T(8,128)(2,1)S(1)} %get-tuple-element.36.refs_5_), channel_id=1, source_target_pairs={{0,8},{8,0},{16,24},{24,16},{1,9},{9,1},{17,25},{25,17},{2,10},{10... | collective-permute-start | bytes 196616 | tf_op jit(solution)/shard_map/ppermute | solution.py:81

commit v3 on v2

--- a/solution.py
+++ b/solution.py
@@ -91,8 +91,7 @@
         hot_out[peer, 0:rows, :] = table[...].astype(BF16)
         hot_out[peer, rows : rows + bags, :] = grads[...]
         hot_out[peer, rows + bags :, :] = looks.astype(F32).astype(BF16)
-    for peer in range(first_out.shape[0]):
-        first_out[peer] = turned
+    first_out[...] = turned
 
 
 def maps_kernel(
@@ -198,34 +197,40 @@
 
 
 def pair_kernel(cold_keep, cold_got, hot_keep, hot_got, own, *sends):
-    slices = cold_keep.shape[0] // (1 + len(sends))
+    slices = own.shape[0]
     place = lax.axis_index("tt") >> 1
-    hot_sum = (hot_keep[...] + hot_got[...].astype(F32)).astype(BF16)
     for bits, out in enumerate((own,) + sends):
         at = pl.ds(pl.multiple_of((place ^ bits) * slices, slices), slices)
         out[0:slices, :] = (cold_keep[at, :] + cold_got[at, :].astype(F32)).astype(BF16)
-        out[slices:, :] = hot_sum
+    sends[0][slices:, :] = (hot_keep[...] + hot_got[...].astype(F32)).astype(BF16)
+
+
+def step_kernel(mine, got, total):
+    rows = total.shape[0]
+    total[...] = (
+        mine[mine.shape[0] - rows :, :].astype(F32) + got[got.shape[0] - rows :, :].astype(F32)
+    ).astype(total.dtype)
 
 
 def line_kernel(*refs):
-    cold, hot_half = refs[-2:]
+    parts, cold = refs[:-1], refs[-1]
     slices = cold.shape[1]
-    total = tree([part[...].astype(F32) for part in refs[:-2]])
-    sent = total[0:slices].astype(BF16)
+    sent = tree([part[0:slices, :].astype(F32) for part in parts]).astype(BF16)
     for peer in range(cold.shape[0]):
         cold[peer] = sent
-    hot_half[...] = total[slices:]
-
-
-def rows_kernel(gathered, maps, keys, hot_part, pooled, slices_of, rows):
-    peers, width, slices = gathered.shape
+
+
+def rows_kernel(maps, keys, hot_part, *refs):
+    gathered, (pooled, slices_of, rows) = refs[:-3], refs[-3:]
+    width, slices = gathered[0].shape
+    me = lax.axis_index("tt")
     looks = keys.shape[1]
     tiles = looks // LANES
     key = keys[0:1, :]
     total = jnp.zeros((width, looks), F32)
-    for peer in range(peers):
-        pick = hot(iota((slices, looks), 0) + peer * slices == key)
-        total = total + mm(gathered[peer], pick)
+    for bits, part in enumerate(gathered):
+        pick = hot(iota((slices, looks), 0) + (me ^ bits) * slices == key)
+        total = total + mm(part[...], pick)
     for t in range(tiles):
         slices_of[t] = total[:, t * LANES : (t + 1) * LANES]
 
@@ -284,7 +289,7 @@
 
     hot_pack, first_pack = call(
         pack_kernel,
-        (((1 if few else hot_peers, rows + bags + PAD, width), BF16), ((tt_peers, width, slices), BF16)),
+        (((1 if few else hot_peers, rows + bags + PAD, width), BF16), ((width, slices), BF16)),
         (hot_table, bag_grads, owner, hot_row, hot_bag, core_first),
         far=6,
     )
@@ -298,8 +303,6 @@
         return [lax.all_to_all(x, "hot", 0, 0, tiled=True)]
 
     hot_all = spread(hot_pack)
-    first_all = lax.all_to_all(first_pack, "tt", 0, 0, tiled=True)
-
     keep, send, maps, keys = call(
         maps_kernel,
         (((held, width), F32), ((held, width), BF16), ((tiles, E3 * RANK * E2, LANES), F32), ((8, looks), jnp.int32)),
@@ -321,25 +324,39 @@
     )
     hot_got = swap(hot_send, "tt", 1)
 
+    half = rows // 2
     pieces = call(
-        pair_kernel, (((slices + rows // 2, width), BF16),) * pairs,
+        pair_kernel,
+        tuple(((slices + (half if bits == 1 else 0), width), BF16) for bits in range(pairs)),
         (keep, got, hot_keep, hot_got),
     )
     parts = [pieces[0]]
     for bits in range(1, pairs):
         parts.append(swap(pieces[bits], "tt", 2 * bits))
 
+    shards = [first_pack]
+    for bits in range(1, pairs):
+        shards.append(swap(first_pack, "tt", 2 * bits))
+    first_all = []
+    for bits, shard in enumerate(shards):
+        first_all += [shard, swap(shard, "tt", 1)]
+
+    mine, theirs, bits = pieces[1], parts[1], 2
+    while bits < pairs:
+        (mine,) = call(step_kernel, (((half, width), BF16),), (mine, theirs))
+        theirs = swap(mine, "tt", 2 * bits)
+        bits *= 2
+    (hot_half,) = call(step_kernel, (((half, width), F32),), (mine, theirs))
+    hot_other = swap(hot_half, "tt", 1)
+
+    (cold_send,) = call(line_kernel, (((1 if few else hot_peers, slices, width), BF16),), parts)
+    cold_all = spread(cold_send)
+
     (pooled,) = call(
         rows_kernel, (((bags, width), F32),),
-        (first_all, maps, keys, hot_part),
+        (maps, keys, hot_part, *first_all),
         (((tiles, width, LANES), F32), ((tiles, width, LANES), F32)),
     )
-
-    cold_send, hot_half = call(
-        line_kernel, (((1 if few else hot_peers, slices, width), BF16), ((rows // 2, width), F32)), parts
-    )
-    cold_all = spread(cold_send)
-    hot_other = swap(hot_half, "tt", 1)
 
     new_first, new_table, new_accum = call(
         final_kernel,

time: 59.5 us -> 59 us (level)
  starting transfers between devices: 18.7 us -> 25.7 us
  waiting for transfers between devices: 23 us -> 16.3 us
  Pallas kernels: 16.8 us -> 16 us
    ppermute x12 -> x20, starting transfers between devices: 12.2 us -> 25.7 us  [swap(): lax.ppermute(x, axis, [(i, i ^ bits) for i in range(lax.axis_size(axis))])]
    ppermute x12 -> x20, waiting for transfers between devices: 23 us -> 16.3 us  [swap(): lax.ppermute(x, axis, [(i, i ^ bits) for i in range(lax.axis_size(axis))])]
    all_to_all x1 -> x0, starting transfers between devices: 6.5 us -> none  [local(): first_all = lax.all_to_all(first_pack, 'tt', 0, 0, tiled=True)]
    pallas_call x7 -> x9, Pallas kernels: 16.8 us -> 16 us  [call(): pl.pallas_call(kernel, out_shape=tuple((jax.ShapeDtypeStruct(s, d) for s,...]
  transfers between devices with their start and end apart: 13 -> 20, of which waited for: 9 -> 7; matrix products, arithmetic and copies ran while one was open for 0% -> 0% of each run, Pallas kernels for 20% -> 9%
where the time goes in v3:
time: 59 us; the launch traced here: 58.8 us
  starting transfers between devices  25.7 us (44%)
  waiting for transfers between devices  16.3 us (28%)
  Pallas kernels  16 us (27%)
  between operations  0.76 us (1%)
    ppermute x20, starting transfers between devices, swap(): lax.ppermute(x, axis, [(i, i ^ bits) for i in range(lax.axis_size(axis))])  25.7 us
    ppermute x20, waiting for transfers between devices, swap(): lax.ppermute(x, axis, [(i, i ^ bits) for i in range(lax.axis_size(axis))])  16.3 us
    pallas_call x9, Pallas kernels, call(): pl.pallas_call(kernel, out_shape=tuple((jax.ShapeDtypeStruct(s, d) for s,...  16 us
  transfers between devices with their start and end apart: 20, of which 7 were waited for; matrix products, arithmetic and copies ran while one was open for 0% of the time, Pallas kernels for 9%

profile of v3, /device:TPU:0, one launch (start us, length us, event | category | flops | bytes accessed | tf_op | source)
XLA Modules:
  0.0 58.8 jit_solution(15553732915036364006)
XLA Ops:
  0.6 9.8 %shard_map.165 = (f32[512,256]{1,0:T(8,128)S(1)}, bf16[512,256]{1,0:T(8,128)(2,1)S(1)}, f32[4,1024,128]{2,1,0:T(8,128)S(1)}, s32[8,512]{1,0:T(8,128)S(1)}) custom-call(bf16[64,8192]{1,0:T(8,128)(2,1)} %refs_0_.3, bf16[64,128]{1,0:T(8,128)(2,1)} %refs_1_.2, s32[1,512]{1,0:T(1,128)} %refs_2_.1, s32[1,512]{1,0:T(1,128)} %refs_3_.3, s32[1,512]{1,0:T(1,128)} %refs_4_.2, ...), custom_call_target="tpu_custom_call" | custom-call | tf_op jit(solution)/shard_map/pallas_call | solution.py:59
  10.5 0.6 collective-permute-start.10
  11.0 1.2 %shard_map.166 = (bf16[1,336,256]{2,1,0:T(8,128)(2,1)S(1)}, bf16[256,128]{1,0:T(8,128)(2,1)S(1)}) custom-call(f32[256,256]{1,0:T(8,128)} %refs_3_.5, bf16[64,256]{1,0:T(8,128)(2,1)} %refs_1_.3, s32[1,256]{1,0:T(1,128)} %bitcast.6, s32[1,256]{1,0:T(1,128)} %refs_3_.4, s32[1,256]{1,0:T(1,128)} %refs_4_.3, f32[128,256]{1,0:T(8,128)} %refs_0_.5), custom_call_target="tpu_custom_call" | custom-call | tf_op jit(solution)/shard_map/pallas_call | solution.py:59
  12.2 2.6 %collective-permute-start = (bf16[1,336,256]{2,1,0:T(8,128)(2,1)S(1)}, bf16[1,336,256]{2,1,0:T(8,128)(2,1)S(1)}, u32[]{:S(2)}, u32[]{:S(2)}) collective-permute-start(bf16[1,336,256]{2,1,0:T(8,128)(2,1)S(1)} %get-tuple-element.22.refs_0_), channel_id=1, source_target_pairs={{0,8},{8,0},{16,24},{24,16},{1,9},{9,1},{17,25},{25,17},{2,10},{10... | collective-permute-start | bytes 516104 | tf_op jit(solution)/shard_map/ppermute | solution.py:81
  14.8 1.5 %collective-permute-start.1 = (bf16[1,336,256]{2,1,0:T(8,128)(2,1)S(1)}, bf16[1,336,256]{2,1,0:T(8,128)(2,1)S(1)}, u32[]{:S(2)}, u32[]{:S(2)}) collective-permute-start(bf16[1,336,256]{2,1,0:T(8,128)(2,1)S(1)} %get-tuple-element.22.refs_0_), channel_id=1, source_target_pairs={{0,16},{8,24},{16,0},{24,8},{1,17},{9,25},{17,1},{25,9},{2,18},{10... | collective-permute-start | bytes 516104 | tf_op jit(solution)/shard_map/ppermute | solution.py:81
  16.3 0.0 collective-permute-start.2
  16.3 3.7 %collective-permute-done.refs_1_ = bf16[1,336,256]{2,1,0:T(8,128)(2,1)S(1)} collective-permute-done((bf16[1,336,256]{2,1,0:T(8,128)(2,1)S(1)}, bf16[1,336,256]{2,1,0:T(8,128)(2,1)S(1)}, u32[]{:S(2)}, u32[]{:S(2)}) %collective-permute-start) | collective-permute-done | bytes 172064 | tf_op jit(solution)/shard_map/ppermute | solution.py:81
  20.0 4.9 %collective-permute-done.1.refs_2_ = bf16[1,336,256]{2,1,0:T(8,128)(2,1)S(1)} collective-permute-done((bf16[1,336,256]{2,1,0:T(8,128)(2,1)S(1)}, bf16[1,336,256]{2,1,0:T(8,128)(2,1)S(1)}, u32[]{:S(2)}, u32[]{:S(2)}) %collective-permute-start.1) | collective-permute-done | bytes 172064 | tf_op jit(solution)/shard_map/ppermute | solution.py:81
  25.0 0.0 collective-permute-done.2.refs_3_
  25.0 0.9 %shard_map.167 = (f32[128,256]{1,0:T(8,128)S(1)}, bf16[128,256]{1,0:T(8,128)(2,1)S(1)}, f32[64,256]{1,0:T(8,128)S(1)}) custom-call(bf16[1,336,256]{2,1,0:T(8,128)(2,1)S(1)} %get-tuple-element.22.refs_0_, bf16[1,336,256]{2,1,0:T(8,128)(2,1)S(1)} %collective-permute-done.refs_1_, bf16[1,336,256]{2,1,0:T(8,128)(2,1)S(1)} %collective-permute-done.1.refs_2_, ...), custom_call_target="tpu_custom_call" | custom-call | tf_op jit(solution)/shard_map/pallas_call | solution.py:59
  25.9 0.1 collective-permute-start.11
  25.9 1.2 %collective-permute-done.11.refs_3_ = bf16[128,256]{1,0:T(8,128)(2,1)S(1)} collective-permute-done((bf16[128,256]{1,0:T(8,128)(2,1)S(1)}, bf16[128,256]{1,0:T(8,128)(2,1)S(1)}, u32[]{:S(2)}, u32[]{:S(2)}) %collective-permute-start.11) | collective-permute-done | bytes 65568 | tf_op jit(solution)/shard_map/ppermute | solution.py:81
  27.2 0.0 collective-permute-done.10.refs_1_
  27.2 0.1 shard_map.169
  27.3 0.0 copy-start
  27.3 0.0 copy-start.1
  27.3 0.0 copy-start.2
  27.3 1.6 %collective-permute-start.12 = (bf16[256,256]{1,0:T(8,128)(2,1)S(1)}, bf16[256,256]{1,0:T(8,128)(2,1)S(1)}, u32[]{:S(2)}, u32[]{:S(2)}) collective-permute-start(bf16[256,256]{1,0:T(8,128)(2,1)S(1)} %get-tuple-element.29.refs_0_), channel_id=1, source_target_pairs={{0,2},{1,3},{2,0},{3,1},{4,6},{5,7},{6,4},{7,5},{8,10},{9,11},{10,... | collective-permute-start | bytes 393224 | tf_op jit(solution)/shard_map/ppermute | solution.py:81
  28.9 4.0 %collective-permute-done.12.refs_1_ = bf16[256,256]{1,0:T(8,128)(2,1)S(1)} collective-permute-done((bf16[256,256]{1,0:T(8,128)(2,1)S(1)}, bf16[256,256]{1,0:T(8,128)(2,1)S(1)}, u32[]{:S(2)}, u32[]{:S(2)}) %collective-permute-start.12) | collective-permute-done | bytes 131104 | tf_op jit(solution)/shard_map/ppermute | solution.py:81
  32.9 2.7 %collective-permute-start.13 = (bf16[128,256]{1,0:T(8,128)(2,1)S(1)}, bf16[128,256]{1,0:T(8,128)(2,1)S(1)}, u32[]{:S(2)}, u32[]{:S(2)}) collective-permute-start(bf16[128,256]{1,0:T(8,128)(2,1)S(1)} %shard_map.170.refs_0_), channel_id=1, source_target_pairs={{0,4},{1,5},{2,6},{3,7},{4,0},{5,1},{6,2},{7,3},{8,12},{9,13},{10,... | collective-permute-start | bytes 196616 | tf_op jit(solution)/shard_map/ppermute | solution.py:81
  35.6 1.6 %collective-permute-start.4 = (bf16[256,128]{1,0:T(8,128)(2,1)S(1)}, bf16[256,128]{1,0:T(8,128)(2,1)S(1)}, u32[]{:S(2)}, u32[]{:S(2)}) collective-permute-start(bf16[256,128]{1,0:T(8,128)(2,1)S(1)} %get-tuple-element.24.refs_3_), channel_id=1, source_target_pairs={{0,2},{1,3},{2,0},{3,1},{4,6},{5,7},{6,4},{7,5},{8,10},{9,11},{10,... | collective-permute-start | bytes 196616 | tf_op jit(solution)/shard_map/ppermute | solution.py:81
  37.2 0.3 collective-permute-start.6
  37.5 2.5 %collective-permute-start.8 = (bf16[256,128]{1,0:T(8,128)(2,1)S(1)}, bf16[256,128]{1,0:T(8,128)(2,1)S(1)}, u32[]{:S(2)}, u32[]{:S(2)}) collective-permute-start(bf16[256,128]{1,0:T(8,128)(2,1)S(1)} %get-tuple-element.24.refs_3_), channel_id=1, source_target_pairs={{0,6},{1,7},{2,4},{3,5},{4,2},{5,3},{6,0},{7,1},{8,14},{9,15},{10,... | collective-permute-start | bytes 196616 | tf_op jit(solution)/shard_map/ppermute | solution.py:81
  40.0 0.1 collective-permute-start.15
  40.1 0.0 collective-permute-done.13.refs_1_
  40.1 7.9 %collective-permute-start.16 = (bf16[128,256]{1,0:T(8,128)(2,1)S(1)}, bf16[128,256]{1,0:T(8,128)(2,1)S(1)}, u32[]{:S(2)}, u32[]{:S(2)}) collective-permute-start(bf16[128,256]{1,0:T(8,128)(2,1)S(1)} %get-tuple-element.32), channel_id=1, source_target_pairs={{0,6},{1,7},{2,4},{3,5},{4,2},{5,3},{6,0},{7,1},{8,14},{9,15},{10,... | collective-permute-start | bytes 196616 | tf_op jit(solution)/shard_map/ppermute | solution.py:81
  48.1 0.0 collective-permute-done.4.refs_5_
  48.1 0.1 collective-permute-start.3
  48.1 0.0 collective-permute-done.6.refs_7_
  48.2 0.5 collective-permute-start.5
  48.6 0.0 collective-permute-done.8.refs_9_
  48.7 0.1 collective-permute-start.7
  48.7 0.4 collective-permute-done.15.refs_2_
  49.2 0.0 collective-permute-start.14
  49.2 1.2 %collective-permute-done.16.refs_3_ = bf16[128,256]{1,0:T(8,128)(2,1)S(1)} collective-permute-done((bf16[128,256]{1,0:T(8,128)(2,1)S(1)}, bf16[128,256]{1,0:T(8,128)(2,1)S(1)}, u32[]{:S(2)}, u32[]{:S(2)}) %collective-permute-start.16) | collective-permute-done | bytes 65568 | tf_op jit(solution)/shard_map/ppermute | solution.py:81
  50.4 0.0 collective-permute-start.9
  50.4 0.0 collective-permute-done.3.refs_4_
  50.4 1.3 %collective-permute-start.17 = (bf16[1,128,256]{2,1,0:T(8,128)(2,1)S(1)}, bf16[1,128,256]{2,1,0:T(8,128)(2,1)S(1)}, u32[]{:S(2)}, u32[]{:S(2)}) collective-permute-start(bf16[1,128,256]{2,1,0:T(8,128)(2,1)S(1)} %shard_map.172.refs_5_), channel_id=1, source_target_pairs={{0,8},{8,0},{16,24},{24,16},{1,9},{9,1},{17,25},{25,17},{2,10},{10... | collective-permute-start | bytes 196616 | tf_op jit(solution)/shard_map/ppermute | solution.py:81
  51.7 0.0 collective-permute-done.5.refs_6_
  51.7 0.8 %collective-permute-start.18 = (bf16[1,128,256]{2,1,0:T(8,128)(2,1)S(1)}, bf16[1,128,256]{2,1,0:T(8,128)(2,1)S(1)}, u32[]{:S(2)}, u32[]{:S(2)}) collective-permute-start(bf16[1,128,256]{2,1,0:T(8,128)(2,1)S(1)} %shard_map.172.refs_5_), channel_id=1, source_target_pairs={{0,16},{8,24},{16,0},{24,8},{1,17},{9,25},{17,1},{25,9},{2,18},{10... | collective-permute-start | bytes 196616 | tf_op jit(solution)/shard_map/ppermute | solution.py:81
  52.6 0.0 collective-permute-done.7.refs_8_
  52.6 1.4 %collective-permute-start.19 = (bf16[1,128,256]{2,1,0:T(8,128)(2,1)S(1)}, bf16[1,128,256]{2,1,0:T(8,128)(2,1)S(1)}, u32[]{:S(2)}, u32[]{:S(2)}) collective-permute-start(bf16[1,128,256]{2,1,0:T(8,128)(2,1)S(1)} %shard_map.172.refs_5_), channel_id=1, source_target_pairs={{0,24},{8,16},{16,8},{24,0},{1,25},{9,17},{17,9},{25,1},{2,26},{10... | collective-permute-start | bytes 196616 | tf_op jit(solution)/shard_map/ppermute | solution.py:81
  54.0 0.0 collective-permute-done.9.refs_10_
  54.0 2.9 %shard_map.168 = f32[64,256]{1,0:T(8,128)} custom-call(f32[4,1024,128]{2,1,0:T(8,128)S(1)} %get-tuple-element.20.refs_0_, s32[8,512]{1,0:T(8,128)S(1)} %get-tuple-element.21.refs_1_, f32[64,256]{1,0:T(8,128)S(1)} %get-tuple-element.23.refs_2_, bf16[256,128]{1,0:T(8,128)(2,1)S(1)} %get-tuple-element.24.refs_3_, ...), custom_call_target="tpu_custom_call" | custom-call | tf_op jit(solution)/shard_map/pallas_call | solution.py:59
  56.9 0.0 collective-permute-done.17.refs_6_
  56.9 0.0 collective-permute-done.18.refs_7_
  56.9 0.8 %collective-permute-done.19.refs_8_ = bf16[1,128,256]{2,1,0:T(8,128)(2,1)S(1)} collective-permute-done((bf16[1,128,256]{2,1,0:T(8,128)(2,1)S(1)}, bf16[1,128,256]{2,1,0:T(8,128)(2,1)S(1)}, u32[]{:S(2)}, u32[]{:S(2)}) %collective-permute-start.19) | collective-permute-done | bytes 65568 | tf_op jit(solution)/shard_map/ppermute | solution.py:81
  57.7 0.0 collective-permute-done.14.refs_2_
  57.7 0.0 copy-done
  57.7 0.0 copy-done.1
  57.7 0.0 copy-done.2
  57.8 1.0 %shard_map.173 = (f32[128,256]{1,0:T(8,128)}, f32[256,256]{1,0:T(8,128)}, f32[1,256]{1,0:T(1,128)}) custom-call(f32[128,256]{1,0:T(8,128)S(1)} %copy-done.1, f32[128,256]{1,0:T(8,128)S(1)} %shard_map.171.refs_1_, f32[128,256]{1,0:T(8,128)S(1)} %collective-permute-done.14.refs_2_, f32[256,256]{1,0:T(8,128)S(1)} %copy-done, f32[1,256]{1,0:T(1,128)S(1)} %bitcast.4, ...), custom_call_target="tpu_custom_call" | custom-call | tf_op jit(solution)/shard_map/pallas_call | solution.py:59
  (3 shorter events, 0.1 us)
Async XLA Ops:
  10.5 16.7 %collective-permute-start.10 = (bf16[512,256]{1,0:T(8,128)(2,1)S(1)}, bf16[512,256]{1,0:T(8,128)(2,1)S(1)}, u32[]{:S(2)}, u32[]{:S(2)}) collective-permute-start(bf16[512,256]{1,0:T(8,128)(2,1)S(1)} %get-tuple-element.26), channel_id=1, source_target_pairs={{0,1},{1,0},{2,3},{3,2},{4,5},{5,4},{6,7},{7,6},{8,9},{9,8},{10,11... | collective-permute-start | bytes 786440 | tf_op jit(solution)/shard_map/ppermute | solution.py:81
  12.2 7.8 %collective-permute-start = (bf16[1,336,256]{2,1,0:T(8,128)(2,1)S(1)}, bf16[1,336,256]{2,1,0:T(8,128)(2,1)S(1)}, u32[]{:S(2)}, u32[]{:S(2)}) collective-permute-start(bf16[1,336,256]{2,1,0:T(8,128)(2,1)S(1)} %get-tuple-element.22.refs_0_), channel_id=1, source_target_pairs={{0,8},{8,0},{16,24},{24,16},{1,9},{9,1},{17,25},{25,17},{2,10},{10... | collective-permute-start | bytes 516104 | tf_op jit(solution)/shard_map/ppermute | solution.py:81
  14.8 10.2 %collective-permute-start.1 = (bf16[1,336,256]{2,1,0:T(8,128)(2,1)S(1)}, bf16[1,336,256]{2,1,0:T(8,128)(2,1)S(1)}, u32[]{:S(2)}, u32[]{:S(2)}) collective-permute-start(bf16[1,336,256]{2,1,0:T(8,128)(2,1)S(1)} %get-tuple-element.22.refs_0_), channel_id=1, source_target_pairs={{0,16},{8,24},{16,0},{24,8},{1,17},{9,25},{17,1},{25,9},{2,18},{10... | collective-permute-start | bytes 516104 | tf_op jit(solution)/shard_map/ppermute | solution.py:81
  16.3 8.7 %collective-permute-start.2 = (bf16[1,336,256]{2,1,0:T(8,128)(2,1)S(1)}, bf16[1,336,256]{2,1,0:T(8,128)(2,1)S(1)}, u32[]{:S(2)}, u32[]{:S(2)}) collective-permute-start(bf16[1,336,256]{2,1,0:T(8,128)(2,1)S(1)} %get-tuple-element.22.refs_0_), channel_id=1, source_target_pairs={{0,24},{8,16},{16,8},{24,0},{1,25},{9,17},{17,9},{25,1},{2,26},{10... | collective-permute-start | bytes 516104 | tf_op jit(solution)/shard_map/ppermute | solution.py:81
  25.9 1.3 %collective-permute-start.11 = (bf16[128,256]{1,0:T(8,128)(2,1)S(1)}, bf16[128,256]{1,0:T(8,128)(2,1)S(1)}, u32[]{:S(2)}, u32[]{:S(2)}) collective-permute-start(bf16[128,256]{1,0:T(8,128)(2,1)S(1)} %get-tuple-element.28), channel_id=1, source_target_pairs={{0,1},{1,0},{2,3},{3,2},{4,5},{5,4},{6,7},{7,6},{8,9},{9,8},{10,11... | collective-permute-start | bytes 196616 | tf_op jit(solution)/shard_map/ppermute | solution.py:81
  27.3 30.5 %copy-start = (f32[256,256]{1,0:T(8,128)S(1)}, f32[256,256]{1,0:T(8,128)}, u32[]{:S(2)}) copy-start(f32[256,256]{1,0:T(8,128)} %refs_3_.5) | copy-start | bytes 786436
  27.3 30.5 %copy-start.1 = (f32[128,256]{1,0:T(8,128)S(1)}, f32[128,256]{1,0:T(8,128)}, u32[]{:S(2)}) copy-start(f32[128,256]{1,0:T(8,128)} %refs_0_.5) | copy-start | bytes 393220
  27.3 30.5 %copy-start.2 = (f32[256]{0:T(256)S(1)}, f32[256]{0:T(256)}, u32[]{:S(2)}) copy-start(f32[256]{0:T(256)} %param.15) | copy-start | bytes 3076
  27.3 5.6 %collective-permute-start.12 = (bf16[256,256]{1,0:T(8,128)(2,1)S(1)}, bf16[256,256]{1,0:T(8,128)(2,1)S(1)}, u32[]{:S(2)}, u32[]{:S(2)}) collective-permute-start(bf16[256,256]{1,0:T(8,128)(2,1)S(1)} %get-tuple-element.29.refs_0_), channel_id=1, source_target_pairs={{0,2},{1,3},{2,0},{3,1},{4,6},{5,7},{6,4},{7,5},{8,10},{9,11},{10,... | collective-permute-start | bytes 393224 | tf_op jit(solution)/shard_map/ppermute | solution.py:81
  32.9 7.2 %collective-permute-start.13 = (bf16[128,256]{1,0:T(8,128)(2,1)S(1)}, bf16[128,256]{1,0:T(8,128)(2,1)S(1)}, u32[]{:S(2)}, u32[]{:S(2)}) collective-permute-start(bf16[128,256]{1,0:T(8,128)(2,1)S(1)} %shard_map.170.refs_0_), channel_id=1, source_target_pairs={{0,4},{1,5},{2,6},{3,7},{4,0},{5,1},{6,2},{7,3},{8,12},{9,13},{10,... | collective-permute-start | bytes 196616 | tf_op jit(solution)/shard_map/ppermute | solution.py:81
  35.6 12.5 %collective-permute-start.4 = (bf16[256,128]{1,0:T(8,128)(2,1)S(1)}, bf16[256,128]{1,0:T(8,128)(2,1)S(1)}, u32[]{:S(2)}, u32[]{:S(2)}) collective-permute-start(bf16[256,128]{1,0:T(8,128)(2,1)S(1)} %get-tuple-element.24.refs_3_), channel_id=1, source_target_pairs={{0,2},{1,3},{2,0},{3,1},{4,6},{5,7},{6,4},{7,5},{8,10},{9,11},{10,... | collective-permute-start | bytes 196616 | tf_op jit(solution)/shard_map/ppermute | solution.py:81
  37.2 11.0 %collective-permute-start.6 = (bf16[256,128]{1,0:T(8,128)(2,1)S(1)}, bf16[256,128]{1,0:T(8,128)(2,1)S(1)}, u32[]{:S(2)}, u32[]{:S(2)}) collective-permute-start(bf16[256,128]{1,0:T(8,128)(2,1)S(1)} %get-tuple-element.24.refs_3_), channel_id=1, source_target_pairs={{0,4},{1,5},{2,6},{3,7},{4,0},{5,1},{6,2},{7,3},{8,12},{9,13},{10,... | collective-permute-start | bytes 196616 | tf_op jit(solution)/shard_map/ppermute | solution.py:81
  37.5 11.1 %collective-permute-start.8 = (bf16[256,128]{1,0:T(8,128)(2,1)S(1)}, bf16[256,128]{1,0:T(8,128)(2,1)S(1)}, u32[]{:S(2)}, u32[]{:S(2)}) collective-permute-start(bf16[256,128]{1,0:T(8,128)(2,1)S(1)} %get-tuple-element.24.refs_3_), channel_id=1, source_target_pairs={{0,6},{1,7},{2,4},{3,5},{4,2},{5,3},{6,0},{7,1},{8,14},{9,15},{10,... | collective-permute-start | bytes 196616 | tf_op jit(solution)/shard_map/ppermute | solution.py:81
  40.0 9.2 %collective-permute-start.15 = (bf16[128,256]{1,0:T(8,128)(2,1)S(1)}, bf16[128,256]{1,0:T(8,128)(2,1)S(1)}, u32[]{:S(2)}, u32[]{:S(2)}) collective-permute-start(bf16[128,256]{1,0:T(8,128)(2,1)S(1)} %get-tuple-element.31), channel_id=1, source_target_pairs={{0,4},{1,5},{2,6},{3,7},{4,0},{5,1},{6,2},{7,3},{8,12},{9,13},{10,... | collective-permute-start | bytes 196616 | tf_op jit(solution)/shard_map/ppermute | solution.py:81
  40.1 10.3 %collective-permute-start.16 = (bf16[128,256]{1,0:T(8,128)(2,1)S(1)}, bf16[128,256]{1,0:T(8,128)(2,1)S(1)}, u32[]{:S(2)}, u32[]{:S(2)}) collective-permute-start(bf16[128,256]{1,0:T(8,128)(2,1)S(1)} %get-tuple-element.32), channel_id=1, source_target_pairs={{0,6},{1,7},{2,4},{3,5},{4,2},{5,3},{6,0},{7,1},{8,14},{9,15},{10,... | collective-permute-start | bytes 196616 | tf_op jit(solution)/shard_map/ppermute | solution.py:81
  48.1 2.4 %collective-permute-start.3 = (bf16[256,128]{1,0:T(8,128)(2,1)S(1)}, bf16[256,128]{1,0:T(8,128)(2,1)S(1)}, u32[]{:S(2)}, u32[]{:S(2)}) collective-permute-start(bf16[256,128]{1,0:T(8,128)(2,1)S(1)} %get-tuple-element.24.refs_3_), channel_id=1, source_target_pairs={{0,1},{1,0},{2,3},{3,2},{4,5},{5,4},{6,7},{7,6},{8,9},{9,8},{10,11... | collective-permute-start | bytes 196616 | tf_op jit(solution)/shard_map/ppermute | solution.py:81
  48.2 3.6 %collective-permute-start.5 = (bf16[256,128]{1,0:T(8,128)(2,1)S(1)}, bf16[256,128]{1,0:T(8,128)(2,1)S(1)}, u32[]{:S(2)}, u32[]{:S(2)}) collective-permute-start(bf16[256,128]{1,0:T(8,128)(2,1)S(1)} %collective-permute-done.4.refs_5_), channel_id=1, source_target_pairs={{0,1},{1,0},{2,3},{3,2},{4,5},{5,4},{6,7},{7,6},{8,9},{9,8},{10,11... | collective-permute-start | bytes 196616 | tf_op jit(solution)/shard_map/ppermute | solution.py:81
  48.7 3.9 %collective-permute-start.7 = (bf16[256,128]{1,0:T(8,128)(2,1)S(1)}, bf16[256,128]{1,0:T(8,128)(2,1)S(1)}, u32[]{:S(2)}, u32[]{:S(2)}) collective-permute-start(bf16[256,128]{1,0:T(8,128)(2,1)S(1)} %collective-permute-done.6.refs_7_), channel_id=1, source_target_pairs={{0,1},{1,0},{2,3},{3,2},{4,5},{5,4},{6,7},{7,6},{8,9},{9,8},{10,11... | collective-permute-start | bytes 196616 | tf_op jit(solution)/shard_map/ppermute | solution.py:81
  49.2 8.6 %collective-permute-start.14 = (f32[128,256]{1,0:T(8,128)S(1)}, f32[128,256]{1,0:T(8,128)S(1)}, u32[]{:S(2)}, u32[]{:S(2)}) collective-permute-start(f32[128,256]{1,0:T(8,128)S(1)} %shard_map.171.refs_1_), channel_id=1, source_target_pairs={{0,1},{1,0},{2,3},{3,2},{4,5},{5,4},{6,7},{7,6},{8,9},{9,8},{10,11... | collective-permute-start | bytes 393224 | tf_op jit(solution)/shard_map/ppermute | solution.py:81
  50.4 3.6 %collective-permute-start.9 = (bf16[256,128]{1,0:T(8,128)(2,1)S(1)}, bf16[256,128]{1,0:T(8,128)(2,1)S(1)}, u32[]{:S(2)}, u32[]{:S(2)}) collective-permute-start(bf16[256,128]{1,0:T(8,128)(2,1)S(1)} %collective-permute-done.8.refs_9_), channel_id=1, source_target_pairs={{0,1},{1,0},{2,3},{3,2},{4,5},{5,4},{6,7},{7,6},{8,9},{9,8},{10,11... | collective-permute-start | bytes 196616 | tf_op jit(solution)/shard_map/ppermute | solution.py:81
  50.4 6.5 %collective-permute-start.17 = (bf16[1,128,256]{2,1,0:T(8,128)(2,1)S(1)}, bf16[1,128,256]{2,1,0:T(8,128)(2,1)S(1)}, u32[]{:S(2)}, u32[]{:S(2)}) collective-permute-start(bf16[1,128,256]{2,1,0:T(8,128)(2,1)S(1)} %shard_map.172.refs_5_), channel_id=1, source_target_pairs={{0,8},{8,0},{16,24},{24,16},{1,9},{9,1},{17,25},{25,17},{2,10},{10... | collective-permute-start | bytes 196616 | tf_op jit(solution)/shard_map/ppermute | solution.py:81
  51.7 5.2 %collective-permute-start.18 = (bf16[1,128,256]{2,1,0:T(8,128)(2,1)S(1)}, bf16[1,128,256]{2,1,0:T(8,128)(2,1)S(1)}, u32[]{:S(2)}, u32[]{:S(2)}) collective-permute-start(bf16[1,128,256]{2,1,0:T(8,128)(2,1)S(1)} %shard_map.172.refs_5_), channel_id=1, source_target_pairs={{0,16},{8,24},{16,0},{24,8},{1,17},{9,25},{17,1},{25,9},{2,18},{10... | collective-permute-start | bytes 196616 | tf_op jit(solution)/shard_map/ppermute | solution.py:81
  52.6 5.2 %collective-permute-start.19 = (bf16[1,128,256]{2,1,0:T(8,128)(2,1)S(1)}, bf16[1,128,256]{2,1,0:T(8,128)(2,1)S(1)}, u32[]{:S(2)}, u32[]{:S(2)}) collective-permute-start(bf16[1,128,256]{2,1,0:T(8,128)(2,1)S(1)} %shard_map.172.refs_5_), channel_id=1, source_target_pairs={{0,24},{8,16},{16,8},{24,0},{1,25},{9,17},{17,9},{25,1},{2,26},{10... | collective-permute-start | bytes 196616 | tf_op jit(solution)/shard_map/ppermute | solution.py:81

commit v4 on v3

--- a/solution.py
+++ b/solution.py
@@ -1,3 +1,4 @@
+import functools
 import math
 
 import jax
@@ -15,6 +16,7 @@
 TAIL = E2 * E3
 LANES = 128
 PAD = 16
+PITCH = RANK + 1
 FEW = 8
 F32 = jnp.float32
 BF16 = jnp.bfloat16
@@ -81,8 +83,13 @@
     return lax.ppermute(x, axis, [(i, i ^ bits) for i in range(lax.axis_size(axis))])
 
 
-def pack_kernel(table, grads, owner, row, bag, first, hot_out, first_out):
+def pack_kernel(table, grads, owner, row, bag, first, *refs):
+    count = len(refs) // 2 - 1
+    hot_out, first_out = refs[count : count + 2]
+    for src, dst in zip((grads,) + refs[:count], refs[count + 2 :]):
+        dst[...] = src[...]
     rows, bags = table.shape[0], grads.shape[0]
+    lower = first_out.shape[0]
     looks = jnp.concatenate(
         [owner[...], row[...], bag[...], jnp.zeros((PAD - 3, row.shape[1]), jnp.int32)], axis=0
     )
@@ -91,7 +98,7 @@
         hot_out[peer, 0:rows, :] = table[...].astype(BF16)
         hot_out[peer, rows : rows + bags, :] = grads[...]
         hot_out[peer, rows + bags :, :] = looks.astype(F32).astype(BF16)
-    first_out[...] = turned
+    first_out[...] = jnp.concatenate([turned[0:lower], turned[lower:]], axis=1)
 
 
 def maps_kernel(
@@ -104,14 +111,16 @@
     def turn(t, _):
         at = pl.ds(pl.multiple_of(t * LANES, LANES), LANES)
         block = mid[:, at].astype(F32)
-        turned[at, :] = jnp.concatenate([block, block], axis=0).T
+        block = jnp.concatenate([block, block], axis=0).T
+        for part in range(LANES // RANK):
+            turned[pl.ds((t * (LANES // RANK) + part) * PITCH, RANK), :] = block[part * RANK : (part + 1) * RANK, :]
         return 0
 
     lax.fori_loop(0, mid.shape[1] // LANES, turn, 0, unroll=4)
     first_half = iota((RANK * E2, 2 * mids), 1) < mids
     for pair in range(RANK // 2):
-        low = turned[pl.ds(2 * pair, RANK * E2, stride=RANK), :]
-        high = turned[pl.ds(2 * pair + 1, RANK * E2, stride=RANK), :]
+        low = turned[pl.ds(2 * pair, RANK * E2, stride=PITCH), :]
+        high = turned[pl.ds(2 * pair + 1, RANK * E2, stride=PITCH), :]
         left[:, pair * 2 * mids : (pair + 1) * 2 * mids] = jnp.where(first_half, low, high).astype(BF16)
     pick_last = hot(iota((lasts, looks), 0) == last_index[...])
     lasts_of[...] = mm(last[...].astype(F32).T.astype(BF16), pick_last)
@@ -142,9 +151,7 @@
         return 0
 
     lax.fori_loop(0, looks // LANES, back, 0)
-    whole = terms[...]
-    high = whole.astype(BF16)
-    low = (whole - high.astype(F32)).astype(BF16)
+    whole = terms[...].astype(BF16)
     own = owner[...]
     held = keep.shape[0]
     slices = held // (lax.axis_size("tt") // 2)
@@ -155,7 +162,7 @@
     for half, out in ((0, keep), (1, send)):
         for start in range(0, held, step):
             pick = hot(iota((step, looks), 0) + (half * held + start) == key)
-            out[start : start + step, :] = (mm_nt(pick, high) + mm_nt(pick, low)).astype(out.dtype)
+            out[start : start + step, :] = mm_nt(pick, whole).astype(out.dtype)
 
 
 def hot_kernel(*refs):
@@ -196,20 +203,20 @@
     send[...] = grad[half:].astype(BF16)
 
 
-def pair_kernel(cold_keep, cold_got, hot_keep, hot_got, own, *sends):
+def pair_kernel(pairs, cold_keep, cold_got, hot_keep, hot_got, *refs):
+    shards, (held, own, *sends) = refs[:-1 - pairs], refs[-1 - pairs :]
     slices = own.shape[0]
     place = lax.axis_index("tt") >> 1
-    for bits, out in enumerate((own,) + sends):
+    for bits, out in enumerate((own, *sends)):
         at = pl.ds(pl.multiple_of((place ^ bits) * slices, slices), slices)
         out[0:slices, :] = (cold_keep[at, :] + cold_got[at, :].astype(F32)).astype(BF16)
     sends[0][slices:, :] = (hot_keep[...] + hot_got[...].astype(F32)).astype(BF16)
-
-
-def step_kernel(mine, got, total):
-    rows = total.shape[0]
-    total[...] = (
-        mine[mine.shape[0] - rows :, :].astype(F32) + got[got.shape[0] - rows :, :].astype(F32)
-    ).astype(total.dtype)
+    for i, shard in enumerate(shards):
+        held[i * slices : (i + 1) * slices, :] = shard[...]
+
+
+def step_kernel(at, mine, got, total):
+    total[...] = (mine[at:, :].astype(F32) + got[at:, :].astype(F32)).astype(total.dtype)
 
 
 def line_kernel(*refs):
@@ -222,15 +229,19 @@
 
 def rows_kernel(maps, keys, hot_part, *refs):
     gathered, (pooled, slices_of, rows) = refs[:-3], refs[-3:]
-    width, slices = gathered[0].shape
+    slices, width = maps.shape[2], pooled.shape[1]
     me = lax.axis_index("tt")
     looks = keys.shape[1]
     tiles = looks // LANES
     key = keys[0:1, :]
-    total = jnp.zeros((width, looks), F32)
-    for bits, part in enumerate(gathered):
-        pick = hot(iota((slices, looks), 0) + (me ^ bits) * slices == key)
-        total = total + mm(part[...], pick)
+    halves = [jnp.zeros((width // 2, looks), F32) for _ in range(2)]
+    for block, part in enumerate(gathered):
+        for i in range(part.shape[0] // slices):
+            pick = hot(iota((slices, looks), 0) + (me ^ (4 * i + block)) * slices == key)
+            for side in range(2):
+                turned = part[i * slices : (i + 1) * slices, side * slices : (side + 1) * slices]
+                halves[side] = halves[side] + mm(turned, pick)
+    total = jnp.concatenate(halves, axis=0)
     for t in range(tiles):
         slices_of[t] = total[:, t * LANES : (t + 1) * LANES]
 
@@ -287,12 +298,16 @@
     few = hot_peers <= FEW
     tiles = looks // LANES
 
-    hot_pack, first_pack = call(
+    assert 2 * slices == width and slices == LANES
+    given = (core_mid, core_last, mid_index, last_index, cold_bag, slice_owner, first_index)
+    hot_pack, first_pack, bag_grads, *given = call(
         pack_kernel,
-        (((1 if few else hot_peers, rows + bags + PAD, width), BF16), ((width, slices), BF16)),
-        (hot_table, bag_grads, owner, hot_row, hot_bag, core_first),
-        far=6,
-    )
+        (((1 if few else hot_peers, rows + bags + PAD, width), BF16), ((slices, width), BF16))
+        + tuple((x.shape, x.dtype) for x in (bag_grads,) + given),
+        (hot_table, bag_grads, owner, hot_row, hot_bag, core_first) + given,
+        far=6 + len(given),
+    )
+    core_mid, core_last, mid_index, last_index, cold_bag, slice_owner, first_index = given
 
     def spread(x):
         if few:
@@ -308,14 +323,13 @@
         (((held, width), F32), ((held, width), BF16), ((tiles, E3 * RANK * E2, LANES), F32), ((8, looks), jnp.int32)),
         (core_mid, core_last, mid_index, last_index, cold_bag, slice_owner, first_index, bag_grads),
         (
-            ((core_mid.shape[1], LANES), F32),
+            ((core_mid.shape[1] // RANK * PITCH, LANES), F32),
             ((RANK * E2, RANK * core_mid.shape[0]), BF16),
             ((RANK * core_mid.shape[0], looks), BF16),
             ((RANK * E3, looks), F32),
             ((width, looks), F32),
             ((width, looks), F32),
         ),
-        far=8,
     )
     got = swap(send, "tt", 1)
 
@@ -324,30 +338,31 @@
     )
     hot_got = swap(hot_send, "tt", 1)
 
+    shards = [first_pack]
+    for bits in range(2, pairs, 2):
+        shards.append(swap(first_pack, "tt", 2 * bits))
     half = rows // 2
-    pieces = call(
-        pair_kernel,
-        tuple(((slices + (half if bits == 1 else 0), width), BF16) for bits in range(pairs)),
-        (keep, got, hot_keep, hot_got),
+    shard_own, *pieces = call(
+        functools.partial(pair_kernel, pairs),
+        (((slices * len(shards), width), BF16),)
+        + tuple(((slices + (half if bits == 1 else 0), width), BF16) for bits in range(pairs)),
+        (keep, got, hot_keep, hot_got, *shards),
     )
     parts = [pieces[0]]
     for bits in range(1, pairs):
         parts.append(swap(pieces[bits], "tt", 2 * bits))
-
-    shards = [first_pack]
-    for bits in range(1, pairs):
-        shards.append(swap(first_pack, "tt", 2 * bits))
-    first_all = []
-    for bits, shard in enumerate(shards):
-        first_all += [shard, swap(shard, "tt", 1)]
-
-    mine, theirs, bits = pieces[1], parts[1], 2
+    neighbour = swap(shard_own, "tt", 2)
+
+    mine, theirs, at, bits = pieces[1], parts[1], slices, 2
     while bits < pairs:
-        (mine,) = call(step_kernel, (((half, width), BF16),), (mine, theirs))
+        (mine,) = call(functools.partial(step_kernel, at), (((half, width), BF16),), (mine, theirs))
         theirs = swap(mine, "tt", 2 * bits)
-        bits *= 2
-    (hot_half,) = call(step_kernel, (((half, width), F32),), (mine, theirs))
+        at, bits = 0, 2 * bits
+    (hot_half,) = call(functools.partial(step_kernel, at), (((half, width), F32),), (mine, theirs))
     hot_other = swap(hot_half, "tt", 1)
+    own_other = swap(shard_own, "tt", 1)
+    neighbour_other = swap(neighbour, "tt", 1)
+    first_all = (shard_own, own_other, neighbour, neighbour_other)
 
     (cold_send,) = call(line_kernel, (((1 if few else hot_peers, slices, width), BF16),), parts)
     cold_all = spread(cold_send)

time: 59 us -> 50 us (0.85)
  starting transfers between devices: 25.7 us -> 20.1 us
  Pallas kernels: 16 us -> 13.1 us
    ppermute x20 -> x17, starting transfers between devices: 25.7 us -> 20.1 us  [swap(): lax.ppermute(x, axis, [(i, i ^ bits) for i in range(lax.axis_size(axis))])]
    pallas_call x9, Pallas kernels: 16 us -> 13.1 us  [call(): pl.pallas_call(kernel, out_shape=tuple((jax.ShapeDtypeStruct(s, d) for s,...]
    ppermute x20 -> x17, waiting for transfers between devices: 16.3 us -> 15.9 us  [swap(): lax.ppermute(x, axis, [(i, i ^ bits) for i in range(lax.axis_size(axis))])]
  transfers between devices with their start and end apart: 20 -> 17, of which waited for: 7 -> 7; matrix products, arithmetic and copies ran while one was open for 0% -> 0% of each run, Pallas kernels for 9% -> 8%
where the time goes in v4:
time: 50 us; the launch traced here: 49.9 us
  starting transfers between devices  20.1 us (40%)
  waiting for transfers between devices  15.9 us (32%)
  Pallas kernels  13.1 us (26%)
  between operations  0.75 us (2%)
    ppermute x17, starting transfers between devices, swap(): lax.ppermute(x, axis, [(i, i ^ bits) for i in range(lax.axis_size(axis))])  20.1 us
    ppermute x17, waiting for transfers between devices, swap(): lax.ppermute(x, axis, [(i, i ^ bits) for i in range(lax.axis_size(axis))])  15.9 us
    pallas_call x9, Pallas kernels, call(): pl.pallas_call(kernel, out_shape=tuple((jax.ShapeDtypeStruct(s, d) for s,...  13.1 us
  transfers between devices with their start and end apart: 17, of which 7 were waited for; matrix products, arithmetic and copies ran while one was open for 0% of the time, Pallas kernels for 8%

profile of v4, /device:TPU:0, one launch (start us, length us, event | category | flops | bytes accessed | tf_op | source)
XLA Modules:
  0.0 49.9 jit_solution(6289931970953349360)
XLA Ops:
  0.6 1.8 %shard_map.165 = (bf16[1,336,256]{2,1,0:T(8,128)(2,1)S(1)}, bf16[128,256]{1,0:T(8,128)(2,1)S(1)}, bf16[64,256]{1,0:T(8,128)(2,1)S(1)}, bf16[64,8192]{1,0:T(8,128...) custom-call(f32[256,256]{1,0:T(8,128)} %refs_3_.3, ...), custom_call_target="tpu_custom_call" | custom-call | tf_op jit(solution)/shard_map/pallas_call | solution.py:61
  2.4 6.2 %shard_map.166 = (f32[512,256]{1,0:T(8,128)S(1)}, bf16[512,256]{1,0:T(8,128)(2,1)S(1)}, f32[4,1024,128]{2,1,0:T(8,128)S(1)}, s32[8,512]{1,0:T(8,128)S(1)}) custom-call(bf16[64,8192]{1,0:T(8,128)(2,1)S(1)} %get-tuple-element.29.refs_0_, bf16[64,128]{1,0:T(8,128)(2,1)S(1)} %get-tuple-element.30.refs_1_, s32[1,512]{1,0:T(1,128)S(1)} %get-tuple-element.31.refs_2_, ...), custom_call_target="tpu_custom_call" | custom-call | tf_op jit(solution)/shard_map/pallas_call | solution.py:61
  8.7 0.6 %collective-permute-start.3 = (bf16[512,256]{1,0:T(8,128)(2,1)S(1)}, bf16[512,256]{1,0:T(8,128)(2,1)S(1)}, u32[]{:S(2)}, u32[]{:S(2)}) collective-permute-start(bf16[512,256]{1,0:T(8,128)(2,1)S(1)} %get-tuple-element.42), channel_id=1, source_target_pairs={{0,1},{1,0},{2,3},{3,2},{4,5},{5,4},{6,7},{7,6},{8,9},{9,8},{10,11... | collective-permute-start | bytes 786440 | tf_op jit(solution)/shard_map/ppermute | solution.py:83
  9.2 2.6 %collective-permute-start = (bf16[1,336,256]{2,1,0:T(8,128)(2,1)S(1)}, bf16[1,336,256]{2,1,0:T(8,128)(2,1)S(1)}, u32[]{:S(2)}, u32[]{:S(2)}) collective-permute-start(bf16[1,336,256]{2,1,0:T(8,128)(2,1)S(1)} %get-tuple-element.39.refs_0_), channel_id=1, source_target_pairs={{0,8},{8,0},{16,24},{24,16},{1,9},{9,1},{17,25},{25,17},{2,10},{10... | collective-permute-start | bytes 516104 | tf_op jit(solution)/shard_map/ppermute | solution.py:83
  11.8 1.5 %collective-permute-start.1 = (bf16[1,336,256]{2,1,0:T(8,128)(2,1)S(1)}, bf16[1,336,256]{2,1,0:T(8,128)(2,1)S(1)}, u32[]{:S(2)}, u32[]{:S(2)}) collective-permute-start(bf16[1,336,256]{2,1,0:T(8,128)(2,1)S(1)} %get-tuple-element.39.refs_0_), channel_id=1, source_target_pairs={{0,16},{8,24},{16,0},{24,8},{1,17},{9,25},{17,1},{25,9},{2,18},{10... | collective-permute-start | bytes 516104 | tf_op jit(solution)/shard_map/ppermute | solution.py:83
  13.3 0.0 collective-permute-start.2
  13.3 3.0 %collective-permute-start.5 = (bf16[128,256]{1,0:T(8,128)(2,1)S(1)}, bf16[128,256]{1,0:T(8,128)(2,1)S(1)}, u32[]{:S(2)}, u32[]{:S(2)}) collective-permute-start(bf16[128,256]{1,0:T(8,128)(2,1)S(1)} %get-tuple-element.45.refs_4_), channel_id=1, source_target_pairs={{0,4},{1,5},{2,6},{3,7},{4,0},{5,1},{6,2},{7,3},{8,12},{9,13},{10,... | collective-permute-start | bytes 196616 | tf_op jit(solution)/shard_map/ppermute | solution.py:83
  16.4 0.6 %collective-permute-done.refs_1_ = bf16[1,336,256]{2,1,0:T(8,128)(2,1)S(1)} collective-permute-done((bf16[1,336,256]{2,1,0:T(8,128)(2,1)S(1)}, bf16[1,336,256]{2,1,0:T(8,128)(2,1)S(1)}, u32[]{:S(2)}, u32[]{:S(2)}) %collective-permute-start) | collective-permute-done | bytes 172064 | tf_op jit(solution)/shard_map/ppermute | solution.py:83
  17.0 4.9 %collective-permute-done.1.refs_2_ = bf16[1,336,256]{2,1,0:T(8,128)(2,1)S(1)} collective-permute-done((bf16[1,336,256]{2,1,0:T(8,128)(2,1)S(1)}, bf16[1,336,256]{2,1,0:T(8,128)(2,1)S(1)}, u32[]{:S(2)}, u32[]{:S(2)}) %collective-permute-start.1) | collective-permute-done | bytes 172064 | tf_op jit(solution)/shard_map/ppermute | solution.py:83
  21.9 0.0 collective-permute-done.2.refs_3_
  21.9 0.9 %shard_map.167 = (f32[128,256]{1,0:T(8,128)S(1)}, bf16[128,256]{1,0:T(8,128)(2,1)S(1)}, f32[64,256]{1,0:T(8,128)S(1)}) custom-call(bf16[1,336,256]{2,1,0:T(8,128)(2,1)S(1)} %get-tuple-element.39.refs_0_, bf16[1,336,256]{2,1,0:T(8,128)(2,1)S(1)} %collective-permute-done.refs_1_, bf16[1,336,256]{2,1,0:T(8,128)(2,1)S(1)} %collective-permute-done.1.refs_2_, ...), custom_call_target="tpu_custom_call" | custom-call | tf_op jit(solution)/shard_map/pallas_call | solution.py:61
  22.8 0.1 collective-permute-start.4
  22.9 0.0 collective-permute-done.5.refs_5_
  22.9 1.2 %collective-permute-done.4.refs_3_ = bf16[128,256]{1,0:T(8,128)(2,1)S(1)} collective-permute-done((bf16[128,256]{1,0:T(8,128)(2,1)S(1)}, bf16[128,256]{1,0:T(8,128)(2,1)S(1)}, u32[]{:S(2)}, u32[]{:S(2)}) %collective-permute-start.4) | collective-permute-done | bytes 65568 | tf_op jit(solution)/shard_map/ppermute | solution.py:83
  24.1 0.0 collective-permute-done.3.refs_1_
  24.1 0.1 shard_map.168
  24.2 0.0 copy-start
  24.2 0.0 copy-start.1
  24.2 0.0 copy-start.2
  24.2 1.6 %collective-permute-start.9 = (bf16[256,256]{1,0:T(8,128)(2,1)S(1)}, bf16[256,256]{1,0:T(8,128)(2,1)S(1)}, u32[]{:S(2)}, u32[]{:S(2)}) collective-permute-start(bf16[256,256]{1,0:T(8,128)(2,1)S(1)} %get-tuple-element.47.refs_0_), channel_id=1, source_target_pairs={{0,2},{1,3},{2,0},{3,1},{4,6},{5,7},{6,4},{7,5},{8,10},{9,11},{10,... | collective-permute-start | bytes 393224 | tf_op jit(solution)/shard_map/ppermute | solution.py:83
  25.9 0.4 collective-permute-start.7
  26.3 0.0 collective-permute-start.6
  26.3 4.3 %collective-permute-done.9.refs_1_ = bf16[256,256]{1,0:T(8,128)(2,1)S(1)} collective-permute-done((bf16[256,256]{1,0:T(8,128)(2,1)S(1)}, bf16[256,256]{1,0:T(8,128)(2,1)S(1)}, u32[]{:S(2)}, u32[]{:S(2)}) %collective-permute-start.9) | collective-permute-done | bytes 131104 | tf_op jit(solution)/shard_map/ppermute | solution.py:83
  30.7 2.7 %collective-permute-start.10 = (bf16[128,256]{1,0:T(8,128)(2,1)S(1)}, bf16[128,256]{1,0:T(8,128)(2,1)S(1)}, u32[]{:S(2)}, u32[]{:S(2)}) collective-permute-start(bf16[128,256]{1,0:T(8,128)(2,1)S(1)} %shard_map.170.refs_0_), channel_id=1, source_target_pairs={{0,4},{1,5},{2,6},{3,7},{4,0},{5,1},{6,2},{7,3},{8,12},{9,13},{10,... | collective-permute-start | bytes 196616 | tf_op jit(solution)/shard_map/ppermute | solution.py:83
  33.3 0.3 collective-permute-start.12
  33.7 0.0 collective-permute-done.7.refs_5_
  33.7 0.0 collective-permute-start.8
  33.7 3.6 %collective-permute-start.13 = (bf16[128,256]{1,0:T(8,128)(2,1)S(1)}, bf16[128,256]{1,0:T(8,128)(2,1)S(1)}, u32[]{:S(2)}, u32[]{:S(2)}) collective-permute-start(bf16[128,256]{1,0:T(8,128)(2,1)S(1)} %get-tuple-element.50), channel_id=1, source_target_pairs={{0,6},{1,7},{2,4},{3,5},{4,2},{5,3},{6,0},{7,1},{8,14},{9,15},{10,... | collective-permute-start | bytes 196616 | tf_op jit(solution)/shard_map/ppermute | solution.py:83
  37.3 0.8 %collective-permute-done.10.refs_1_ = bf16[128,256]{1,0:T(8,128)(2,1)S(1)} collective-permute-done((bf16[128,256]{1,0:T(8,128)(2,1)S(1)}, bf16[128,256]{1,0:T(8,128)(2,1)S(1)}, u32[]{:S(2)}, u32[]{:S(2)}) %collective-permute-start.10) | collective-permute-done | bytes 65568 | tf_op jit(solution)/shard_map/ppermute | solution.py:83
  38.1 0.1 collective-permute-start.11
  38.1 3.3 %collective-permute-done.12.refs_2_ = bf16[128,256]{1,0:T(8,128)(2,1)S(1)} collective-permute-done((bf16[128,256]{1,0:T(8,128)(2,1)S(1)}, bf16[128,256]{1,0:T(8,128)(2,1)S(1)}, u32[]{:S(2)}, u32[]{:S(2)}) %collective-permute-start.12) | collective-permute-done | bytes 65568 | tf_op jit(solution)/shard_map/ppermute | solution.py:83
  41.5 0.0 collective-permute-done.13.refs_3_
  41.5 1.3 %collective-permute-start.14 = (bf16[1,128,256]{2,1,0:T(8,128)(2,1)S(1)}, bf16[1,128,256]{2,1,0:T(8,128)(2,1)S(1)}, u32[]{:S(2)}, u32[]{:S(2)}) collective-permute-start(bf16[1,128,256]{2,1,0:T(8,128)(2,1)S(1)} %shard_map.172.refs_5_), channel_id=1, source_target_pairs={{0,8},{8,0},{16,24},{24,16},{1,9},{9,1},{17,25},{25,17},{2,10},{10... | collective-permute-start | bytes 196616 | tf_op jit(solution)/shard_map/ppermute | solution.py:83
  42.8 0.8 %collective-permute-start.15 = (bf16[1,128,256]{2,1,0:T(8,128)(2,1)S(1)}, bf16[1,128,256]{2,1,0:T(8,128)(2,1)S(1)}, u32[]{:S(2)}, u32[]{:S(2)}) collective-permute-start(bf16[1,128,256]{2,1,0:T(8,128)(2,1)S(1)} %shard_map.172.refs_5_), channel_id=1, source_target_pairs={{0,16},{8,24},{16,0},{24,8},{1,17},{9,25},{17,1},{25,9},{2,18},{10... | collective-permute-start | bytes 196616 | tf_op jit(solution)/shard_map/ppermute | solution.py:83
  43.6 0.0 collective-permute-done.6.refs_4_
  43.6 1.4 %collective-permute-start.16 = (bf16[1,128,256]{2,1,0:T(8,128)(2,1)S(1)}, bf16[1,128,256]{2,1,0:T(8,128)(2,1)S(1)}, u32[]{:S(2)}, u32[]{:S(2)}) collective-permute-start(bf16[1,128,256]{2,1,0:T(8,128)(2,1)S(1)} %shard_map.172.refs_5_), channel_id=1, source_target_pairs={{0,24},{8,16},{16,8},{24,0},{1,25},{9,17},{17,9},{25,1},{2,26},{10... | collective-permute-start | bytes 196616 | tf_op jit(solution)/shard_map/ppermute | solution.py:83
  45.1 0.0 collective-permute-done.8.refs_6_
  45.1 3.1 %shard_map.169 = f32[64,256]{1,0:T(8,128)} custom-call(f32[4,1024,128]{2,1,0:T(8,128)S(1)} %get-tuple-element.37.refs_0_, s32[8,512]{1,0:T(8,128)S(1)} %get-tuple-element.38.refs_1_, f32[64,256]{1,0:T(8,128)S(1)} %get-tuple-element.40.refs_2_, bf16[256,256]{1,0:T(8,128)(2,1)S(1)} %get-tuple-element.46.refs_3_, ...), custom_call_target="tpu_custom_call" | custom-call | tf_op jit(solution)/shard_map/pallas_call | solution.py:61
  48.1 0.0 collective-permute-done.14.refs_6_
  48.1 0.0 collective-permute-done.15.refs_7_
  48.1 0.7 %collective-permute-done.16.refs_8_ = bf16[1,128,256]{2,1,0:T(8,128)(2,1)S(1)} collective-permute-done((bf16[1,128,256]{2,1,0:T(8,128)(2,1)S(1)}, bf16[1,128,256]{2,1,0:T(8,128)(2,1)S(1)}, u32[]{:S(2)}, u32[]{:S(2)}) %collective-permute-start.16) | collective-permute-done | bytes 65568 | tf_op jit(solution)/shard_map/ppermute | solution.py:83
  48.8 0.0 collective-permute-done.11.refs_2_
  48.8 0.0 copy-done
  48.8 0.0 copy-done.1
  48.8 0.0 copy-done.2
  48.8 1.0 %shard_map.173 = (f32[128,256]{1,0:T(8,128)}, f32[256,256]{1,0:T(8,128)}, f32[1,256]{1,0:T(1,128)}) custom-call(f32[128,256]{1,0:T(8,128)S(1)} %copy-done.1, f32[128,256]{1,0:T(8,128)S(1)} %shard_map.171.refs_1_, f32[128,256]{1,0:T(8,128)S(1)} %collective-permute-done.11.refs_2_, f32[256,256]{1,0:T(8,128)S(1)} %copy-done, f32[1,256]{1,0:T(1,128)S(1)} %bitcast.4, ...), custom_call_target="tpu_custom_call" | custom-call | tf_op jit(solution)/shard_map/pallas_call | solution.py:61
  (3 shorter events, 0.1 us)
Async XLA Ops:
  8.7 15.4 %collective-permute-start.3 = (bf16[512,256]{1,0:T(8,128)(2,1)S(1)}, bf16[512,256]{1,0:T(8,128)(2,1)S(1)}, u32[]{:S(2)}, u32[]{:S(2)}) collective-permute-start(bf16[512,256]{1,0:T(8,128)(2,1)S(1)} %get-tuple-element.42), channel_id=1, source_target_pairs={{0,1},{1,0},{2,3},{3,2},{4,5},{5,4},{6,7},{7,6},{8,9},{9,8},{10,11... | collective-permute-start | bytes 786440 | tf_op jit(solution)/shard_map/ppermute | solution.py:83
  9.2 7.8 %collective-permute-start = (bf16[1,336,256]{2,1,0:T(8,128)(2,1)S(1)}, bf16[1,336,256]{2,1,0:T(8,128)(2,1)S(1)}, u32[]{:S(2)}, u32[]{:S(2)}) collective-permute-start(bf16[1,336,256]{2,1,0:T(8,128)(2,1)S(1)} %get-tuple-element.39.refs_0_), channel_id=1, source_target_pairs={{0,8},{8,0},{16,24},{24,16},{1,9},{9,1},{17,25},{25,17},{2,10},{10... | collective-permute-start | bytes 516104 | tf_op jit(solution)/shard_map/ppermute | solution.py:83
  11.8 10.1 %collective-permute-start.1 = (bf16[1,336,256]{2,1,0:T(8,128)(2,1)S(1)}, bf16[1,336,256]{2,1,0:T(8,128)(2,1)S(1)}, u32[]{:S(2)}, u32[]{:S(2)}) collective-permute-start(bf16[1,336,256]{2,1,0:T(8,128)(2,1)S(1)} %get-tuple-element.39.refs_0_), channel_id=1, source_target_pairs={{0,16},{8,24},{16,0},{24,8},{1,17},{9,25},{17,1},{25,9},{2,18},{10... | collective-permute-start | bytes 516104 | tf_op jit(solution)/shard_map/ppermute | solution.py:83
  13.3 8.6 %collective-permute-start.2 = (bf16[1,336,256]{2,1,0:T(8,128)(2,1)S(1)}, bf16[1,336,256]{2,1,0:T(8,128)(2,1)S(1)}, u32[]{:S(2)}, u32[]{:S(2)}) collective-permute-start(bf16[1,336,256]{2,1,0:T(8,128)(2,1)S(1)} %get-tuple-element.39.refs_0_), channel_id=1, source_target_pairs={{0,24},{8,16},{16,8},{24,0},{1,25},{9,17},{17,9},{25,1},{2,26},{10... | collective-permute-start | bytes 516104 | tf_op jit(solution)/shard_map/ppermute | solution.py:83
  13.3 9.6 %collective-permute-start.5 = (bf16[128,256]{1,0:T(8,128)(2,1)S(1)}, bf16[128,256]{1,0:T(8,128)(2,1)S(1)}, u32[]{:S(2)}, u32[]{:S(2)}) collective-permute-start(bf16[128,256]{1,0:T(8,128)(2,1)S(1)} %get-tuple-element.45.refs_4_), channel_id=1, source_target_pairs={{0,4},{1,5},{2,6},{3,7},{4,0},{5,1},{6,2},{7,3},{8,12},{9,13},{10,... | collective-permute-start | bytes 196616 | tf_op jit(solution)/shard_map/ppermute | solution.py:83
  22.8 1.3 %collective-permute-start.4 = (bf16[128,256]{1,0:T(8,128)(2,1)S(1)}, bf16[128,256]{1,0:T(8,128)(2,1)S(1)}, u32[]{:S(2)}, u32[]{:S(2)}) collective-permute-start(bf16[128,256]{1,0:T(8,128)(2,1)S(1)} %get-tuple-element.44), channel_id=1, source_target_pairs={{0,1},{1,0},{2,3},{3,2},{4,5},{5,4},{6,7},{7,6},{8,9},{9,8},{10,11... | collective-permute-start | bytes 196616 | tf_op jit(solution)/shard_map/ppermute | solution.py:83
  24.2 24.6 %copy-start = (f32[256,256]{1,0:T(8,128)S(1)}, f32[256,256]{1,0:T(8,128)}, u32[]{:S(2)}) copy-start(f32[256,256]{1,0:T(8,128)} %refs_3_.3) | copy-start | bytes 786436
  24.2 24.6 %copy-start.1 = (f32[128,256]{1,0:T(8,128)S(1)}, f32[128,256]{1,0:T(8,128)}, u32[]{:S(2)}) copy-start(f32[128,256]{1,0:T(8,128)} %refs_0_.3) | copy-start | bytes 393220
  24.2 24.6 %copy-start.2 = (f32[256]{0:T(256)S(1)}, f32[256]{0:T(256)}, u32[]{:S(2)}) copy-start(f32[256]{0:T(256)} %param.15) | copy-start | bytes 3076
  24.2 6.4 %collective-permute-start.9 = (bf16[256,256]{1,0:T(8,128)(2,1)S(1)}, bf16[256,256]{1,0:T(8,128)(2,1)S(1)}, u32[]{:S(2)}, u32[]{:S(2)}) collective-permute-start(bf16[256,256]{1,0:T(8,128)(2,1)S(1)} %get-tuple-element.47.refs_0_), channel_id=1, source_target_pairs={{0,2},{1,3},{2,0},{3,1},{4,6},{5,7},{6,4},{7,5},{8,10},{9,11},{10,... | collective-permute-start | bytes 393224 | tf_op jit(solution)/shard_map/ppermute | solution.py:83
  25.9 7.8 %collective-permute-start.7 = (bf16[256,256]{1,0:T(8,128)(2,1)S(1)}, bf16[256,256]{1,0:T(8,128)(2,1)S(1)}, u32[]{:S(2)}, u32[]{:S(2)}) collective-permute-start(bf16[256,256]{1,0:T(8,128)(2,1)S(1)} %get-tuple-element.46.refs_3_), channel_id=1, source_target_pairs={{0,2},{1,3},{2,0},{3,1},{4,6},{5,7},{6,4},{7,5},{8,10},{9,11},{10,... | collective-permute-start | bytes 393224 | tf_op jit(solution)/shard_map/ppermute | solution.py:83
  26.3 17.3 %collective-permute-start.6 = (bf16[256,256]{1,0:T(8,128)(2,1)S(1)}, bf16[256,256]{1,0:T(8,128)(2,1)S(1)}, u32[]{:S(2)}, u32[]{:S(2)}) collective-permute-start(bf16[256,256]{1,0:T(8,128)(2,1)S(1)} %get-tuple-element.46.refs_3_), channel_id=1, source_target_pairs={{0,1},{1,0},{2,3},{3,2},{4,5},{5,4},{6,7},{7,6},{8,9},{9,8},{10,11... | collective-permute-start | bytes 393224 | tf_op jit(solution)/shard_map/ppermute | solution.py:83
  30.7 7.4 %collective-permute-start.10 = (bf16[128,256]{1,0:T(8,128)(2,1)S(1)}, bf16[128,256]{1,0:T(8,128)(2,1)S(1)}, u32[]{:S(2)}, u32[]{:S(2)}) collective-permute-start(bf16[128,256]{1,0:T(8,128)(2,1)S(1)} %shard_map.170.refs_0_), channel_id=1, source_target_pairs={{0,4},{1,5},{2,6},{3,7},{4,0},{5,1},{6,2},{7,3},{8,12},{9,13},{10,... | collective-permute-start | bytes 196616 | tf_op jit(solution)/shard_map/ppermute | solution.py:83
  33.3 8.1 %collective-permute-start.12 = (bf16[128,256]{1,0:T(8,128)(2,1)S(1)}, bf16[128,256]{1,0:T(8,128)(2,1)S(1)}, u32[]{:S(2)}, u32[]{:S(2)}) collective-permute-start(bf16[128,256]{1,0:T(8,128)(2,1)S(1)} %get-tuple-element.49), channel_id=1, source_target_pairs={{0,4},{1,5},{2,6},{3,7},{4,0},{5,1},{6,2},{7,3},{8,12},{9,13},{10,... | collective-permute-start | bytes 196616 | tf_op jit(solution)/shard_map/ppermute | solution.py:83
  33.7 11.4 %collective-permute-start.8 = (bf16[256,256]{1,0:T(8,128)(2,1)S(1)}, bf16[256,256]{1,0:T(8,128)(2,1)S(1)}, u32[]{:S(2)}, u32[]{:S(2)}) collective-permute-start(bf16[256,256]{1,0:T(8,128)(2,1)S(1)} %collective-permute-done.7.refs_5_), channel_id=1, source_target_pairs={{0,1},{1,0},{2,3},{3,2},{4,5},{5,4},{6,7},{7,6},{8,9},{9,8},{10,11... | collective-permute-start | bytes 393224 | tf_op jit(solution)/shard_map/ppermute | solution.py:83
  33.7 7.8 %collective-permute-start.13 = (bf16[128,256]{1,0:T(8,128)(2,1)S(1)}, bf16[128,256]{1,0:T(8,128)(2,1)S(1)}, u32[]{:S(2)}, u32[]{:S(2)}) collective-permute-start(bf16[128,256]{1,0:T(8,128)(2,1)S(1)} %get-tuple-element.50), channel_id=1, source_target_pairs={{0,6},{1,7},{2,4},{3,5},{4,2},{5,3},{6,0},{7,1},{8,14},{9,15},{10,... | collective-permute-start | bytes 196616 | tf_op jit(solution)/shard_map/ppermute | solution.py:83
  38.1 10.7 %collective-permute-start.11 = (f32[128,256]{1,0:T(8,128)S(1)}, f32[128,256]{1,0:T(8,128)S(1)}, u32[]{:S(2)}, u32[]{:S(2)}) collective-permute-start(f32[128,256]{1,0:T(8,128)S(1)} %shard_map.171.refs_1_), channel_id=1, source_target_pairs={{0,1},{1,0},{2,3},{3,2},{4,5},{5,4},{6,7},{7,6},{8,9},{9,8},{10,11... | collective-permute-start | bytes 393224 | tf_op jit(solution)/shard_map/ppermute | solution.py:83
  41.5 6.6 %collective-permute-start.14 = (bf16[1,128,256]{2,1,0:T(8,128)(2,1)S(1)}, bf16[1,128,256]{2,1,0:T(8,128)(2,1)S(1)}, u32[]{:S(2)}, u32[]{:S(2)}) collective-permute-start(bf16[1,128,256]{2,1,0:T(8,128)(2,1)S(1)} %shard_map.172.refs_5_), channel_id=1, source_target_pairs={{0,8},{8,0},{16,24},{24,16},{1,9},{9,1},{17,25},{25,17},{2,10},{10... | collective-permute-start | bytes 196616 | tf_op jit(solution)/shard_map/ppermute | solution.py:83
  42.8 5.3 %collective-permute-start.15 = (bf16[1,128,256]{2,1,0:T(8,128)(2,1)S(1)}, bf16[1,128,256]{2,1,0:T(8,128)(2,1)S(1)}, u32[]{:S(2)}, u32[]{:S(2)}) collective-permute-start(bf16[1,128,256]{2,1,0:T(8,128)(2,1)S(1)} %shard_map.172.refs_5_), channel_id=1, source_target_pairs={{0,16},{8,24},{16,0},{24,8},{1,17},{9,25},{17,1},{25,9},{2,18},{10... | collective-permute-start | bytes 196616 | tf_op jit(solution)/shard_map/ppermute | solution.py:83
  43.6 5.2 %collective-permute-start.16 = (bf16[1,128,256]{2,1,0:T(8,128)(2,1)S(1)}, bf16[1,128,256]{2,1,0:T(8,128)(2,1)S(1)}, u32[]{:S(2)}, u32[]{:S(2)}) collective-permute-start(bf16[1,128,256]{2,1,0:T(8,128)(2,1)S(1)} %shard_map.172.refs_5_), channel_id=1, source_target_pairs={{0,24},{8,16},{16,8},{24,0},{1,25},{9,17},{17,9},{25,1},{2,26},{10... | collective-permute-start | bytes 196616 | tf_op jit(solution)/shard_map/ppermute | solution.py:83

commit v5 on v4

--- a/solution.py
+++ b/solution.py
@@ -17,6 +17,7 @@
 LANES = 128
 PAD = 16
 PITCH = RANK + 1
+STEP = E2 + 1
 FEW = 8
 F32 = jnp.float32
 BF16 = jnp.bfloat16
@@ -66,6 +67,7 @@
         scratch_shapes=[pltpu.VMEM(s, d) for s, d in scratch]
         + ([pltpu.SemaphoreType.DMA((far,))] if far else []),
         compiler_params=pltpu.CompilerParams(vmem_limit_bytes=held + spare),
+        cost_estimate=pl.CostEstimate(flops=2 * 10**9, bytes_accessed=10 << 20, transcendentals=0) if far else None,
     )(*args)
 
 
@@ -108,20 +110,25 @@
     mids, lasts = mid.shape[0], last.shape[0]
     looks = bag.shape[1]
 
+    blocks = mid.shape[1] // (2 * LANES)
+
     def turn(t, _):
-        at = pl.ds(pl.multiple_of(t * LANES, LANES), LANES)
-        block = mid[:, at].astype(F32)
-        block = jnp.concatenate([block, block], axis=0).T
+        block = jnp.concatenate(
+            [mid[:, pl.ds(pl.multiple_of((t + half) * LANES, LANES), LANES)] for half in (0, blocks)], axis=0
+        ).astype(F32).T
         for part in range(LANES // RANK):
             turned[pl.ds((t * (LANES // RANK) + part) * PITCH, RANK), :] = block[part * RANK : (part + 1) * RANK, :]
         return 0
 
-    lax.fori_loop(0, mid.shape[1] // LANES, turn, 0, unroll=4)
-    first_half = iota((RANK * E2, 2 * mids), 1) < mids
+    lax.fori_loop(0, blocks, turn, 0, unroll=8)
+    count = RANK * E2 // 2
+    first_half = iota((count, 2 * mids), 1) < mids
     for pair in range(RANK // 2):
-        low = turned[pl.ds(2 * pair, RANK * E2, stride=PITCH), :]
-        high = turned[pl.ds(2 * pair + 1, RANK * E2, stride=PITCH), :]
-        left[:, pair * 2 * mids : (pair + 1) * 2 * mids] = jnp.where(first_half, low, high).astype(BF16)
+        low = turned[pl.ds(2 * pair, count, stride=PITCH), :]
+        high = turned[pl.ds(2 * pair + 1, count, stride=PITCH), :]
+        at = slice(pair * 2 * mids, (pair + 1) * 2 * mids)
+        left[0:count, at] = jnp.where(first_half, low, pltpu.roll(high, mids, 1)).astype(BF16)
+        left[count:, at] = jnp.where(first_half, pltpu.roll(low, mids, 1), high).astype(BF16)
     pick_last = hot(iota((lasts, looks), 0) == last_index[...])
     lasts_of[...] = mm(last[...].astype(F32).T.astype(BF16), pick_last)
     pick_bag = hot(iota((grads.shape[0], looks), 0) == bag[...])
@@ -135,19 +142,22 @@
                 right[b * mids + part : b * mids + part + PAD, :] = pick_mid[part : part + PAD, :] * spread
         made = mm(left[...], right[...]).astype(BF16).astype(F32)
         for t in range(looks // LANES):
-            maps[t, e3 * RANK * E2 : (e3 + 1) * RANK * E2, :] = made[:, t * LANES : (t + 1) * LANES]
+            for a in range(RANK):
+                at = (e3 * RANK + a) * STEP
+                maps[t, at : at + E2, :] = made[a * E2 : (a + 1) * E2, t * LANES : (t + 1) * LANES]
 
     def back(t, _):
         lanes = pl.ds(pl.multiple_of(t * LANES, LANES), LANES)
-        sums = [jnp.zeros((RANK, LANES), F32) for _ in range(E1)]
-        for e2 in range(E2):
-            for e3 in range(E3):
-                part = maps[t, pl.ds(e3 * RANK * E2 + e2, RANK, stride=E2), :]
-                for e1 in range(E1):
-                    at = e1 * TAIL + e2 * E3 + e3
-                    sums[e1] = sums[e1] + part * cot[at : at + 1, lanes]
-        for e1 in range(E1):
-            terms[e1 * RANK : (e1 + 1) * RANK, lanes] = sums[e1]
+        for first in range(0, E1, E1 // 2):
+            sums = [jnp.zeros((RANK, LANES), F32) for _ in range(E1 // 2)]
+            for e2 in range(E2):
+                for e3 in range(E3):
+                    part = maps[t, pl.ds(e3 * RANK * STEP + e2, RANK, stride=STEP), :]
+                    for i in range(E1 // 2):
+                        at = (first + i) * TAIL + e2 * E3 + e3
+                        sums[i] = sums[i] + part * cot[at : at + 1, lanes]
+            for i in range(E1 // 2):
+                terms[(first + i) * RANK : (first + i + 1) * RANK, lanes] = sums[i]
         return 0
 
     lax.fori_loop(0, looks // LANES, back, 0)
@@ -165,42 +175,46 @@
             out[start : start + step, :] = mm_nt(pick, whole).astype(out.dtype)
 
 
-def hot_kernel(*refs):
-    gathered, (keep, send, pooled) = refs[:-3], refs[-3:]
+def packs_of(gathered):
     me = lax.axis_index("hot")
     if len(gathered) > 1:
-        sources = [(me ^ bits, part.at[0]) for bits, part in enumerate(gathered)]
-        mine = gathered[0].at[0]
-    else:
-        sources = [(peer, gathered[0].at[peer]) for peer in range(gathered[0].shape[0])]
-        mine = gathered[0].at[me]
-    bags = pooled.shape[0]
+        return [(me ^ bits, part.at[0]) for bits, part in enumerate(gathered)], gathered[0].at[0]
+    whole = gathered[0]
+    return [(peer, whole.at[peer]) for peer in range(whole.shape[0])], whole.at[me]
+
+
+def lookups_of(part, at):
+    sent = part[at:, :].astype(F32).astype(jnp.int32)
+    return sent[0:1, :], sent[1:2, :], sent[2:3, :]
+
+
+def hot_kernel(bags, *refs):
+    gathered, (keep, send) = refs[:-2], refs[-2:]
     half = keep.shape[0]
     rows = 2 * half
-
-    def lookups(part):
-        sent = part[rows + bags :, :].astype(F32).astype(jnp.int32)
-        return sent[0:1, :], sent[1:2, :], sent[2:3, :]
-
-    owner, row, bag = lookups(mine)
-    looks = row.shape[1]
-    at = iota((rows, looks), 0)
-    pick_bag = hot(iota((bags, looks), 0) == bag)
-    total = jnp.zeros(pooled.shape, F32)
-    for peer, part in sources:
-        pick = hot((at == row) & (owner == peer))
-        total = total + mm(mm_nt(pick_bag, pick).astype(BF16), part[0:rows, :])
-    pooled[...] = total
-    grad = jnp.zeros((rows, pooled.shape[1]), F32)
-    for peer, part in sources:
-        theirs, place, their_bag = lookups(part)
+    grad = jnp.zeros((rows, keep.shape[1]), F32)
+    for peer, part in packs_of(gathered)[0]:
+        owner, place, bag = lookups_of(part, rows + bags)
         upper = (place >= half).astype(jnp.int32)
         place = (upper ^ core_of()) * half + place - upper * half
-        pick = hot((at == place) & (theirs == me))
-        count = mm_nt(pick, hot(iota((bags, looks), 0) == their_bag))
+        pick = hot((iota((rows, place.shape[1]), 0) == place) & (owner == lax.axis_index("hot")))
+        count = mm_nt(pick, hot(iota((bags, bag.shape[1]), 0) == bag))
         grad = grad + mm(count.astype(BF16), part[rows : rows + bags, :])
     keep[...] = grad[0:half]
     send[...] = grad[half:].astype(BF16)
+
+
+def bags_kernel(rows, *refs):
+    gathered, pooled = refs[:-1], refs[-1]
+    bags = pooled.shape[0]
+    sources, mine = packs_of(gathered)
+    owner, row, bag = lookups_of(mine, rows + bags)
+    pick_bag = hot(iota((bags, bag.shape[1]), 0) == bag)
+    total = jnp.zeros(pooled.shape, F32)
+    for peer, part in sources:
+        pick = hot((iota((rows, row.shape[1]), 0) == row) & (owner == peer))
+        total = total + mm(mm_nt(pick_bag, pick).astype(BF16), part[0:rows, :])
+    pooled[...] = total
 
 
 def pair_kernel(pairs, cold_keep, cold_got, hot_keep, hot_got, *refs):
@@ -248,7 +262,7 @@
     def forward(t, _):
         sums = [[jnp.zeros((E2, LANES), F32) for _ in range(E3)] for _ in range(E1)]
         for a in range(RANK):
-            parts = [maps[t, e3 * RANK * E2 + a * E2 : e3 * RANK * E2 + a * E2 + E2, :] for e3 in range(E3)]
+            parts = [maps[t, (e3 * RANK + a) * STEP : (e3 * RANK + a) * STEP + E2, :] for e3 in range(E3)]
             for e1 in range(E1):
                 entry = slices_of[t, e1 * RANK + a : e1 * RANK + a + 1, :]
                 for e3 in range(E3):
@@ -299,7 +313,7 @@
     tiles = looks // LANES
 
     assert 2 * slices == width and slices == LANES
-    given = (core_mid, core_last, mid_index, last_index, cold_bag, slice_owner, first_index)
+    given = (core_last, mid_index, last_index, cold_bag, slice_owner, first_index)
     hot_pack, first_pack, bag_grads, *given = call(
         pack_kernel,
         (((1 if few else hot_peers, rows + bags + PAD, width), BF16), ((slices, width), BF16))
@@ -307,7 +321,7 @@
         (hot_table, bag_grads, owner, hot_row, hot_bag, core_first) + given,
         far=6 + len(given),
     )
-    core_mid, core_last, mid_index, last_index, cold_bag, slice_owner, first_index = given
+    core_last, mid_index, last_index, cold_bag, slice_owner, first_index = given
 
     def spread(x):
         if few:
@@ -320,10 +334,10 @@
     hot_all = spread(hot_pack)
     keep, send, maps, keys = call(
         maps_kernel,
-        (((held, width), F32), ((held, width), BF16), ((tiles, E3 * RANK * E2, LANES), F32), ((8, looks), jnp.int32)),
+        (((held, width), F32), ((held, width), BF16), ((tiles, E3 * RANK * STEP, LANES), F32), ((8, looks), jnp.int32)),
         (core_mid, core_last, mid_index, last_index, cold_bag, slice_owner, first_index, bag_grads),
         (
-            ((core_mid.shape[1] // RANK * PITCH, LANES), F32),
+            ((RANK * E2 // 2 * PITCH, LANES), F32),
             ((RANK * E2, RANK * core_mid.shape[0]), BF16),
             ((RANK * core_mid.shape[0], looks), BF16),
             ((RANK * E3, looks), F32),
@@ -333,9 +347,11 @@
     )
     got = swap(send, "tt", 1)
 
-    hot_keep, hot_send, hot_part = call(
-        hot_kernel, (((rows // 2, width), F32), ((rows // 2, width), BF16), ((bags, width), F32)), hot_all
-    )
+    hot_keep, hot_send = call(
+        functools.partial(hot_kernel, bags),
+        (((rows // 2, width), F32), ((rows // 2, width), BF16)), hot_all,
+    )
+    (hot_part,) = call(functools.partial(bags_kernel, rows), (((bags, width), F32),), hot_all)
     hot_got = swap(hot_send, "tt", 1)
 
     shards = [first_pack]

time: 50 us -> 48 us (0.960)
  Pallas kernels: 13.1 us -> 11.8 us
  waiting for transfers between devices: 15.9 us -> 15.1 us
    pallas_call x9 -> x10, Pallas kernels: 13.1 us -> 11.8 us  [call(): pl.pallas_call(kernel, out_shape=tuple((jax.ShapeDtypeStruct(s, d) for s,...]
    ppermute x17, waiting for transfers between devices: 15.9 us -> 15.1 us  [swap(): lax.ppermute(x, axis, [(i, i ^ bits) for i in range(lax.axis_size(axis))])]
  transfers between devices with their start and end apart: 17 -> 17, of which waited for: 7 -> 8; matrix products, arithmetic and copies ran while one was open for 0% -> 0% of each run, Pallas kernels for 8% -> 9%
where the time goes in v5:
time: 48 us; the launch traced here: 47.8 us
  starting transfers between devices  20.1 us (42%)
  waiting for transfers between devices  15.1 us (31%)
  Pallas kernels  11.8 us (25%)
  between operations  0.75 us (2%)
    ppermute x17, starting transfers between devices, swap(): lax.ppermute(x, axis, [(i, i ^ bits) for i in range(lax.axis_size(axis))])  20.1 us
    ppermute x17, waiting for transfers between devices, swap(): lax.ppermute(x, axis, [(i, i ^ bits) for i in range(lax.axis_size(axis))])  15.1 us
    pallas_call x10, Pallas kernels, call(): pl.pallas_call(kernel, out_shape=tuple((jax.ShapeDtypeStruct(s, d) for s,...  11.8 us
  transfers between devices with their start and end apart: 17, of which 8 were waited for; matrix products, arithmetic and copies ran while one was open for 0% of the time, Pallas kernels for 9%

profile of v5, /device:TPU:0, one launch (start us, length us, event | category | flops | bytes accessed | tf_op | source)
XLA Modules:
  0.0 47.8 jit_solution(8399422661249887031)
XLA Ops:
  0.6 0.0 copy-start
  0.6 1.4 %shard_map.165 = (bf16[1,336,256]{2,1,0:T(8,128)(2,1)S(1)}, bf16[128,256]{1,0:T(8,128)(2,1)S(1)}, bf16[64,256]{1,0:T(8,128)(2,1)S(1)}, bf16[64,128]{1,0:T(8,128)...) custom-call(f32[256,256]{1,0:T(8,128)} %refs_3_.3, ...), custom_call_target="tpu_custom_call" | custom-call | flops 2000000000 | bytes 10485760 | tf_op jit(solution)/shard_map/pallas_call | solution.py:62
  2.0 0.1 copy-done
  2.1 5.1 %shard_map.166 = (f32[512,256]{1,0:T(8,128)S(1)}, bf16[512,256]{1,0:T(8,128)(2,1)S(1)}, f32[4,1152,128]{2,1,0:T(8,128)S(1)}, s32[8,512]{1,0:T(8,128)S(1)}) custom-call(bf16[64,8192]{1,0:T(8,128)(2,1)S(1)} %copy-done, bf16[64,128]{1,0:T(8,128)(2,1)S(1)} %get-tuple-element.27.refs_1_, s32[1,512]{1,0:T(1,128)S(1)} %get-tuple-element.28.refs_2_, ...), custom_call_target="tpu_custom_call" | custom-call | tf_op jit(solution)/shard_map/pallas_call | solution.py:62
  7.2 0.6 %collective-permute-start.3 = (bf16[512,256]{1,0:T(8,128)(2,1)S(1)}, bf16[512,256]{1,0:T(8,128)(2,1)S(1)}, u32[]{:S(2)}, u32[]{:S(2)}) collective-permute-start(bf16[512,256]{1,0:T(8,128)(2,1)S(1)} %get-tuple-element.38), channel_id=1, source_target_pairs={{0,1},{1,0},{2,3},{3,2},{4,5},{5,4},{6,7},{7,6},{8,9},{9,8},{10,11... | collective-permute-start | bytes 786440 | tf_op jit(solution)/shard_map/ppermute | solution.py:85
  7.7 3.5 %collective-permute-start.2 = (bf16[1,336,256]{2,1,0:T(8,128)(2,1)S(1)}, bf16[1,336,256]{2,1,0:T(8,128)(2,1)S(1)}, u32[]{:S(2)}, u32[]{:S(2)}) collective-permute-start(bf16[1,336,256]{2,1,0:T(8,128)(2,1)S(1)} %get-tuple-element.36.refs_0_), channel_id=1, source_target_pairs={{0,24},{8,16},{16,8},{24,0},{1,25},{9,17},{17,9},{25,1},{2,26},{10... | collective-permute-start | bytes 516104 | tf_op jit(solution)/shard_map/ppermute | solution.py:85
  11.2 0.5 %collective-permute-start.1 = (bf16[1,336,256]{2,1,0:T(8,128)(2,1)S(1)}, bf16[1,336,256]{2,1,0:T(8,128)(2,1)S(1)}, u32[]{:S(2)}, u32[]{:S(2)}) collective-permute-start(bf16[1,336,256]{2,1,0:T(8,128)(2,1)S(1)} %get-tuple-element.36.refs_0_), channel_id=1, source_target_pairs={{0,16},{8,24},{16,0},{24,8},{1,17},{9,25},{17,1},{25,9},{2,18},{10... | collective-permute-start | bytes 516104 | tf_op jit(solution)/shard_map/ppermute | solution.py:85
  11.7 0.1 collective-permute-start
  11.9 3.0 %collective-permute-start.5 = (bf16[128,256]{1,0:T(8,128)(2,1)S(1)}, bf16[128,256]{1,0:T(8,128)(2,1)S(1)}, u32[]{:S(2)}, u32[]{:S(2)}) collective-permute-start(bf16[128,256]{1,0:T(8,128)(2,1)S(1)} %get-tuple-element.41.refs_4_), channel_id=1, source_target_pairs={{0,4},{1,5},{2,6},{3,7},{4,0},{5,1},{6,2},{7,3},{8,12},{9,13},{10,... | collective-permute-start | bytes 196616 | tf_op jit(solution)/shard_map/ppermute | solution.py:85
  14.9 1.6 %collective-permute-done.2.refs_3_ = bf16[1,336,256]{2,1,0:T(8,128)(2,1)S(1)} collective-permute-done((bf16[1,336,256]{2,1,0:T(8,128)(2,1)S(1)}, bf16[1,336,256]{2,1,0:T(8,128)(2,1)S(1)}, u32[]{:S(2)}, u32[]{:S(2)}) %collective-permute-start.2) | collective-permute-done | bytes 172064 | tf_op jit(solution)/shard_map/ppermute | solution.py:85
  16.5 3.4 %collective-permute-done.1.refs_2_ = bf16[1,336,256]{2,1,0:T(8,128)(2,1)S(1)} collective-permute-done((bf16[1,336,256]{2,1,0:T(8,128)(2,1)S(1)}, bf16[1,336,256]{2,1,0:T(8,128)(2,1)S(1)}, u32[]{:S(2)}, u32[]{:S(2)}) %collective-permute-start.1) | collective-permute-done | bytes 172064 | tf_op jit(solution)/shard_map/ppermute | solution.py:85
  19.9 0.3 collective-permute-done.refs_1_
  20.2 0.6 %shard_map.168 = (f32[128,256]{1,0:T(8,128)S(1)}, bf16[128,256]{1,0:T(8,128)(2,1)S(1)}) custom-call(bf16[1,336,256]{2,1,0:T(8,128)(2,1)S(1)} %get-tuple-element.36.refs_0_, bf16[1,336,256]{2,1,0:T(8,128)(2,1)S(1)} %collective-permute-done.refs_1_, bf16[1,336,256]{2,1,0:T(8,128)(2,1)S(1)} %collective-permute-done.1.refs_2_, ...), custom_call_target="tpu_custom_call" | custom-call | tf_op jit(solution)/shard_map/pallas_call | solution.py:62
  20.8 0.1 collective-permute-start.4
  20.9 0.0 collective-permute-done.5.refs_5_
  20.9 1.2 %collective-permute-done.4.refs_3_ = bf16[128,256]{1,0:T(8,128)(2,1)S(1)} collective-permute-done((bf16[128,256]{1,0:T(8,128)(2,1)S(1)}, bf16[128,256]{1,0:T(8,128)(2,1)S(1)}, u32[]{:S(2)}, u32[]{:S(2)}) %collective-permute-start.4) | collective-permute-done | bytes 65568 | tf_op jit(solution)/shard_map/ppermute | solution.py:85
  22.1 0.0 collective-permute-done.3.refs_1_
  22.1 0.1 shard_map.169
  22.2 1.6 %collective-permute-start.9 = (bf16[256,256]{1,0:T(8,128)(2,1)S(1)}, bf16[256,256]{1,0:T(8,128)(2,1)S(1)}, u32[]{:S(2)}, u32[]{:S(2)}) collective-permute-start(bf16[256,256]{1,0:T(8,128)(2,1)S(1)} %get-tuple-element.43.refs_0_), channel_id=1, source_target_pairs={{0,2},{1,3},{2,0},{3,1},{4,6},{5,7},{6,4},{7,5},{8,10},{9,11},{10,... | collective-permute-start | bytes 393224 | tf_op jit(solution)/shard_map/ppermute | solution.py:85
  23.8 0.0 copy-start.1
  23.8 0.0 copy-start.2
  23.8 0.0 copy-start.3
  23.8 0.4 collective-permute-start.7
  24.3 0.0 collective-permute-start.6
  24.3 4.3 %collective-permute-done.9.refs_1_ = bf16[256,256]{1,0:T(8,128)(2,1)S(1)} collective-permute-done((bf16[256,256]{1,0:T(8,128)(2,1)S(1)}, bf16[256,256]{1,0:T(8,128)(2,1)S(1)}, u32[]{:S(2)}, u32[]{:S(2)}) %collective-permute-start.9) | collective-permute-done | bytes 131104 | tf_op jit(solution)/shard_map/ppermute | solution.py:85
  28.6 2.6 %collective-permute-start.10 = (bf16[128,256]{1,0:T(8,128)(2,1)S(1)}, bf16[128,256]{1,0:T(8,128)(2,1)S(1)}, u32[]{:S(2)}, u32[]{:S(2)}) collective-permute-start(bf16[128,256]{1,0:T(8,128)(2,1)S(1)} %shard_map.171.refs_0_), channel_id=1, source_target_pairs={{0,4},{1,5},{2,6},{3,7},{4,0},{5,1},{6,2},{7,3},{8,12},{9,13},{10,... | collective-permute-start | bytes 196616 | tf_op jit(solution)/shard_map/ppermute | solution.py:85
  31.3 0.3 collective-permute-start.12
  31.6 3.6 %collective-permute-start.13 = (bf16[128,256]{1,0:T(8,128)(2,1)S(1)}, bf16[128,256]{1,0:T(8,128)(2,1)S(1)}, u32[]{:S(2)}, u32[]{:S(2)}) collective-permute-start(bf16[128,256]{1,0:T(8,128)(2,1)S(1)} %get-tuple-element.46), channel_id=1, source_target_pairs={{0,6},{1,7},{2,4},{3,5},{4,2},{5,3},{6,0},{7,1},{8,14},{9,15},{10,... | collective-permute-start | bytes 196616 | tf_op jit(solution)/shard_map/ppermute | solution.py:85
  35.2 0.0 collective-permute-done.7.refs_5_
  35.2 0.0 collective-permute-start.8
  35.2 1.5 %collective-permute-done.10.refs_1_ = bf16[128,256]{1,0:T(8,128)(2,1)S(1)} collective-permute-done((bf16[128,256]{1,0:T(8,128)(2,1)S(1)}, bf16[128,256]{1,0:T(8,128)(2,1)S(1)}, u32[]{:S(2)}, u32[]{:S(2)}) %collective-permute-start.10) | collective-permute-done | bytes 65568 | tf_op jit(solution)/shard_map/ppermute | solution.py:85
  36.7 0.1 collective-permute-start.11
  36.8 2.6 %collective-permute-done.12.refs_2_ = bf16[128,256]{1,0:T(8,128)(2,1)S(1)} collective-permute-done((bf16[128,256]{1,0:T(8,128)(2,1)S(1)}, bf16[128,256]{1,0:T(8,128)(2,1)S(1)}, u32[]{:S(2)}, u32[]{:S(2)}) %collective-permute-start.12) | collective-permute-done | bytes 65568 | tf_op jit(solution)/shard_map/ppermute | solution.py:85
  39.4 0.0 collective-permute-done.13.refs_3_
  39.5 1.7 %collective-permute-start.16 = (bf16[1,128,256]{2,1,0:T(8,128)(2,1)S(1)}, bf16[1,128,256]{2,1,0:T(8,128)(2,1)S(1)}, u32[]{:S(2)}, u32[]{:S(2)}) collective-permute-start(bf16[1,128,256]{2,1,0:T(8,128)(2,1)S(1)} %shard_map.173.refs_5_), channel_id=1, source_target_pairs={{0,24},{8,16},{16,8},{24,0},{1,25},{9,17},{17,9},{25,1},{2,26},{10... | collective-permute-start | bytes 196616 | tf_op jit(solution)/shard_map/ppermute | solution.py:85
  41.1 1.3 %collective-permute-start.15 = (bf16[1,128,256]{2,1,0:T(8,128)(2,1)S(1)}, bf16[1,128,256]{2,1,0:T(8,128)(2,1)S(1)}, u32[]{:S(2)}, u32[]{:S(2)}) collective-permute-start(bf16[1,128,256]{2,1,0:T(8,128)(2,1)S(1)} %shard_map.173.refs_5_), channel_id=1, source_target_pairs={{0,16},{8,24},{16,0},{24,8},{1,17},{9,25},{17,1},{25,9},{2,18},{10... | collective-permute-start | bytes 196616 | tf_op jit(solution)/shard_map/ppermute | solution.py:85
  42.5 0.0 collective-permute-done.6.refs_4_
  42.5 0.5 %collective-permute-start.14 = (bf16[1,128,256]{2,1,0:T(8,128)(2,1)S(1)}, bf16[1,128,256]{2,1,0:T(8,128)(2,1)S(1)}, u32[]{:S(2)}, u32[]{:S(2)}) collective-permute-start(bf16[1,128,256]{2,1,0:T(8,128)(2,1)S(1)} %shard_map.173.refs_5_), channel_id=1, source_target_pairs={{0,8},{8,0},{16,24},{24,16},{1,9},{9,1},{17,25},{25,17},{2,10},{10... | collective-permute-start | bytes 196616 | tf_op jit(solution)/shard_map/ppermute | solution.py:85
  43.0 0.5 shard_map.167.refs_2_
  43.5 0.0 collective-permute-done.8.refs_6_
  43.5 3.1 %shard_map.170 = f32[64,256]{1,0:T(8,128)} custom-call(f32[4,1152,128]{2,1,0:T(8,128)S(1)} %get-tuple-element.34.refs_0_, s32[8,512]{1,0:T(8,128)S(1)} %get-tuple-element.35.refs_1_, f32[64,256]{1,0:T(8,128)S(1)} %shard_map.167.refs_2_, bf16[256,256]{1,0:T(8,128)(2,1)S(1)} %get-tuple-element.42.refs_3_, bf16[256,256]{1,0:T(8,128)(2,1)S(1)} %collective-permute-done.6.refs_4_, ...), custom_call_target="tpu_custom_call" | custom-call | tf_op jit(solution)/shard_map/pallas_call | solution.py:62
  46.6 0.0 collective-permute-done.16.refs_8_
  46.6 0.0 collective-permute-done.15.refs_7_
  46.6 0.1 collective-permute-done.14.refs_6_
  46.7 0.0 collective-permute-done.11.refs_2_
  46.8 0.0 copy-done.1
  46.8 0.0 copy-done.2
  46.8 0.0 copy-done.3
  46.8 1.0 %shard_map.174 = (f32[128,256]{1,0:T(8,128)}, f32[256,256]{1,0:T(8,128)}, f32[1,256]{1,0:T(1,128)}) custom-call(f32[128,256]{1,0:T(8,128)S(1)} %copy-done.2, f32[128,256]{1,0:T(8,128)S(1)} %shard_map.172.refs_1_, f32[128,256]{1,0:T(8,128)S(1)} %collective-permute-done.11.refs_2_, f32[256,256]{1,0:T(8,128)S(1)} %copy-done.1, f32[1,256]{1,0:T(1,128)S(1)} %bitcast.4, ...), custom_call_target="tpu_custom_call" | custom-call | tf_op jit(solution)/shard_map/pallas_call | solution.py:62
  (3 shorter events, 0.1 us)
Async XLA Ops:
  0.6 1.5 %copy-start = (bf16[64,8192]{1,0:T(8,128)(2,1)S(1)}, bf16[64,8192]{1,0:T(8,128)(2,1)}, u32[]{:S(2)}) copy-start(bf16[64,8192]{1,0:T(8,128)(2,1)} %refs_0_.4) | copy-start | bytes 3145732
  7.2 14.9 %collective-permute-start.3 = (bf16[512,256]{1,0:T(8,128)(2,1)S(1)}, bf16[512,256]{1,0:T(8,128)(2,1)S(1)}, u32[]{:S(2)}, u32[]{:S(2)}) collective-permute-start(bf16[512,256]{1,0:T(8,128)(2,1)S(1)} %get-tuple-element.38), channel_id=1, source_target_pairs={{0,1},{1,0},{2,3},{3,2},{4,5},{5,4},{6,7},{7,6},{8,9},{9,8},{10,11... | collective-permute-start | bytes 786440 | tf_op jit(solution)/shard_map/ppermute | solution.py:85
  7.7 8.8 %collective-permute-start.2 = (bf16[1,336,256]{2,1,0:T(8,128)(2,1)S(1)}, bf16[1,336,256]{2,1,0:T(8,128)(2,1)S(1)}, u32[]{:S(2)}, u32[]{:S(2)}) collective-permute-start(bf16[1,336,256]{2,1,0:T(8,128)(2,1)S(1)} %get-tuple-element.36.refs_0_), channel_id=1, source_target_pairs={{0,24},{8,16},{16,8},{24,0},{1,25},{9,17},{17,9},{25,1},{2,26},{10... | collective-permute-start | bytes 516104 | tf_op jit(solution)/shard_map/ppermute | solution.py:85
  11.2 8.7 %collective-permute-start.1 = (bf16[1,336,256]{2,1,0:T(8,128)(2,1)S(1)}, bf16[1,336,256]{2,1,0:T(8,128)(2,1)S(1)}, u32[]{:S(2)}, u32[]{:S(2)}) collective-permute-start(bf16[1,336,256]{2,1,0:T(8,128)(2,1)S(1)} %get-tuple-element.36.refs_0_), channel_id=1, source_target_pairs={{0,16},{8,24},{16,0},{24,8},{1,17},{9,25},{17,1},{25,9},{2,18},{10... | collective-permute-start | bytes 516104 | tf_op jit(solution)/shard_map/ppermute | solution.py:85
  11.7 8.4 %collective-permute-start = (bf16[1,336,256]{2,1,0:T(8,128)(2,1)S(1)}, bf16[1,336,256]{2,1,0:T(8,128)(2,1)S(1)}, u32[]{:S(2)}, u32[]{:S(2)}) collective-permute-start(bf16[1,336,256]{2,1,0:T(8,128)(2,1)S(1)} %get-tuple-element.36.refs_0_), channel_id=1, source_target_pairs={{0,8},{8,0},{16,24},{24,16},{1,9},{9,1},{17,25},{25,17},{2,10},{10... | collective-permute-start | bytes 516104 | tf_op jit(solution)/shard_map/ppermute | solution.py:85
  11.9 9.0 %collective-permute-start.5 = (bf16[128,256]{1,0:T(8,128)(2,1)S(1)}, bf16[128,256]{1,0:T(8,128)(2,1)S(1)}, u32[]{:S(2)}, u32[]{:S(2)}) collective-permute-start(bf16[128,256]{1,0:T(8,128)(2,1)S(1)} %get-tuple-element.41.refs_4_), channel_id=1, source_target_pairs={{0,4},{1,5},{2,6},{3,7},{4,0},{5,1},{6,2},{7,3},{8,12},{9,13},{10,... | collective-permute-start | bytes 196616 | tf_op jit(solution)/shard_map/ppermute | solution.py:85
  20.8 1.3 %collective-permute-start.4 = (bf16[128,256]{1,0:T(8,128)(2,1)S(1)}, bf16[128,256]{1,0:T(8,128)(2,1)S(1)}, u32[]{:S(2)}, u32[]{:S(2)}) collective-permute-start(bf16[128,256]{1,0:T(8,128)(2,1)S(1)} %get-tuple-element.40), channel_id=1, source_target_pairs={{0,1},{1,0},{2,3},{3,2},{4,5},{5,4},{6,7},{7,6},{8,9},{9,8},{10,11... | collective-permute-start | bytes 196616 | tf_op jit(solution)/shard_map/ppermute | solution.py:85
  22.2 6.4 %collective-permute-start.9 = (bf16[256,256]{1,0:T(8,128)(2,1)S(1)}, bf16[256,256]{1,0:T(8,128)(2,1)S(1)}, u32[]{:S(2)}, u32[]{:S(2)}) collective-permute-start(bf16[256,256]{1,0:T(8,128)(2,1)S(1)} %get-tuple-element.43.refs_0_), channel_id=1, source_target_pairs={{0,2},{1,3},{2,0},{3,1},{4,6},{5,7},{6,4},{7,5},{8,10},{9,11},{10,... | collective-permute-start | bytes 393224 | tf_op jit(solution)/shard_map/ppermute | solution.py:85
  23.8 22.9 %copy-start.1 = (f32[256,256]{1,0:T(8,128)S(1)}, f32[256,256]{1,0:T(8,128)}, u32[]{:S(2)}) copy-start(f32[256,256]{1,0:T(8,128)} %refs_3_.3) | copy-start | bytes 786436
  23.8 22.9 %copy-start.2 = (f32[128,256]{1,0:T(8,128)S(1)}, f32[128,256]{1,0:T(8,128)}, u32[]{:S(2)}) copy-start(f32[128,256]{1,0:T(8,128)} %refs_0_.5) | copy-start | bytes 393220
  23.8 22.9 %copy-start.3 = (f32[256]{0:T(256)S(1)}, f32[256]{0:T(256)}, u32[]{:S(2)}) copy-start(f32[256]{0:T(256)} %param.15) | copy-start | bytes 3076
  23.8 11.4 %collective-permute-start.7 = (bf16[256,256]{1,0:T(8,128)(2,1)S(1)}, bf16[256,256]{1,0:T(8,128)(2,1)S(1)}, u32[]{:S(2)}, u32[]{:S(2)}) collective-permute-start(bf16[256,256]{1,0:T(8,128)(2,1)S(1)} %get-tuple-element.42.refs_3_), channel_id=1, source_target_pairs={{0,2},{1,3},{2,0},{3,1},{4,6},{5,7},{6,4},{7,5},{8,10},{9,11},{10,... | collective-permute-start | bytes 393224 | tf_op jit(solution)/shard_map/ppermute | solution.py:85
  24.3 18.2 %collective-permute-start.6 = (bf16[256,256]{1,0:T(8,128)(2,1)S(1)}, bf16[256,256]{1,0:T(8,128)(2,1)S(1)}, u32[]{:S(2)}, u32[]{:S(2)}) collective-permute-start(bf16[256,256]{1,0:T(8,128)(2,1)S(1)} %get-tuple-element.42.refs_3_), channel_id=1, source_target_pairs={{0,1},{1,0},{2,3},{3,2},{4,5},{5,4},{6,7},{7,6},{8,9},{9,8},{10,11... | collective-permute-start | bytes 393224 | tf_op jit(solution)/shard_map/ppermute | solution.py:85
  28.6 8.1 %collective-permute-start.10 = (bf16[128,256]{1,0:T(8,128)(2,1)S(1)}, bf16[128,256]{1,0:T(8,128)(2,1)S(1)}, u32[]{:S(2)}, u32[]{:S(2)}) collective-permute-start(bf16[128,256]{1,0:T(8,128)(2,1)S(1)} %shard_map.171.refs_0_), channel_id=1, source_target_pairs={{0,4},{1,5},{2,6},{3,7},{4,0},{5,1},{6,2},{7,3},{8,12},{9,13},{10,... | collective-permute-start | bytes 196616 | tf_op jit(solution)/shard_map/ppermute | solution.py:85
  31.3 8.1 %collective-permute-start.12 = (bf16[128,256]{1,0:T(8,128)(2,1)S(1)}, bf16[128,256]{1,0:T(8,128)(2,1)S(1)}, u32[]{:S(2)}, u32[]{:S(2)}) collective-permute-start(bf16[128,256]{1,0:T(8,128)(2,1)S(1)} %get-tuple-element.45), channel_id=1, source_target_pairs={{0,4},{1,5},{2,6},{3,7},{4,0},{5,1},{6,2},{7,3},{8,12},{9,13},{10,... | collective-permute-start | bytes 196616 | tf_op jit(solution)/shard_map/ppermute | solution.py:85
  31.6 7.8 %collective-permute-start.13 = (bf16[128,256]{1,0:T(8,128)(2,1)S(1)}, bf16[128,256]{1,0:T(8,128)(2,1)S(1)}, u32[]{:S(2)}, u32[]{:S(2)}) collective-permute-start(bf16[128,256]{1,0:T(8,128)(2,1)S(1)} %get-tuple-element.46), channel_id=1, source_target_pairs={{0,6},{1,7},{2,4},{3,5},{4,2},{5,3},{6,0},{7,1},{8,14},{9,15},{10,... | collective-permute-start | bytes 196616 | tf_op jit(solution)/shard_map/ppermute | solution.py:85
  35.2 8.3 %collective-permute-start.8 = (bf16[256,256]{1,0:T(8,128)(2,1)S(1)}, bf16[256,256]{1,0:T(8,128)(2,1)S(1)}, u32[]{:S(2)}, u32[]{:S(2)}) collective-permute-start(bf16[256,256]{1,0:T(8,128)(2,1)S(1)} %collective-permute-done.7.refs_5_), channel_id=1, source_target_pairs={{0,1},{1,0},{2,3},{3,2},{4,5},{5,4},{6,7},{7,6},{8,9},{9,8},{10,11... | collective-permute-start | bytes 393224 | tf_op jit(solution)/shard_map/ppermute | solution.py:85
  36.7 10.0 %collective-permute-start.11 = (f32[128,256]{1,0:T(8,128)S(1)}, f32[128,256]{1,0:T(8,128)S(1)}, u32[]{:S(2)}, u32[]{:S(2)}) collective-permute-start(f32[128,256]{1,0:T(8,128)S(1)} %shard_map.172.refs_1_), channel_id=1, source_target_pairs={{0,1},{1,0},{2,3},{3,2},{4,5},{5,4},{6,7},{7,6},{8,9},{9,8},{10,11... | collective-permute-start | bytes 393224 | tf_op jit(solution)/shard_map/ppermute | solution.py:85
  39.5 7.2 %collective-permute-start.16 = (bf16[1,128,256]{2,1,0:T(8,128)(2,1)S(1)}, bf16[1,128,256]{2,1,0:T(8,128)(2,1)S(1)}, u32[]{:S(2)}, u32[]{:S(2)}) collective-permute-start(bf16[1,128,256]{2,1,0:T(8,128)(2,1)S(1)} %shard_map.173.refs_5_), channel_id=1, source_target_pairs={{0,24},{8,16},{16,8},{24,0},{1,25},{9,17},{17,9},{25,1},{2,26},{10... | collective-permute-start | bytes 196616 | tf_op jit(solution)/shard_map/ppermute | solution.py:85
  41.1 5.5 %collective-permute-start.15 = (bf16[1,128,256]{2,1,0:T(8,128)(2,1)S(1)}, bf16[1,128,256]{2,1,0:T(8,128)(2,1)S(1)}, u32[]{:S(2)}, u32[]{:S(2)}) collective-permute-start(bf16[1,128,256]{2,1,0:T(8,128)(2,1)S(1)} %shard_map.173.refs_5_), channel_id=1, source_target_pairs={{0,16},{8,24},{16,0},{24,8},{1,17},{9,25},{17,1},{25,9},{2,18},{10... | collective-permute-start | bytes 196616 | tf_op jit(solution)/shard_map/ppermute | solution.py:85
  42.5 4.3 %collective-permute-start.14 = (bf16[1,128,256]{2,1,0:T(8,128)(2,1)S(1)}, bf16[1,128,256]{2,1,0:T(8,128)(2,1)S(1)}, u32[]{:S(2)}, u32[]{:S(2)}) collective-permute-start(bf16[1,128,256]{2,1,0:T(8,128)(2,1)S(1)} %shard_map.173.refs_5_), channel_id=1, source_target_pairs={{0,8},{8,0},{16,24},{24,16},{1,9},{9,1},{17,25},{25,17},{2,10},{10... | collective-permute-start | bytes 196616 | tf_op jit(solution)/shard_map/ppermute | solution.py:85

commit v6 on v5

--- a/solution.py
+++ b/solution.py
@@ -204,8 +204,9 @@
     send[...] = grad[half:].astype(BF16)
 
 
-def bags_kernel(rows, *refs):
-    gathered, pooled = refs[:-1], refs[-1]
+def bags_kernel(rows, keys, own, other, *refs):
+    gathered, (pooled, near) = refs[:-2], refs[-2:]
+    near[...] = slices_from(keys, ((0, own), (1, other)), near.shape[0])
     bags = pooled.shape[0]
     sources, mine = packs_of(gathered)
     owner, row, bag = lookups_of(mine, rows + bags)
@@ -241,21 +242,23 @@
         cold[peer] = sent
 
 
-def rows_kernel(maps, keys, hot_part, *refs):
-    gathered, (pooled, slices_of, rows) = refs[:-3], refs[-3:]
-    slices, width = maps.shape[2], pooled.shape[1]
+def slices_from(keys, blocks, width):
+    slices, looks = LANES, keys.shape[1]
     me = lax.axis_index("tt")
-    looks = keys.shape[1]
-    tiles = looks // LANES
-    key = keys[0:1, :]
     halves = [jnp.zeros((width // 2, looks), F32) for _ in range(2)]
-    for block, part in enumerate(gathered):
+    for block, part in blocks:
         for i in range(part.shape[0] // slices):
-            pick = hot(iota((slices, looks), 0) + (me ^ (4 * i + block)) * slices == key)
+            pick = hot(iota((slices, looks), 0) + (me ^ (4 * i + block)) * slices == keys[0:1, :])
             for side in range(2):
                 turned = part[i * slices : (i + 1) * slices, side * slices : (side + 1) * slices]
                 halves[side] = halves[side] + mm(turned, pick)
-    total = jnp.concatenate(halves, axis=0)
+    return jnp.concatenate(halves, axis=0)
+
+
+def rows_kernel(maps, keys, hot_part, near, third, fourth, pooled, slices_of, rows):
+    width, looks = near.shape
+    tiles = looks // LANES
+    total = near[...] + slices_from(keys, ((2, third), (3, fourth)), width)
     for t in range(tiles):
         slices_of[t] = total[:, t * LANES : (t + 1) * LANES]
 
@@ -351,7 +354,6 @@
         functools.partial(hot_kernel, bags),
         (((rows // 2, width), F32), ((rows // 2, width), BF16)), hot_all,
     )
-    (hot_part,) = call(functools.partial(bags_kernel, rows), (((bags, width), F32),), hot_all)
     hot_got = swap(hot_send, "tt", 1)
 
     shards = [first_pack]
@@ -377,15 +379,18 @@
     (hot_half,) = call(functools.partial(step_kernel, at), (((half, width), F32),), (mine, theirs))
     hot_other = swap(hot_half, "tt", 1)
     own_other = swap(shard_own, "tt", 1)
+    hot_part, near = call(
+        functools.partial(bags_kernel, rows), (((bags, width), F32), ((width, looks), F32)),
+        (keys, shard_own, own_other, *hot_all),
+    )
     neighbour_other = swap(neighbour, "tt", 1)
-    first_all = (shard_own, own_other, neighbour, neighbour_other)
 
     (cold_send,) = call(line_kernel, (((1 if few else hot_peers, slices, width), BF16),), parts)
     cold_all = spread(cold_send)
 
     (pooled,) = call(
         rows_kernel, (((bags, width), F32),),
-        (maps, keys, hot_part, *first_all),
+        (maps, keys, hot_part, near, neighbour, neighbour_other),
         (((tiles, width, LANES), F32), ((tiles, width, LANES), F32)),
     )
 

time: 48 us -> 48 us (level)
  no operation moved by 1% of the time
where the time goes in v6:
time: 48 us; the launch traced here: 47.8 us
  starting transfers between devices  20.1 us (42%)
  waiting for transfers between devices  15.1 us (31%)
  Pallas kernels  11.8 us (25%)
  between operations  0.77 us (2%)
    ppermute x17, starting transfers between devices, swap(): lax.ppermute(x, axis, [(i, i ^ bits) for i in range(lax.axis_size(axis))])  20.1 us
    ppermute x17, waiting for transfers between devices, swap(): lax.ppermute(x, axis, [(i, i ^ bits) for i in range(lax.axis_size(axis))])  15.1 us
    pallas_call x10, Pallas kernels, call(): pl.pallas_call(kernel, out_shape=tuple((jax.ShapeDtypeStruct(s, d) for s,...  11.8 us
  transfers between devices with their start and end apart: 17, of which 8 were waited for; matrix products, arithmetic and copies ran while one was open for 0% of the time, Pallas kernels for 9%

profile of v6, /device:TPU:0, one launch (start us, length us, event | category | flops | bytes accessed | tf_op | source)
XLA Modules:
  0.0 47.8 jit_solution(15782454025780639591)
XLA Ops:
  0.6 0.0 copy-start
  0.6 1.4 %shard_map.165 = (bf16[1,336,256]{2,1,0:T(8,128)(2,1)S(1)}, bf16[128,256]{1,0:T(8,128)(2,1)S(1)}, bf16[64,256]{1,0:T(8,128)(2,1)S(1)}, bf16[64,128]{1,0:T(8,128)...) custom-call(f32[256,256]{1,0:T(8,128)} %refs_3_.3, ...), custom_call_target="tpu_custom_call" | custom-call | flops 2000000000 | bytes 10485760 | tf_op jit(solution)/shard_map/pallas_call | solution.py:62
  2.0 0.1 copy-done
  2.1 5.1 %shard_map.166 = (f32[512,256]{1,0:T(8,128)S(1)}, bf16[512,256]{1,0:T(8,128)(2,1)S(1)}, f32[4,1152,128]{2,1,0:T(8,128)S(1)}, s32[8,512]{1,0:T(8,128)S(1)}) custom-call(bf16[64,8192]{1,0:T(8,128)(2,1)S(1)} %copy-done, bf16[64,128]{1,0:T(8,128)(2,1)S(1)} %get-tuple-element.29.refs_1_, s32[1,512]{1,0:T(1,128)S(1)} %get-tuple-element.30.refs_2_, ...), custom_call_target="tpu_custom_call" | custom-call | tf_op jit(solution)/shard_map/pallas_call | solution.py:62
  7.2 0.6 %collective-permute-start = (bf16[512,256]{1,0:T(8,128)(2,1)S(1)}, bf16[512,256]{1,0:T(8,128)(2,1)S(1)}, u32[]{:S(2)}, u32[]{:S(2)}) collective-permute-start(bf16[512,256]{1,0:T(8,128)(2,1)S(1)} %get-tuple-element.39), channel_id=1, source_target_pairs={{0,1},{1,0},{2,3},{3,2},{4,5},{5,4},{6,7},{7,6},{8,9},{9,8},{10,11... | collective-permute-start | bytes 786440 | tf_op jit(solution)/shard_map/ppermute | solution.py:85
  7.7 3.5 %collective-permute-start.3 = (bf16[1,336,256]{2,1,0:T(8,128)(2,1)S(1)}, bf16[1,336,256]{2,1,0:T(8,128)(2,1)S(1)}, u32[]{:S(2)}, u32[]{:S(2)}) collective-permute-start(bf16[1,336,256]{2,1,0:T(8,128)(2,1)S(1)} %get-tuple-element.40.refs_0_.refs_3_), channel_id=1, source_target_pairs={{0,24},{8,16},{16,8},{24,0},{1,25},{9,17},{17,9},{25,1},{2,26},{10... | collective-permute-start | bytes 516104 | tf_op jit(solution)/shard_map/ppermute | solution.py:85
  11.2 0.5 %collective-permute-start.2 = (bf16[1,336,256]{2,1,0:T(8,128)(2,1)S(1)}, bf16[1,336,256]{2,1,0:T(8,128)(2,1)S(1)}, u32[]{:S(2)}, u32[]{:S(2)}) collective-permute-start(bf16[1,336,256]{2,1,0:T(8,128)(2,1)S(1)} %get-tuple-element.40.refs_0_.refs_3_), channel_id=1, source_target_pairs={{0,16},{8,24},{16,0},{24,8},{1,17},{9,25},{17,1},{25,9},{2,18},{10... | collective-permute-start | bytes 516104 | tf_op jit(solution)/shard_map/ppermute | solution.py:85
  11.7 0.1 collective-permute-start.1
  11.9 3.0 %collective-permute-start.5 = (bf16[128,256]{1,0:T(8,128)(2,1)S(1)}, bf16[128,256]{1,0:T(8,128)(2,1)S(1)}, u32[]{:S(2)}, u32[]{:S(2)}) collective-permute-start(bf16[128,256]{1,0:T(8,128)(2,1)S(1)} %get-tuple-element.43.refs_4_), channel_id=1, source_target_pairs={{0,4},{1,5},{2,6},{3,7},{4,0},{5,1},{6,2},{7,3},{8,12},{9,13},{10,... | collective-permute-start | bytes 196616 | tf_op jit(solution)/shard_map/ppermute | solution.py:85
  14.9 1.6 %collective-permute-done.3.refs_3_.refs_6_ = bf16[1,336,256]{2,1,0:T(8,128)(2,1)S(1)} collective-permute-done((bf16[1,336,256]{2,1,0:T(8,128)(2,1)S(1)}, bf16[1,336,256]{2,1,0:T(8,128)(2,1)S(1)}, u32[]{:S(2)}, u32[]{:S(2)}) %collective-permute-start.3) | collective-permute-done | bytes 172064 | tf_op jit(solution)/shard_map/ppermute | solution.py:85
  16.5 3.4 %collective-permute-done.2.refs_2_.refs_5_ = bf16[1,336,256]{2,1,0:T(8,128)(2,1)S(1)} collective-permute-done((bf16[1,336,256]{2,1,0:T(8,128)(2,1)S(1)}, bf16[1,336,256]{2,1,0:T(8,128)(2,1)S(1)}, u32[]{:S(2)}, u32[]{:S(2)}) %collective-permute-start.2) | collective-permute-done | bytes 172064 | tf_op jit(solution)/shard_map/ppermute | solution.py:85
  19.9 0.3 collective-permute-done.1.refs_1_.refs_4_
  20.2 0.6 %shard_map.167 = (f32[128,256]{1,0:T(8,128)S(1)}, bf16[128,256]{1,0:T(8,128)(2,1)S(1)}) custom-call(bf16[1,336,256]{2,1,0:T(8,128)(2,1)S(1)} %get-tuple-element.40.refs_0_.refs_3_, bf16[1,336,256]{2,1,0:T(8,128)(2,1)S(1)} %collective-permute-done.1.refs_1_.refs_4_, bf16[1,336,256]{2,1,0:T(8,128)(2,1)S(1)} %collective-permute-done.2.refs_2_.refs_5_, ...), custom_call_target="tpu_custom_call" | custom-call | tf_op jit(solution)/shard_map/pallas_call | solution.py:62
  20.8 0.1 collective-permute-start.4
  20.9 0.0 collective-permute-done.5.refs_5_
  20.9 1.2 %collective-permute-done.4.refs_3_ = bf16[128,256]{1,0:T(8,128)(2,1)S(1)} collective-permute-done((bf16[128,256]{1,0:T(8,128)(2,1)S(1)}, bf16[128,256]{1,0:T(8,128)(2,1)S(1)}, u32[]{:S(2)}, u32[]{:S(2)}) %collective-permute-start.4) | collective-permute-done | bytes 65568 | tf_op jit(solution)/shard_map/ppermute | solution.py:85
  22.1 0.0 collective-permute-done.refs_1_
  22.1 0.1 shard_map.168
  22.2 1.6 %collective-permute-start.9 = (bf16[256,256]{1,0:T(8,128)(2,1)S(1)}, bf16[256,256]{1,0:T(8,128)(2,1)S(1)}, u32[]{:S(2)}, u32[]{:S(2)}) collective-permute-start(bf16[256,256]{1,0:T(8,128)(2,1)S(1)} %get-tuple-element.47.refs_0_), channel_id=1, source_target_pairs={{0,2},{1,3},{2,0},{3,1},{4,6},{5,7},{6,4},{7,5},{8,10},{9,11},{10,... | collective-permute-start | bytes 393224 | tf_op jit(solution)/shard_map/ppermute | solution.py:85
  23.8 0.4 collective-permute-start.7
  24.3 0.0 collective-permute-start.6
  24.3 4.3 %collective-permute-done.9.refs_1_ = bf16[256,256]{1,0:T(8,128)(2,1)S(1)} collective-permute-done((bf16[256,256]{1,0:T(8,128)(2,1)S(1)}, bf16[256,256]{1,0:T(8,128)(2,1)S(1)}, u32[]{:S(2)}, u32[]{:S(2)}) %collective-permute-start.9) | collective-permute-done | bytes 131104 | tf_op jit(solution)/shard_map/ppermute | solution.py:85
  28.6 2.6 %collective-permute-start.10 = (bf16[128,256]{1,0:T(8,128)(2,1)S(1)}, bf16[128,256]{1,0:T(8,128)(2,1)S(1)}, u32[]{:S(2)}, u32[]{:S(2)}) collective-permute-start(bf16[128,256]{1,0:T(8,128)(2,1)S(1)} %shard_map.171.refs_0_), channel_id=1, source_target_pairs={{0,4},{1,5},{2,6},{3,7},{4,0},{5,1},{6,2},{7,3},{8,12},{9,13},{10,... | collective-permute-start | bytes 196616 | tf_op jit(solution)/shard_map/ppermute | solution.py:85
  31.3 0.3 collective-permute-start.12
  31.6 0.0 collective-permute-done.7.refs_4_
  31.6 0.0 collective-permute-start.8
  31.6 3.6 %collective-permute-start.13 = (bf16[128,256]{1,0:T(8,128)(2,1)S(1)}, bf16[128,256]{1,0:T(8,128)(2,1)S(1)}, u32[]{:S(2)}, u32[]{:S(2)}) collective-permute-start(bf16[128,256]{1,0:T(8,128)(2,1)S(1)} %get-tuple-element.50), channel_id=1, source_target_pairs={{0,6},{1,7},{2,4},{3,5},{4,2},{5,3},{6,0},{7,1},{8,14},{9,15},{10,... | collective-permute-start | bytes 196616 | tf_op jit(solution)/shard_map/ppermute | solution.py:85
  35.2 0.8 %collective-permute-done.10.refs_1_ = bf16[128,256]{1,0:T(8,128)(2,1)S(1)} collective-permute-done((bf16[128,256]{1,0:T(8,128)(2,1)S(1)}, bf16[128,256]{1,0:T(8,128)(2,1)S(1)}, u32[]{:S(2)}, u32[]{:S(2)}) %collective-permute-start.10) | collective-permute-done | bytes 65568 | tf_op jit(solution)/shard_map/ppermute | solution.py:85
  36.0 0.0 copy-start.1
  36.0 0.0 copy-start.2
  36.0 0.0 copy-start.3
  36.0 0.1 collective-permute-start.11
  36.1 3.3 %collective-permute-done.12.refs_2_ = bf16[128,256]{1,0:T(8,128)(2,1)S(1)} collective-permute-done((bf16[128,256]{1,0:T(8,128)(2,1)S(1)}, bf16[128,256]{1,0:T(8,128)(2,1)S(1)}, u32[]{:S(2)}, u32[]{:S(2)}) %collective-permute-start.12) | collective-permute-done | bytes 65568 | tf_op jit(solution)/shard_map/ppermute | solution.py:85
  39.4 0.0 collective-permute-done.13.refs_3_
  39.5 1.7 %collective-permute-start.16 = (bf16[1,128,256]{2,1,0:T(8,128)(2,1)S(1)}, bf16[1,128,256]{2,1,0:T(8,128)(2,1)S(1)}, u32[]{:S(2)}, u32[]{:S(2)}) collective-permute-start(bf16[1,128,256]{2,1,0:T(8,128)(2,1)S(1)} %shard_map.173.refs_5_), channel_id=1, source_target_pairs={{0,24},{8,16},{16,8},{24,0},{1,25},{9,17},{17,9},{25,1},{2,26},{10... | collective-permute-start | bytes 196616 | tf_op jit(solution)/shard_map/ppermute | solution.py:85
  41.1 1.3 %collective-permute-start.15 = (bf16[1,128,256]{2,1,0:T(8,128)(2,1)S(1)}, bf16[1,128,256]{2,1,0:T(8,128)(2,1)S(1)}, u32[]{:S(2)}, u32[]{:S(2)}) collective-permute-start(bf16[1,128,256]{2,1,0:T(8,128)(2,1)S(1)} %shard_map.173.refs_5_), channel_id=1, source_target_pairs={{0,16},{8,24},{16,0},{24,8},{1,17},{9,25},{17,1},{25,9},{2,18},{10... | collective-permute-start | bytes 196616 | tf_op jit(solution)/shard_map/ppermute | solution.py:85
  42.5 0.0 collective-permute-done.6.refs_2_
  42.5 0.5 %collective-permute-start.14 = (bf16[1,128,256]{2,1,0:T(8,128)(2,1)S(1)}, bf16[1,128,256]{2,1,0:T(8,128)(2,1)S(1)}, u32[]{:S(2)}, u32[]{:S(2)}) collective-permute-start(bf16[1,128,256]{2,1,0:T(8,128)(2,1)S(1)} %shard_map.173.refs_5_), channel_id=1, source_target_pairs={{0,8},{8,0},{16,24},{24,16},{1,9},{9,1},{17,25},{25,17},{2,10},{10... | collective-permute-start | bytes 196616 | tf_op jit(solution)/shard_map/ppermute | solution.py:85
  43.0 0.7 %shard_map.169 = (f32[64,256]{1,0:T(8,128)S(1)}, f32[256,512]{1,0:T(8,128)S(1)}) custom-call(s32[8,512]{1,0:T(8,128)S(1)} %get-tuple-element.37.refs_0_.refs_1_, bf16[256,256]{1,0:T(8,128)(2,1)S(1)} %get-tuple-element.44.refs_1_, bf16[256,256]{1,0:T(8,128)(2,1)S(1)} %collective-permute-done.6.refs_2_, ...), custom_call_target="tpu_custom_call" | custom-call | tf_op jit(solution)/shard_map/pallas_call | solution.py:62
  43.8 0.0 collective-permute-done.8.refs_5_
  43.8 2.8 %shard_map.170 = f32[64,256]{1,0:T(8,128)} custom-call(f32[4,1152,128]{2,1,0:T(8,128)S(1)} %get-tuple-element.36.refs_0_, s32[8,512]{1,0:T(8,128)S(1)} %get-tuple-element.37.refs_0_.refs_1_, f32[64,256]{1,0:T(8,128)S(1)} %get-tuple-element.45.refs_2_, f32[256,512]{1,0:T(8,128)S(1)} %get-tuple-element.46.refs_3_, ...), custom_call_target="tpu_custom_call" | custom-call | tf_op jit(solution)/shard_map/pallas_call | solution.py:62
  46.6 0.0 collective-permute-done.16.refs_8_
  46.6 0.0 collective-permute-done.15.refs_7_
  46.6 0.1 collective-permute-done.14.refs_6_
  46.7 0.0 collective-permute-done.11.refs_2_
  46.8 0.0 copy-done.1
  46.8 0.0 copy-done.2
  46.8 0.0 copy-done.3
  46.8 1.0 %shard_map.174 = (f32[128,256]{1,0:T(8,128)}, f32[256,256]{1,0:T(8,128)}, f32[1,256]{1,0:T(1,128)}) custom-call(f32[128,256]{1,0:T(8,128)S(1)} %copy-done.2, f32[128,256]{1,0:T(8,128)S(1)} %shard_map.172.refs_1_, f32[128,256]{1,0:T(8,128)S(1)} %collective-permute-done.11.refs_2_, f32[256,256]{1,0:T(8,128)S(1)} %copy-done.1, f32[1,256]{1,0:T(1,128)S(1)} %bitcast.4, ...), custom_call_target="tpu_custom_call" | custom-call | tf_op jit(solution)/shard_map/pallas_call | solution.py:62
  (3 shorter events, 0.1 us)
Async XLA Ops:
  0.6 1.5 %copy-start = (bf16[64,8192]{1,0:T(8,128)(2,1)S(1)}, bf16[64,8192]{1,0:T(8,128)(2,1)}, u32[]{:S(2)}) copy-start(bf16[64,8192]{1,0:T(8,128)(2,1)} %refs_0_.4) | copy-start | bytes 3145732
  7.2 14.9 %collective-permute-start = (bf16[512,256]{1,0:T(8,128)(2,1)S(1)}, bf16[512,256]{1,0:T(8,128)(2,1)S(1)}, u32[]{:S(2)}, u32[]{:S(2)}) collective-permute-start(bf16[512,256]{1,0:T(8,128)(2,1)S(1)} %get-tuple-element.39), channel_id=1, source_target_pairs={{0,1},{1,0},{2,3},{3,2},{4,5},{5,4},{6,7},{7,6},{8,9},{9,8},{10,11... | collective-permute-start | bytes 786440 | tf_op jit(solution)/shard_map/ppermute | solution.py:85
  7.7 8.8 %collective-permute-start.3 = (bf16[1,336,256]{2,1,0:T(8,128)(2,1)S(1)}, bf16[1,336,256]{2,1,0:T(8,128)(2,1)S(1)}, u32[]{:S(2)}, u32[]{:S(2)}) collective-permute-start(bf16[1,336,256]{2,1,0:T(8,128)(2,1)S(1)} %get-tuple-element.40.refs_0_.refs_3_), channel_id=1, source_target_pairs={{0,24},{8,16},{16,8},{24,0},{1,25},{9,17},{17,9},{25,1},{2,26},{10... | collective-permute-start | bytes 516104 | tf_op jit(solution)/shard_map/ppermute | solution.py:85
  11.2 8.7 %collective-permute-start.2 = (bf16[1,336,256]{2,1,0:T(8,128)(2,1)S(1)}, bf16[1,336,256]{2,1,0:T(8,128)(2,1)S(1)}, u32[]{:S(2)}, u32[]{:S(2)}) collective-permute-start(bf16[1,336,256]{2,1,0:T(8,128)(2,1)S(1)} %get-tuple-element.40.refs_0_.refs_3_), channel_id=1, source_target_pairs={{0,16},{8,24},{16,0},{24,8},{1,17},{9,25},{17,1},{25,9},{2,18},{10... | collective-permute-start | bytes 516104 | tf_op jit(solution)/shard_map/ppermute | solution.py:85
  11.7 8.4 %collective-permute-start.1 = (bf16[1,336,256]{2,1,0:T(8,128)(2,1)S(1)}, bf16[1,336,256]{2,1,0:T(8,128)(2,1)S(1)}, u32[]{:S(2)}, u32[]{:S(2)}) collective-permute-start(bf16[1,336,256]{2,1,0:T(8,128)(2,1)S(1)} %get-tuple-element.40.refs_0_.refs_3_), channel_id=1, source_target_pairs={{0,8},{8,0},{16,24},{24,16},{1,9},{9,1},{17,25},{25,17},{2,10},{10... | collective-permute-start | bytes 516104 | tf_op jit(solution)/shard_map/ppermute | solution.py:85
  11.9 9.0 %collective-permute-start.5 = (bf16[128,256]{1,0:T(8,128)(2,1)S(1)}, bf16[128,256]{1,0:T(8,128)(2,1)S(1)}, u32[]{:S(2)}, u32[]{:S(2)}) collective-permute-start(bf16[128,256]{1,0:T(8,128)(2,1)S(1)} %get-tuple-element.43.refs_4_), channel_id=1, source_target_pairs={{0,4},{1,5},{2,6},{3,7},{4,0},{5,1},{6,2},{7,3},{8,12},{9,13},{10,... | collective-permute-start | bytes 196616 | tf_op jit(solution)/shard_map/ppermute | solution.py:85
  20.8 1.3 %collective-permute-start.4 = (bf16[128,256]{1,0:T(8,128)(2,1)S(1)}, bf16[128,256]{1,0:T(8,128)(2,1)S(1)}, u32[]{:S(2)}, u32[]{:S(2)}) collective-permute-start(bf16[128,256]{1,0:T(8,128)(2,1)S(1)} %get-tuple-element.42), channel_id=1, source_target_pairs={{0,1},{1,0},{2,3},{3,2},{4,5},{5,4},{6,7},{7,6},{8,9},{9,8},{10,11... | collective-permute-start | bytes 196616 | tf_op jit(solution)/shard_map/ppermute | solution.py:85
  22.2 6.4 %collective-permute-start.9 = (bf16[256,256]{1,0:T(8,128)(2,1)S(1)}, bf16[256,256]{1,0:T(8,128)(2,1)S(1)}, u32[]{:S(2)}, u32[]{:S(2)}) collective-permute-start(bf16[256,256]{1,0:T(8,128)(2,1)S(1)} %get-tuple-element.47.refs_0_), channel_id=1, source_target_pairs={{0,2},{1,3},{2,0},{3,1},{4,6},{5,7},{6,4},{7,5},{8,10},{9,11},{10,... | collective-permute-start | bytes 393224 | tf_op jit(solution)/shard_map/ppermute | solution.py:85
  23.8 7.8 %collective-permute-start.7 = (bf16[256,256]{1,0:T(8,128)(2,1)S(1)}, bf16[256,256]{1,0:T(8,128)(2,1)S(1)}, u32[]{:S(2)}, u32[]{:S(2)}) collective-permute-start(bf16[256,256]{1,0:T(8,128)(2,1)S(1)} %get-tuple-element.44.refs_1_), channel_id=1, source_target_pairs={{0,2},{1,3},{2,0},{3,1},{4,6},{5,7},{6,4},{7,5},{8,10},{9,11},{10,... | collective-permute-start | bytes 393224 | tf_op jit(solution)/shard_map/ppermute | solution.py:85
  24.3 18.2 %collective-permute-start.6 = (bf16[256,256]{1,0:T(8,128)(2,1)S(1)}, bf16[256,256]{1,0:T(8,128)(2,1)S(1)}, u32[]{:S(2)}, u32[]{:S(2)}) collective-permute-start(bf16[256,256]{1,0:T(8,128)(2,1)S(1)} %get-tuple-element.44.refs_1_), channel_id=1, source_target_pairs={{0,1},{1,0},{2,3},{3,2},{4,5},{5,4},{6,7},{7,6},{8,9},{9,8},{10,11... | collective-permute-start | bytes 393224 | tf_op jit(solution)/shard_map/ppermute | solution.py:85
  28.6 7.4 %collective-permute-start.10 = (bf16[128,256]{1,0:T(8,128)(2,1)S(1)}, bf16[128,256]{1,0:T(8,128)(2,1)S(1)}, u32[]{:S(2)}, u32[]{:S(2)}) collective-permute-start(bf16[128,256]{1,0:T(8,128)(2,1)S(1)} %shard_map.171.refs_0_), channel_id=1, source_target_pairs={{0,4},{1,5},{2,6},{3,7},{4,0},{5,1},{6,2},{7,3},{8,12},{9,13},{10,... | collective-permute-start | bytes 196616 | tf_op jit(solution)/shard_map/ppermute | solution.py:85
  31.3 8.1 %collective-permute-start.12 = (bf16[128,256]{1,0:T(8,128)(2,1)S(1)}, bf16[128,256]{1,0:T(8,128)(2,1)S(1)}, u32[]{:S(2)}, u32[]{:S(2)}) collective-permute-start(bf16[128,256]{1,0:T(8,128)(2,1)S(1)} %get-tuple-element.49), channel_id=1, source_target_pairs={{0,4},{1,5},{2,6},{3,7},{4,0},{5,1},{6,2},{7,3},{8,12},{9,13},{10,... | collective-permute-start | bytes 196616 | tf_op jit(solution)/shard_map/ppermute | solution.py:85
  31.6 12.1 %collective-permute-start.8 = (bf16[256,256]{1,0:T(8,128)(2,1)S(1)}, bf16[256,256]{1,0:T(8,128)(2,1)S(1)}, u32[]{:S(2)}, u32[]{:S(2)}) collective-permute-start(bf16[256,256]{1,0:T(8,128)(2,1)S(1)} %collective-permute-done.7.refs_4_), channel_id=1, source_target_pairs={{0,1},{1,0},{2,3},{3,2},{4,5},{5,4},{6,7},{7,6},{8,9},{9,8},{10,11... | collective-permute-start | bytes 393224 | tf_op jit(solution)/shard_map/ppermute | solution.py:85
  31.6 7.8 %collective-permute-start.13 = (bf16[128,256]{1,0:T(8,128)(2,1)S(1)}, bf16[128,256]{1,0:T(8,128)(2,1)S(1)}, u32[]{:S(2)}, u32[]{:S(2)}) collective-permute-start(bf16[128,256]{1,0:T(8,128)(2,1)S(1)} %get-tuple-element.50), channel_id=1, source_target_pairs={{0,6},{1,7},{2,4},{3,5},{4,2},{5,3},{6,0},{7,1},{8,14},{9,15},{10,... | collective-permute-start | bytes 196616 | tf_op jit(solution)/shard_map/ppermute | solution.py:85
  36.0 10.8 %copy-start.1 = (f32[256,256]{1,0:T(8,128)S(1)}, f32[256,256]{1,0:T(8,128)}, u32[]{:S(2)}) copy-start(f32[256,256]{1,0:T(8,128)} %refs_3_.3) | copy-start | bytes 786436
  36.0 10.7 %copy-start.2 = (f32[128,256]{1,0:T(8,128)S(1)}, f32[128,256]{1,0:T(8,128)}, u32[]{:S(2)}) copy-start(f32[128,256]{1,0:T(8,128)} %refs_0_.5) | copy-start | bytes 393220
  36.0 10.7 %copy-start.3 = (f32[256]{0:T(256)S(1)}, f32[256]{0:T(256)}, u32[]{:S(2)}) copy-start(f32[256]{0:T(256)} %param.15) | copy-start | bytes 3076
  36.0 10.7 %collective-permute-start.11 = (f32[128,256]{1,0:T(8,128)S(1)}, f32[128,256]{1,0:T(8,128)S(1)}, u32[]{:S(2)}, u32[]{:S(2)}) collective-permute-start(f32[128,256]{1,0:T(8,128)S(1)} %shard_map.172.refs_1_), channel_id=1, source_target_pairs={{0,1},{1,0},{2,3},{3,2},{4,5},{5,4},{6,7},{7,6},{8,9},{9,8},{10,11... | collective-permute-start | bytes 393224 | tf_op jit(solution)/shard_map/ppermute | solution.py:85
  39.5 7.2 %collective-permute-start.16 = (bf16[1,128,256]{2,1,0:T(8,128)(2,1)S(1)}, bf16[1,128,256]{2,1,0:T(8,128)(2,1)S(1)}, u32[]{:S(2)}, u32[]{:S(2)}) collective-permute-start(bf16[1,128,256]{2,1,0:T(8,128)(2,1)S(1)} %shard_map.173.refs_5_), channel_id=1, source_target_pairs={{0,24},{8,16},{16,8},{24,0},{1,25},{9,17},{17,9},{25,1},{2,26},{10... | collective-permute-start | bytes 196616 | tf_op jit(solution)/shard_map/ppermute | solution.py:85
  41.1 5.5 %collective-permute-start.15 = (bf16[1,128,256]{2,1,0:T(8,128)(2,1)S(1)}, bf16[1,128,256]{2,1,0:T(8,128)(2,1)S(1)}, u32[]{:S(2)}, u32[]{:S(2)}) collective-permute-start(bf16[1,128,256]{2,1,0:T(8,128)(2,1)S(1)} %shard_map.173.refs_5_), channel_id=1, source_target_pairs={{0,16},{8,24},{16,0},{24,8},{1,17},{9,25},{17,1},{25,9},{2,18},{10... | collective-permute-start | bytes 196616 | tf_op jit(solution)/shard_map/ppermute | solution.py:85
  42.5 4.3 %collective-permute-start.14 = (bf16[1,128,256]{2,1,0:T(8,128)(2,1)S(1)}, bf16[1,128,256]{2,1,0:T(8,128)(2,1)S(1)}, u32[]{:S(2)}, u32[]{:S(2)}) collective-permute-start(bf16[1,128,256]{2,1,0:T(8,128)(2,1)S(1)} %shard_map.173.refs_5_), channel_id=1, source_target_pairs={{0,8},{8,0},{16,24},{24,16},{1,9},{9,1},{17,25},{25,17},{2,10},{10... | collective-permute-start | bytes 196616 | tf_op jit(solution)/shard_map/ppermute | solution.py:85
